TPU v7x, 32 devices: a whole 2x2x4 slice. The times are simulated.
32 devices in a mesh: group: 4 (over z), expert: 8 (over y, x, core).
Axes of the slice: x: 2, y: 2, z: 4, core: 2. Of those that a mesh axis runs over, the one named last changes fastest.
Arguments:
- tokens: bfloat16 [2, 4096, 1536], P(None, ('group', 'expert')), may hold values from -6 to 6
- cotangent: bfloat16 [2, 4096, 1536], P(None, ('group', 'expert')), may hold values from -6 to 6
- routes: int32 [2, 4096, 8], P(None, ('group', 'expert')), may hold values from 0 to 31, all different within a row; in each aligned block of 128 rows (0 to 127, 128 to 255, ..., all dimensions but the last counted through in order) at most 48 rows name the same one
- norm_one: bfloat16 [1536], P('group'), may hold values from 0.5 to 1.5
- query_key_value_weight: bfloat16 [1536, 2560], P('group'), may hold values from -0.15625 to 0.15625
- out_weight: bfloat16 [1536, 1536], P('group'), may hold values from -3.5 to 3.5
- norm_two: bfloat16 [1536], P('group'), may hold values from 0.5 to 1.5
- router_weight: bfloat16 [1536, 32], P('group'), may hold values from -0.078125 to 0.078125
- gate_weight: bfloat16 [32, 1536, 512], P('expert', 'group'), may hold values from -0.15625 to 0.15625
- up_weight: bfloat16 [32, 1536, 512], P('expert', 'group'), may hold values from -0.15625 to 0.15625
- down_weight: bfloat16 [32, 512, 1536], P('expert', None, 'group'), may hold values from -1 to 1
Outputs:
- block_out: bfloat16 [2, 4096, 1536], P(None, ('group', 'expert'))
- input_grad: float32 [2, 4096, 1536], P(None, ('group', 'expert'))
- norm_one_grad: float32 [1536], P('group')
- qkv_grad: float32 [1536, 2560], P('group')
- out_grad: float32 [1536, 1536], P('group')
- norm_two_grad: float32 [1536], P('group')
- router_grad: float32 [1536, 32], P('group')
- gate_grad: float32 [32, 1536, 512], P('expert', 'group')
- up_grad: float32 [32, 1536, 512], P('expert', 'group')
- down_grad: float32 [32, 512, 1536], P('expert', None, 'group')
Inputs may be any that keep to these rules, and one draw needn't show every extreme that they name: `routes`: in the rows of one device in one micro-batch (aligned blocks of 128 rows) no expert is named more than 48 times, and in some blocks one is named exactly 48 times; a row names 8 different experts.
All inputs are finite; a program needn't handle non-finite values.
Results may differ from a plain program's by a relative error of at most 0.022.
Values may be sent and summed in bfloat16 or wider, within the bound.
A program may use at most 256 MiB of HBM per device.

v0:
```python
import jax
import jax.numpy as jnp
from jax import lax
from jax.sharding import PartitionSpec as P

MODEL_WIDTH = 1536
QUERY_HEADS = 24
KEY_VALUE_HEADS = 8
HEAD_SIZE = 64
TOPK = 8
CONT = 256
PR_DEV = 64


SCORE_SCALE = 0.125
NEG_FILL = -1e30
HIGHEST = lax.Precision.HIGHEST


def rms_parts(inputs, gain):
    inverse = lax.rsqrt(jnp.mean(inputs * inputs, axis=-1, keepdims=True) + 1e-05)
    return (inputs * inverse * gain, inverse)


def rms_back(inputs, inverse, gain, upstream):
    scaled = gain * upstream
    return inverse * scaled - inputs * inverse * inverse * inverse * jnp.mean(
        scaled * inputs, axis=-1, keepdims=True
    )


def rope_tables(positions):
    half_dim = HEAD_SIZE // 2
    frequency = 10000.0 ** (-jnp.arange(half_dim, dtype=jnp.float32) * (2.0 / HEAD_SIZE))
    angle_table = positions.astype(jnp.float32)[:, None] * frequency[None, :]
    return (jnp.cos(angle_table)[:, None, :], jnp.sin(angle_table)[:, None, :])


def rotate_halves(values, cosine_table, sine_table):
    half_dim = values.shape[-1] // 2
    first_half = values[..., :half_dim]
    second = values[..., half_dim:]
    return jnp.concatenate(
        [
            first_half * cosine_table - second * sine_table,
            second * cosine_table + first_half * sine_table,
        ],
        axis=-1,
    )


def token_meta(index, prompt_len):
    tokens_per_device = 2 * PR_DEV
    device_id = index // tokens_per_device
    local_id = index % tokens_per_device
    is_prompt = local_id < PR_DEV
    cont_index = device_id * PR_DEV + local_id - PR_DEV
    seq_id = jnp.where(is_prompt, -1, cont_index // CONT)
    position = jnp.where(is_prompt, device_id * PR_DEV + local_id, prompt_len + cont_index % CONT)
    return (is_prompt, seq_id, position)


def fetch_rows(key_low, value_low):
    key_for_row, value_for_row = (
        lax.all_gather(key_low, "expert", axis=0, tiled=True),
        lax.all_gather(value_low, "expert", axis=0, tiled=True),
    )
    key_total = key_for_row.shape[0]
    return (
        key_for_row,
        value_for_row,
        jnp.arange(key_total, dtype=jnp.int32),
        jnp.ones((key_total,), jnp.bool_),
    )


def return_grads(key_summands, value_summands):
    return (
        lax.psum_scatter(
            key_summands.astype(jnp.bfloat16), "expert", scatter_dimension=0, tiled=True
        ).astype(jnp.float32),
        lax.psum_scatter(
            value_summands.astype(jnp.bfloat16), "expert", scatter_dimension=0, tiled=True
        ).astype(jnp.float32),
    )


def key_blocks(key_for_row, value_for_row, key_index, key_valid):
    key_total = key_for_row.shape[0]
    block_length = min(512, key_total)
    pad_len = -key_total % block_length
    number_of_blocks = (key_total + pad_len) // block_length
    return (
        key_for_row.reshape(number_of_blocks, block_length, KEY_VALUE_HEADS, HEAD_SIZE),
        value_for_row.reshape(number_of_blocks, block_length, KEY_VALUE_HEADS, HEAD_SIZE),
        key_index.reshape(number_of_blocks, block_length),
        key_valid.reshape(number_of_blocks, block_length),
    )


def block_scores(
    query_by_group, key_block, index_block, valid_block, query_seq, query_pos, prompt_len
):
    key_prompt, key_seq, key_pos = token_meta(index_block, prompt_len)
    allowed = (
        (key_prompt[None, :] | (query_seq[:, None] == key_seq[None, :]))
        & (key_pos[None, :] <= query_pos[:, None])
        & valid_block[None, :]
    )
    scores = (
        jnp.einsum("qgrd,kgd->grqk", query_by_group, key_block, preferred_element_type=jnp.float32)
        * SCORE_SCALE
    )
    return (scores, allowed[None, None])


def attention_forward(query_by_group, fetched, query_seq, query_pos, prompt_len):
    keys_blocked, values_blocked, index_blocked, valid_blocked = key_blocks(*fetched)
    statistics_shape = (KEY_VALUE_HEADS, QUERY_HEADS // KEY_VALUE_HEADS, query_by_group.shape[0])

    def stats_step(carry, block_inputs):
        running_max, running_sum = carry
        key_block, index_block, valid_block = block_inputs
        scores, allowed = block_scores(
            query_by_group, key_block, index_block, valid_block, query_seq, query_pos, prompt_len
        )
        scores = jnp.where(allowed, scores, NEG_FILL)
        new_max = jnp.maximum(running_max, jnp.max(scores, axis=-1))
        block_sum = jnp.sum(jnp.where(allowed, jnp.exp(scores - new_max[..., None]), 0.0), axis=-1)
        return ((new_max, running_sum * jnp.exp(running_max - new_max) + block_sum), None)

    start_stats = (
        jnp.full(statistics_shape, NEG_FILL, jnp.float32),
        jnp.zeros(statistics_shape, jnp.float32),
    )
    (final_max, final_sum), unused = lax.scan(
        stats_step, start_stats, (keys_blocked, index_blocked, valid_blocked)
    )
    log_total = final_max + jnp.log(final_sum)

    def output_step(total_acc, block_inputs):
        key_block, value_block, index_block, valid_block = block_inputs
        scores, allowed = block_scores(
            query_by_group, key_block, index_block, valid_block, query_seq, query_pos, prompt_len
        )
        probs = jnp.where(allowed, jnp.exp(scores - log_total[..., None]), 0.0).astype(jnp.bfloat16)
        return (
            total_acc
            + jnp.einsum("grqk,kgd->qgrd", probs, value_block, preferred_element_type=jnp.float32),
            None,
        )

    mixed_heads, unused = lax.scan(
        output_step,
        jnp.zeros(query_by_group.shape, jnp.float32),
        (keys_blocked, values_blocked, index_blocked, valid_blocked),
    )
    return (mixed_heads, log_total)


def attention_backward(
    query_by_group, fetched, log_total, d_mixed, delta, query_seq, query_pos, prompt_len
):
    keys_blocked, values_blocked, index_blocked, valid_blocked = key_blocks(*fetched)

    def grad_step(dq_acc, block_inputs):
        key_block, value_block, index_block, valid_block = block_inputs
        scores, allowed = block_scores(
            query_by_group, key_block, index_block, valid_block, query_seq, query_pos, prompt_len
        )
        probs = jnp.where(allowed, jnp.exp(scores - log_total[..., None]), 0.0)
        d_probs = jnp.einsum(
            "qgrd,kgd->grqk", d_mixed, value_block, preferred_element_type=jnp.float32
        )
        d_scores = (probs * (d_probs - delta[..., None])).astype(jnp.bfloat16)
        dq_acc = (
            dq_acc
            + jnp.einsum("grqk,kgd->qgrd", d_scores, key_block, preferred_element_type=jnp.float32)
            * SCORE_SCALE
        )
        d_key = (
            jnp.einsum(
                "grqk,qgrd->kgd", d_scores, query_by_group, preferred_element_type=jnp.float32
            )
            * SCORE_SCALE
        )
        d_value = jnp.einsum(
            "grqk,qgrd->kgd",
            probs.astype(jnp.bfloat16),
            d_mixed,
            preferred_element_type=jnp.float32,
        )
        return (dq_acc, (d_key, d_value))

    query_gradient, (key_summands, value_summands) = lax.scan(
        grad_step,
        jnp.zeros(query_by_group.shape, jnp.float32),
        (keys_blocked, values_blocked, index_blocked, valid_blocked),
    )
    return (
        query_gradient,
        key_summands.reshape(-1, KEY_VALUE_HEADS * HEAD_SIZE),
        value_summands.reshape(-1, KEY_VALUE_HEADS * HEAD_SIZE),
    )


def per_device(
    tokens,
    cotangent,
    routes,
    norm_one,
    query_key_value_weight,
    out_weight,
    norm_two,
    router_weight,
    gate_weight,
    up_weight,
    down_weight,
):
    expert_count = lax.axis_size("expert")
    my_index = lax.axis_index("expert")
    micro_count = tokens.shape[0]
    tokens_per_device = tokens.shape[1]
    exp_here = gate_weight.shape[0]
    prompt_len = PR_DEV * expert_count
    query_width = QUERY_HEADS * HEAD_SIZE
    key_value_width = KEY_VALUE_HEADS * HEAD_SIZE
    repeat_heads = QUERY_HEADS // KEY_VALUE_HEADS
    full_weights = (
        lax.all_gather(norm_one, "group", axis=0, tiled=True),
        lax.all_gather(query_key_value_weight, "group", axis=0, tiled=True),
        lax.all_gather(out_weight, "group", axis=0, tiled=True),
        lax.all_gather(norm_two, "group", axis=0, tiled=True),
        lax.all_gather(router_weight, "group", axis=0, tiled=True),
        lax.all_gather(gate_weight, "group", axis=1, tiled=True),
        lax.all_gather(up_weight, "group", axis=1, tiled=True),
        lax.all_gather(down_weight, "group", axis=2, tiled=True),
    )
    gain_one, qkv_full, out_full, gain_two, router_full, gate_full, up_full, down_full = (
        full_weights
    )
    gain_one = gain_one.astype(jnp.float32)
    gain_two = gain_two.astype(jnp.float32)
    expert_total = router_full.shape[1]
    slot_cap = max(2, 3 * TOPK * PR_DEV // expert_total)
    expert_ids = jnp.arange(expert_total, dtype=jnp.int32)
    local_index = my_index * tokens_per_device + jnp.arange(tokens_per_device, dtype=jnp.int32)
    query_prompt, query_seq, query_pos = token_meta(local_index, prompt_len)
    cosine_table, sine_table = rope_tables(query_pos)
    pair_token = jnp.arange(tokens_per_device * TOPK, dtype=jnp.int32) // TOPK
    outputs = []
    kept = []
    for micro_index in range(micro_count):
        inputs = tokens[micro_index].astype(jnp.float32)
        normed, inverse_one = rms_parts(inputs, gain_one)
        normed_low = normed.astype(jnp.bfloat16)
        project_inputs = jnp.dot(normed_low, qkv_full, preferred_element_type=jnp.float32)
        query_lower_precision = rotate_halves(
            project_inputs[:, :query_width].reshape(tokens_per_device, QUERY_HEADS, HEAD_SIZE),
            cosine_table,
            sine_table,
        ).astype(jnp.bfloat16)
        key_low = (
            rotate_halves(
                project_inputs[:, query_width : query_width + key_value_width].reshape(
                    tokens_per_device, KEY_VALUE_HEADS, HEAD_SIZE
                ),
                cosine_table,
                sine_table,
            )
            .astype(jnp.bfloat16)
            .reshape(tokens_per_device, key_value_width)
        )
        value_low = project_inputs[:, query_width + key_value_width :].astype(jnp.bfloat16)
        fetched = fetch_rows(key_low, value_low)
        query_by_group = query_lower_precision.reshape(
            tokens_per_device, KEY_VALUE_HEADS, repeat_heads, HEAD_SIZE
        )
        mixed_heads, log_total = attention_forward(
            query_by_group, fetched, query_seq, query_pos, prompt_len
        )
        mixed_low = mixed_heads.reshape(tokens_per_device, query_width).astype(jnp.bfloat16)
        hidden = inputs + jnp.dot(mixed_low, out_full, preferred_element_type=jnp.float32)
        normed_two, inverse_two = rms_parts(hidden, gain_two)
        normed_two_low = normed_two.astype(jnp.bfloat16)
        logits = jnp.dot(normed_two_low, router_full, preferred_element_type=jnp.float32)
        route_rows = routes[micro_index]
        onehot = (route_rows[:, :, None] == expert_ids[None, None, :]).astype(jnp.float32)
        picked = jnp.sum(onehot * logits[:, None, :], axis=-1)
        gate_probs = jax.nn.softmax(picked, axis=-1)
        pair_expert = route_rows.reshape(-1)
        pair_hits = (pair_expert[:, None] == expert_ids[None, :]).astype(jnp.int32)
        slot_rank = jnp.sum((jnp.cumsum(pair_hits, axis=0) - 1) * pair_hits, axis=1)
        slot_place = pair_expert * slot_cap + slot_rank
        send_rows = (
            jnp.zeros((expert_total * slot_cap, MODEL_WIDTH), jnp.bfloat16)
            .at[slot_place]
            .set(normed_two_low[pair_token])
        )
        arrived = lax.all_to_all(
            send_rows.reshape(expert_count, exp_here, slot_cap, MODEL_WIDTH),
            "expert",
            split_axis=0,
            concat_axis=2,
            tiled=True,
        )
        arrived = arrived.reshape(exp_here, expert_count * slot_cap, MODEL_WIDTH)
        gate_pre = jnp.einsum(
            "erd,edf->erf", arrived, gate_full, preferred_element_type=jnp.float32
        )
        up_pre = jnp.einsum("erd,edf->erf", arrived, up_full, preferred_element_type=jnp.float32)
        active = (jax.nn.silu(gate_pre) * up_pre).astype(jnp.bfloat16)
        expert_out = jnp.einsum(
            "erf,efd->erd", active, down_full, preferred_element_type=jnp.float32
        ).astype(jnp.bfloat16)
        returned = lax.all_to_all(
            expert_out.reshape(1, exp_here, expert_count * slot_cap, MODEL_WIDTH),
            "expert",
            split_axis=2,
            concat_axis=0,
            tiled=True,
        )
        chosen = returned.reshape(expert_total * slot_cap, MODEL_WIDTH)[slot_place].reshape(
            tokens_per_device, TOPK, MODEL_WIDTH
        )
        mixture = jnp.sum(gate_probs[:, :, None] * chosen, axis=1)
        outputs.append((hidden + mixture).astype(jnp.bfloat16))
        stored_kv = (key_low, value_low)
        kept.append(
            (
                inputs,
                inverse_one,
                normed_low,
                query_by_group,
                stored_kv,
                log_total,
                mixed_heads,
                mixed_low,
                hidden,
                inverse_two,
                normed_two_low,
                onehot,
                gate_probs,
                slot_place,
                arrived,
                gate_pre,
                up_pre,
                active,
                chosen,
            )
        )
    back_weights = (
        lax.all_gather(norm_one, "group", axis=0, tiled=True),
        lax.all_gather(query_key_value_weight, "group", axis=0, tiled=True),
        lax.all_gather(out_weight, "group", axis=0, tiled=True),
        lax.all_gather(norm_two, "group", axis=0, tiled=True),
        lax.all_gather(router_weight, "group", axis=0, tiled=True),
        lax.all_gather(gate_weight, "group", axis=1, tiled=True),
        lax.all_gather(up_weight, "group", axis=1, tiled=True),
        lax.all_gather(down_weight, "group", axis=2, tiled=True),
    )
    gain_one, qkv_full, out_full, gain_two, router_full, gate_full, up_full, down_full = (
        back_weights
    )
    gain_one = gain_one.astype(jnp.float32)
    gain_two = gain_two.astype(jnp.float32)
    router_wide = router_full.astype(jnp.float32)
    acc_one = jnp.zeros(gain_one.shape, jnp.float32)
    acc_qkv = jnp.zeros(qkv_full.shape, jnp.float32)
    acc_out = jnp.zeros(out_full.shape, jnp.float32)
    acc_two = jnp.zeros(gain_two.shape, jnp.float32)
    acc_router = jnp.zeros(router_full.shape, jnp.float32)
    acc_gate = jnp.zeros(gate_full.shape, jnp.float32)
    acc_up = jnp.zeros(up_full.shape, jnp.float32)
    acc_down = jnp.zeros(down_full.shape, jnp.float32)
    input_grads = []
    for micro_index in range(micro_count):
        (
            inputs,
            inverse_one,
            normed_low,
            query_by_group,
            stored_kv,
            log_total,
            mixed_heads,
            mixed_low,
            hidden,
            inverse_two,
            normed_two_low,
            onehot,
            gate_probs,
            slot_place,
            arrived,
            gate_pre,
            up_pre,
            active,
            chosen,
        ) = kept[micro_index]
        d_out = cotangent[micro_index].astype(jnp.float32)
        d_gates = jnp.sum(d_out[:, None, :] * chosen, axis=-1)
        d_pairs = (
            (gate_probs[:, :, None] * d_out[:, None, :])
            .astype(jnp.bfloat16)
            .reshape(tokens_per_device * TOPK, MODEL_WIDTH)
        )
        grad_rows = (
            jnp.zeros((expert_total * slot_cap, MODEL_WIDTH), jnp.bfloat16)
            .at[slot_place]
            .set(d_pairs)
        )
        grad_arrived = lax.all_to_all(
            grad_rows.reshape(expert_count, exp_here, slot_cap, MODEL_WIDTH),
            "expert",
            split_axis=0,
            concat_axis=2,
            tiled=True,
        )
        grad_arrived = grad_arrived.reshape(exp_here, expert_count * slot_cap, MODEL_WIDTH)
        d_active = jnp.einsum(
            "erd,efd->erf", grad_arrived, down_full, preferred_element_type=jnp.float32
        )
        acc_down = acc_down + jnp.einsum(
            "erf,erd->efd", active, grad_arrived, preferred_element_type=jnp.float32
        )
        sigmoid_gate = jax.nn.sigmoid(gate_pre)
        d_up = (d_active * gate_pre * sigmoid_gate).astype(jnp.bfloat16)
        d_gate = (
            d_active * up_pre * sigmoid_gate * (1.0 + gate_pre * (1.0 - sigmoid_gate))
        ).astype(jnp.bfloat16)
        acc_gate = acc_gate + jnp.einsum(
            "erd,erf->edf", arrived, d_gate, preferred_element_type=jnp.float32
        )
        acc_up = acc_up + jnp.einsum(
            "erd,erf->edf", arrived, d_up, preferred_element_type=jnp.float32
        )
        d_arrived = jnp.einsum(
            "erf,edf->erd", d_gate, gate_full, preferred_element_type=jnp.float32
        )
        d_arrived = (
            d_arrived
            + jnp.einsum("erf,edf->erd", d_up, up_full, preferred_element_type=jnp.float32)
        ).astype(jnp.bfloat16)
        grad_back = lax.all_to_all(
            d_arrived.reshape(1, exp_here, expert_count * slot_cap, MODEL_WIDTH),
            "expert",
            split_axis=2,
            concat_axis=0,
            tiled=True,
        )
        d_normed_two = jnp.sum(
            grad_back.reshape(expert_total * slot_cap, MODEL_WIDTH)[slot_place].reshape(
                tokens_per_device, TOPK, MODEL_WIDTH
            ),
            axis=1,
            dtype=jnp.float32,
        )
        d_picked = gate_probs * (d_gates - jnp.sum(gate_probs * d_gates, axis=-1, keepdims=True))
        d_logits = jnp.sum(onehot * d_picked[:, :, None], axis=1)
        acc_router = acc_router + jnp.einsum(
            "td,te->de", normed_two_low.astype(jnp.float32), d_logits, precision=HIGHEST
        )
        d_normed_two = d_normed_two + jnp.einsum(
            "te,de->td", d_logits, router_wide, precision=HIGHEST
        )
        acc_two = acc_two + jnp.sum(d_normed_two * hidden * inverse_two, axis=0)
        d_hidden = d_out + rms_back(hidden, inverse_two, gain_two, d_normed_two)
        d_attended = d_hidden.astype(jnp.bfloat16)
        acc_out = acc_out + jnp.einsum(
            "tf,td->fd", mixed_low, d_attended, preferred_element_type=jnp.float32
        )
        d_mixed = (
            jnp.einsum("td,fd->tf", d_attended, out_full, preferred_element_type=jnp.float32)
            .astype(jnp.bfloat16)
            .reshape(tokens_per_device, KEY_VALUE_HEADS, repeat_heads, HEAD_SIZE)
        )
        delta = jnp.sum(d_mixed * mixed_heads, axis=-1).transpose(1, 2, 0)
        fetched = fetch_rows(stored_kv[0], stored_kv[1])
        query_gradient, key_summands, value_summands = attention_backward(
            query_by_group, fetched, log_total, d_mixed, delta, query_seq, query_pos, prompt_len
        )
        own_key_gradient, d_value_own = return_grads(key_summands, value_summands)
        d_query_low = (
            rotate_halves(
                query_gradient.reshape(tokens_per_device, QUERY_HEADS, HEAD_SIZE),
                cosine_table,
                -sine_table,
            )
            .astype(jnp.bfloat16)
            .reshape(tokens_per_device, query_width)
        )
        d_key_low = (
            rotate_halves(
                own_key_gradient.reshape(tokens_per_device, KEY_VALUE_HEADS, HEAD_SIZE),
                cosine_table,
                -sine_table,
            )
            .astype(jnp.bfloat16)
            .reshape(tokens_per_device, key_value_width)
        )
        d_value_low = d_value_own.astype(jnp.bfloat16)
        d_project = jnp.concatenate([d_query_low, d_key_low, d_value_low], axis=1)
        acc_qkv = acc_qkv + jnp.einsum(
            "td,tf->df", normed_low, d_project, preferred_element_type=jnp.float32
        )
        d_normed = jnp.einsum("tf,df->td", d_project, qkv_full, preferred_element_type=jnp.float32)
        acc_one = acc_one + jnp.sum(d_normed * inputs * inverse_one, axis=0)
        input_grads.append(d_hidden + rms_back(inputs, inverse_one, gain_one, d_normed))
    group_sums = (
        lax.psum_scatter(
            acc_one.astype(jnp.bfloat16), "group", scatter_dimension=0, tiled=True
        ).astype(jnp.float32),
        lax.psum_scatter(
            acc_qkv.astype(jnp.bfloat16), "group", scatter_dimension=0, tiled=True
        ).astype(jnp.float32),
        lax.psum_scatter(
            acc_out.astype(jnp.bfloat16), "group", scatter_dimension=0, tiled=True
        ).astype(jnp.float32),
        lax.psum_scatter(
            acc_two.astype(jnp.bfloat16), "group", scatter_dimension=0, tiled=True
        ).astype(jnp.float32),
        lax.psum_scatter(
            acc_router.astype(jnp.bfloat16), "group", scatter_dimension=0, tiled=True
        ).astype(jnp.float32),
        lax.psum_scatter(
            acc_gate.astype(jnp.bfloat16), "group", scatter_dimension=1, tiled=True
        ).astype(jnp.float32),
        lax.psum_scatter(
            acc_up.astype(jnp.bfloat16), "group", scatter_dimension=1, tiled=True
        ).astype(jnp.float32),
        lax.psum_scatter(
            acc_down.astype(jnp.bfloat16), "group", scatter_dimension=2, tiled=True
        ).astype(jnp.float32),
    )
    grad_one, grad_qkv, grad_out, grad_two, grad_router, grad_gate, grad_up, grad_down = group_sums
    grad_one, grad_qkv, grad_out, grad_two, grad_router = (
        lax.psum(grad_one.astype(jnp.bfloat16), "expert").astype(jnp.float32),
        lax.psum(grad_qkv.astype(jnp.bfloat16), "expert").astype(jnp.float32),
        lax.psum(grad_out.astype(jnp.bfloat16), "expert").astype(jnp.float32),
        lax.psum(grad_two.astype(jnp.bfloat16), "expert").astype(jnp.float32),
        lax.psum(grad_router.astype(jnp.bfloat16), "expert").astype(jnp.float32),
    )
    return (
        jnp.stack(outputs),
        jnp.stack(input_grads),
        grad_one,
        grad_qkv,
        grad_out,
        grad_two,
        grad_router,
        grad_gate,
        grad_up,
        grad_down,
    )


def solution(mesh):
    placed = (
        P(None, ("group", "expert"), None),
        P(None, ("group", "expert"), None),
        P(None, ("group", "expert"), None),
        P("group"),
        P("group", None),
        P("group", None),
        P("group"),
        P("group", None),
        P("expert", "group", None),
        P("expert", "group", None),
        P("expert", None, "group"),
    )
    return jax.shard_map(
        per_device,
        mesh=mesh,
        in_specs=placed,
        out_specs=(
            P(None, ("group", "expert"), None),
            P(None, ("group", "expert"), None),
            P("group"),
            P("group", None),
            P("group", None),
            P("group"),
            P("group", None),
            P("expert", "group", None),
            P("expert", "group", None),
            P("expert", None, "group"),
        ),
        check_vma=False,
    )
```

profile of v0, /device:TPU:0, one launch (start us, length us, event | category | flops | bytes accessed | tf_op | source)
XLA Modules:
  0.0 2031.5 jit_solution(14149869059944396973)
XLA Ops:
  8.6 13.6 all-gather
  23.7 129.7 %all-gather.12.cloned.1.call-done = bf16[1536,2560]{1,0:T(8,128)(2,1)} async-done(((bf16[384,2560]{1,0:T(8,128)(2,1)}), bf16[1536,2560]{1,0:T(8,128)(2,1)}) %all-gather.12.cloned.1.call-update) | async-done | bytes 7864336 | tf_op jit(solution)/shard_map/all_gather | solution.py:231
  168.8 12.1 all-gather.1
  208.6 17.4 while.108
  233.0 64.4 %all-gather.18.cloned.1.call-done = bf16[1536,1536]{1,0:T(8,128)(2,1)} async-done(((bf16[384,1536]{1,0:T(8,128)(2,1)}), bf16[1536,1536]{1,0:T(8,128)(2,1)}) %all-gather.18.cloned.1.call-update) | async-done | bytes 4718608 | tf_op jit(solution)/shard_map/all_gather | solution.py:232
  301.6 20.7 %scatter_custom_fusion = bf16[1536,1536]{1,0:T(8,128)(2,1)} fusion(s32[1024]{0:T(1024)S(1)} %bitcast.696, bf16[128,1536]{1,0:T(8,128)(2,1)} %multiply_convert_fusion.7, s32[1024]{0:T(1024)} %broadcast_clamp_fusion.2, bf16[]{:T(256)} %constant.915.clone.1), kind=kCustom, calls=%fused_computation.370 | custom fusion | bytes 4719104 | tf_op jit(solution)/shard_map/scatter | solution.py:298
  327.9 18.2 all_gather.54
  359.1 22.8 %all-to-all-done = bf16[8,4,48,1536]{3,2,1,0:T(8,128)(2,1)} async-done(((bf16[8,4,48,1536]{3,2,1,0:T(8,128)(2,1)}), bf16[8,4,48,1536]{3,2,1,0:T(8,128)(2,1)}, u32[]{:S(2)}, u32[]{:S(2)}) %all-to-all-start) | async-done | bytes 4718624 | tf_op jit(solution)/shard_map/all_to_all | solution.py:300
  391.3 49.9 %all-to-all-done.4 = bf16[8,4,48,1536]{3,2,1,0:T(8,128)(2,1)} async-done(((bf16[8,4,48,1536]{3,2,1,0:T(8,128)(2,1)}), bf16[8,4,48,1536]{3,2,1,0:T(8,128)(2,1)}, u32[]{:S(2)}, u32[]{:S(2)}) %all-to-all-start.4) | async-done | bytes 4718624 | tf_op jit(solution)/shard_map/all_to_all | solution.py:411
  454.6 74.5 %all-gather.22.cloned.1.call-done = bf16[4,1536,512]{2,1,0:T(8,128)(2,1)} async-done(((bf16[4,384,512]{2,1,0:T(8,128)(2,1)}), bf16[4,1536,512]{2,1,0:T(8,128)(2,1)}) %all-gather.22.cloned.1.call-update) | async-done | bytes 6291472 | tf_op jit(solution)/shard_map/all_gather | solution.py:236
  537.6 106.6 %all-gather.24.cloned.1.call-done = bf16[4,512,1536]{2,1,0:T(8,128)(2,1)} async-done(((bf16[4,512,384]{2,1,0:T(8,128)(2,1)}), bf16[4,512,1536]{2,1,0:T(8,128)(2,1)}) %all-gather.24.cloned.1.call-update) | async-done | bytes 6291472 | tf_op jit(solution)/shard_map/all_gather | solution.py:237
  644.2 11.2 multiply_convert_fusion.2
  695.4 24.9 %all-gather.28.cloned.1.call-done = bf16[1024,512]{0,1:T(8,128)(2,1)} async-done(((bf16[128,512]{0,1:T(8,128)(2,1)}), bf16[1024,512]{0,1:T(8,128)(2,1)}) %all-gather.28.cloned.1.call-update) | async-done | bytes 1048592 | tf_op jit(solution)/shard_map/all_gather | solution.py:65
  749.7 16.9 while.110
  833.7 19.2 scatter_custom_fusion.1
  867.3 45.3 %all-to-all-done.2 = bf16[8,4,48,1536]{3,2,1,0:T(8,128)(2,1)} async-done(((bf16[8,4,48,1536]{3,2,1,0:T(8,128)(2,1)}), bf16[8,4,48,1536]{3,2,1,0:T(8,128)(2,1)}, u32[]{:S(2)}, u32[]{:S(2)}) %all-to-all-start.2) | async-done | bytes 4718624 | tf_op jit(solution)/shard_map/all_to_all | solution.py:300
  922.3 49.7 %all-to-all-done.6 = bf16[8,4,48,1536]{3,2,1,0:T(8,128)(2,1)} async-done(((bf16[8,4,48,1536]{3,2,1,0:T(8,128)(2,1)}), bf16[8,4,48,1536]{3,2,1,0:T(8,128)(2,1)}, u32[]{:S(2)}, u32[]{:S(2)}) %all-to-all-start.6) | async-done | bytes 4718624 | tf_op jit(solution)/shard_map/all_to_all | solution.py:411
  1033.0 43.3 %all-to-all-done.7 = bf16[1,4,384,1536]{3,1,0,2:T(4,128)(2,1)} async-done(((bf16[1,4,384,1536]{3,1,0,2:T(4,128)(2,1)}), bf16[1,4,384,1536]{3,1,0,2:T(4,128)(2,1)}, u32[]{:S(2)}, u32[]{:S(2)}) %all-to-all-start.7) | async-done | bytes 4718624 | tf_op jit(solution)/shard_map/all_to_all | solution.py:443
  1101.9 33.7 %all-to-all-done.3 = bf16[1,4,384,1536]{3,1,0,2:T(4,128)(2,1)} async-done(((bf16[1,4,384,1536]{3,1,0,2:T(4,128)(2,1)}), bf16[1,4,384,1536]{3,1,0,2:T(4,128)(2,1)}, u32[]{:S(2)}, u32[]{:S(2)}) %all-to-all-start.3) | async-done | bytes 4718624 | tf_op jit(solution)/shard_map/all_to_all | solution.py:316
  1173.5 28.6 %while.112 = (s32[]{:T(128)}, f32[128,8,3,64]{0,3,2,1:T(8,128)}, bf16[2,512,8,64]{1,3,2,0:T(8,128)(2,1)}, bf16[2,512,8,64]{1,3,2,0:T(8,128)(2,1)}, bf16[2,512,8,...) while((s32[]{:T(128)}, f32[128,8,3,64]{0,3,2,1:T(8,128)}, ...), condition=%wide.region_40.41_spmd.clone.clone.clone, body=%wide.region_39.40_spmd.clone.clone.clone.sunk | while | flops 1023516416 | bytes 102131216 | solution.py:195
  1209.1 24.6 %while.113 = (s32[]{:T(128)}, f32[128,8,3,64]{0,3,2,1:T(8,128)}, bf16[2,512,8,64]{1,3,2,0:T(8,128)(2,1)}, bf16[2,512,8,64]{1,3,2,0:T(8,128)(2,1)}, bf16[2,512,8,...) while((s32[]{:T(128)}, f32[128,8,3,64]{0,3,2,1:T(8,128)}, ...), condition=%wide.region_52.53_spmd.clone.clone.clone, body=%wide.region_51.52_spmd.clone.clone.clone.sunk | while | flops 1023516416 | bytes 102131216 | solution.py:195
  1266.3 12.2 reduce-scatter.35.cloned.1.call-done
  1279.6 38.5 %reduce-scatter.37.cloned.1.call-done = bf16[128,512]{1,0:T(8,128)(2,1)} async-done(((bf16[1024,512]{1,0:T(8,128)(2,1)}), bf16[128,512]{1,0:T(8,128)(2,1)}) %reduce-scatter.37.cloned.1.call-update) | async-done | bytes 131088
  1319.2 38.1 %reduce-scatter.33.cloned.1.call-done = bf16[128,512]{1,0:T(8,128)(2,1)} async-done(((bf16[1024,512]{1,0:T(8,128)(2,1)}), bf16[128,512]{1,0:T(8,128)(2,1)}) %reduce-scatter.33.cloned.1.call-update) | async-done | bytes 131088
  1391.8 11.2 copy.347
  1471.6 133.3 %reduce-scatter.23.cloned.1.call-done = bf16[384,2560]{1,0:T(8,128)(2,1)} async-done(((bf16[1536,2560]{1,0:T(8,128)(2,1)}), bf16[384,2560]{1,0:T(8,128)(2,1)}) %reduce-scatter.23.cloned.1.call-update) | async-done | bytes 1966096 | tf_op jit(solution)/shard_map/reduce_scatter | solution.py:512
  1605.0 11.2 all-reduce.4
  1616.4 23.3 %all-reduce.2 = (bf16[384]{0:T(512)(128)(2,1)S(1)}, bf16[384]{0:T(512)(128)(2,1)S(1)}, bf16[384,32]{0,1:T(8,128)(2,1)S(1)}) all-reduce(bf16[384]{0:T(512)(128)(2,1)S(1)} %dynamic-slice.1, bf16[384]{0:T(512)(128)(2,1)S(1)} %dynamic-slice.3, bf16[384,32]{0,1:T(8,128)(2,1)S(1)} %copy-done.90), channel_id=1, replica_groups=mesh['group'=4,'expert'=8] {'expert'}, use_global_device_ids=true, to_apply=%region_59.60 | all-reduce | flops 13056 | bytes 52224 | tf_op jit(solution)/shard_map/psum | solution.py:536
  1644.4 74.0 %reduce-scatter.41.cloned.1.call-done = bf16[384,2048]{1,0:T(8,128)(2,1)} async-done(((bf16[1536,2048]{1,0:T(8,128)(2,1)}), bf16[384,2048]{1,0:T(8,128)(2,1)}) %reduce-scatter.41.cloned.1.call-update) | async-done | bytes 1572880
  1724.8 107.1 %reduce-scatter.27.cloned.1.call-done = bf16[4,384,512]{2,1,0:T(8,128)(2,1)} async-done(((bf16[4,1536,512]{2,1,0:T(8,128)(2,1)}), bf16[4,384,512]{2,1,0:T(8,128)(2,1)}) %reduce-scatter.27.cloned.1.call-update) | async-done | bytes 1572880 | tf_op jit(solution)/shard_map/reduce_scatter | solution.py:524
  1835.4 110.1 %reduce-scatter.29.cloned.1.call-done = bf16[4,384,512]{2,1,0:T(8,128)(2,1)} async-done(((bf16[4,1536,512]{2,1,0:T(8,128)(2,1)}), bf16[4,384,512]{2,1,0:T(8,128)(2,1)}) %reduce-scatter.29.cloned.1.call-update) | async-done | bytes 1572880 | tf_op jit(solution)/shard_map/reduce_scatter | solution.py:527
  1949.0 69.6 %all-reduce.7.cloned.1.call-done = (bf16[384,2560]{1,0:T(8,128)(2,1)}, bf16[384,1536]{1,0:T(8,128)(2,1)}) async-done(((bf16[384,2560]{1,0:T(8,128)(2,1)}, bf16[384,1536]{1,0:T(8,128)(2,1)}), (bf16[384,2560]{1,0:T(8,128)(2,1)}, bf16[384,1536]{1,0:T(8,128)(2,1)})) %all-reduce.7.cloned.1.call-update) | async-done | bytes 3145744 | tf_op jit(solution)/shard_map/psum | solution.py:537
  (701 shorter events, 659.3 us)
Async XLA Ops:
  7.2 146.2 %all-gather.12.cloned.1.call-start = ((), (), s32[]{:S(2)}) async-start(), calls=%async_computation.18 | async-start | bytes 9830400 | tf_op jit(solution)/shard_map/all_gather | solution.py:231
  7.9 187.1 %all-gather.14.cloned.1.call-start = ((), (), s32[]{:S(2)}) async-start(), calls=%async_computation.19 | async-start | bytes 1179648 | tf_op jit(solution)/shard_map/all_gather | solution.py:66
  158.8 47.7 %all-gather.16.cloned.1.call-start = ((), (), s32[]{:S(2)}) async-start(), calls=%async_computation.20 | async-start | bytes 1179648 | tf_op jit(solution)/shard_map/all_gather | solution.py:65
  166.1 131.3 %all-gather.18.cloned.1.call-start = ((), (), s32[]{:S(2)}) async-start(), calls=%async_computation.21 | async-start | bytes 5898240 | tf_op jit(solution)/shard_map/all_gather | solution.py:232
  166.7 279.3 %all-gather.20.cloned.1.call-start = ((), (), s32[]{:S(2)}) async-start(), calls=%async_computation.22 | async-start | bytes 7864320 | tf_op jit(solution)/shard_map/all_gather | solution.py:235
  167.3 361.8 %all-gather.22.cloned.1.call-start = ((), (), s32[]{:S(2)}) async-start(), calls=%async_computation.23 | async-start | bytes 7864320 | tf_op jit(solution)/shard_map/all_gather | solution.py:236
  191.3 158.6 %copy-start.107 = (s32[1024,1]{0,1:T(1,128)}, s32[1024,1]{0,1:T(1,128)S(1)}, u32[]{:S(2)}) copy-start(s32[1024,1]{0,1:T(1,128)S(1)} %compare_select_fusion.86) | copy-start | bytes 12292
  322.4 59.5 %all-to-all-start = ((bf16[8,4,48,1536]{3,2,1,0:T(8,128)(2,1)}), bf16[8,4,48,1536]{3,2,1,0:T(8,128)(2,1)}, u32[]{:S(2)}, u32[]{:S(2)}) async-start(bf16[8,4,48,1536]{3,2,1,0:T(8,128)(2,1)} %bitcast.641), calls=%async_computation | async-start | bytes 9437184 | tf_op jit(solution)/shard_map/all_to_all | solution.py:300
  327.1 317.1 %all-gather.24.cloned.1.call-start = ((), (), s32[]{:S(2)}) async-start(), calls=%async_computation.24 | async-start | bytes 7864320 | tf_op jit(solution)/shard_map/all_gather | solution.py:237
  381.8 59.3 %all-to-all-start.4 = ((bf16[8,4,48,1536]{3,2,1,0:T(8,128)(2,1)}), bf16[8,4,48,1536]{3,2,1,0:T(8,128)(2,1)}, u32[]{:S(2)}, u32[]{:S(2)}) async-start(bf16[8,4,48,1536]{3,2,1,0:T(8,128)(2,1)} %bitcast.643), calls=%async_computation.4 | async-start | bytes 9437184 | tf_op jit(solution)/shard_map/all_to_all | solution.py:411
  677.5 67.4 %all-to-all-start.5 = ((bf16[1,4,384,1536]{3,1,0,2:T(4,128)(2,1)}), bf16[1,4,384,1536]{3,1,0,2:T(4,128)(2,1)}, u32[]{:S(2)}, u32[]{:S(2)}) async-start(bf16[1,4,384,1536]{3,1,0,2:T(4,128)(2,1)} %copy.283), calls=%async_computation.5 | async-start | bytes 9437184 | tf_op jit(solution)/shard_map/all_to_all | solution.py:443
  682.2 38.1 %all-gather.28.cloned.1.call-start = ((), (), s32[]{:S(2)}) async-start(), calls=%async_computation.26 | async-start | bytes 1179648 | tf_op jit(solution)/shard_map/all_gather | solution.py:65
  683.0 83.7 %all-gather.26.cloned.1.call-start = ((), (), s32[]{:S(2)}) async-start(), calls=%async_computation.25 | async-start | bytes 1179648 | tf_op jit(solution)/shard_map/all_gather | solution.py:66
  744.8 64.5 %all-to-all-start.1 = ((bf16[1,4,384,1536]{3,1,0,2:T(4,128)(2,1)}), bf16[1,4,384,1536]{3,1,0,2:T(4,128)(2,1)}, u32[]{:S(2)}, u32[]{:S(2)}) async-start(bf16[1,4,384,1536]{3,1,0,2:T(4,128)(2,1)} %copy.264), calls=%async_computation.1 | async-start | bytes 9437184 | tf_op jit(solution)/shard_map/all_to_all | solution.py:316
  852.9 59.7 %all-to-all-start.2 = ((bf16[8,4,48,1536]{3,2,1,0:T(8,128)(2,1)}), bf16[8,4,48,1536]{3,2,1,0:T(8,128)(2,1)}, u32[]{:S(2)}, u32[]{:S(2)}) async-start(bf16[8,4,48,1536]{3,2,1,0:T(8,128)(2,1)} %bitcast.642), calls=%async_computation.2 | async-start | bytes 9437184 | tf_op jit(solution)/shard_map/all_to_all | solution.py:300
  912.6 59.3 %all-to-all-start.6 = ((bf16[8,4,48,1536]{3,2,1,0:T(8,128)(2,1)}), bf16[8,4,48,1536]{3,2,1,0:T(8,128)(2,1)}, u32[]{:S(2)}, u32[]{:S(2)}) async-start(bf16[8,4,48,1536]{3,2,1,0:T(8,128)(2,1)} %bitcast.644), calls=%async_computation.6 | async-start | bytes 9437184 | tf_op jit(solution)/shard_map/all_to_all | solution.py:411
  1016.8 59.5 %all-to-all-start.7 = ((bf16[1,4,384,1536]{3,1,0,2:T(4,128)(2,1)}), bf16[1,4,384,1536]{3,1,0,2:T(4,128)(2,1)}, u32[]{:S(2)}, u32[]{:S(2)}) async-start(bf16[1,4,384,1536]{3,1,0,2:T(4,128)(2,1)} %copy.294), calls=%async_computation.7 | async-start | bytes 9437184 | tf_op jit(solution)/shard_map/all_to_all | solution.py:443
  1076.2 59.4 %all-to-all-start.3 = ((bf16[1,4,384,1536]{3,1,0,2:T(4,128)(2,1)}), bf16[1,4,384,1536]{3,1,0,2:T(4,128)(2,1)}, u32[]{:S(2)}, u32[]{:S(2)}) async-start(bf16[1,4,384,1536]{3,1,0,2:T(4,128)(2,1)} %copy.279), calls=%async_computation.3 | async-start | bytes 9437184 | tf_op jit(solution)/shard_map/all_to_all | solution.py:316
  1080.9 184.2 %reduce-scatter.31.cloned.1.call-start = ((), (), s32[]{:S(2)}) async-start(), calls=%async_computation.31 | async-start | bytes 1179648
  1206.8 71.7 %reduce-scatter.35.cloned.1.call-start = ((), (), s32[]{:S(2)}) async-start(), calls=%async_computation.33 | async-start | bytes 1179648
  1238.5 79.6 %reduce-scatter.37.cloned.1.call-start = ((), (), s32[]{:S(2)}) async-start(), calls=%async_computation.34 | async-start | bytes 1179648
  1242.4 114.9 %reduce-scatter.33.cloned.1.call-start = ((), (), s32[]{:S(2)}) async-start(), calls=%async_computation.32 | async-start | bytes 1179648
  1247.2 209.4 %reduce-scatter.39.cloned.1.call-start = ((), (), s32[]{:S(2)}) async-start(), calls=%async_computation.35 | async-start | bytes 491520
  1255.9 215.7 %reduce-scatter.25.cloned.1.call-start = ((), (), s32[]{:S(2)}) async-start(), calls=%async_computation.28 | async-start | bytes 5898240 | tf_op jit(solution)/shard_map/reduce_scatter | solution.py:515
  1263.4 341.5 %reduce-scatter.23.cloned.1.call-start = ((), (), s32[]{:S(2)}) async-start(), calls=%async_computation.27 | async-start | bytes 9830400 | tf_op jit(solution)/shard_map/reduce_scatter | solution.py:512
  1376.8 341.7 %reduce-scatter.41.cloned.1.call-start = ((), (), s32[]{:S(2)}) async-start(), calls=%async_computation.36 | async-start | bytes 7864320
  1411.3 420.6 %reduce-scatter.27.cloned.1.call-start = ((), (), s32[]{:S(2)}) async-start(), calls=%async_computation.29 | async-start | bytes 7864320 | tf_op jit(solution)/shard_map/reduce_scatter | solution.py:524
  1432.5 512.9 %reduce-scatter.29.cloned.1.call-start = ((), (), s32[]{:S(2)}) async-start(), calls=%async_computation.30 | async-start | bytes 7864320 | tf_op jit(solution)/shard_map/reduce_scatter | solution.py:527
  1453.8 564.8 %all-reduce.7.cloned.1.call-start = ((), (), s32[]{:S(2)}) async-start(), calls=%async_computation.37 | async-start | bytes 6291456 | tf_op jit(solution)/shard_map/psum | solution.py:537
  1464.3 177.2 %copy-start.23 = (f32[128,1536]{1,0:T(8,128)S(1)}, f32[128,1536]{1,0:T(8,128)}, u32[]{:S(2)}) copy-start(f32[128,1536]{1,0:T(8,128)} %copy-done.21) | copy-start | bytes 2359300
  1464.3 177.2 %copy-start.26 = (f32[128,1536]{1,0:T(8,128)S(1)}, f32[128,1536]{1,0:T(8,128)}, u32[]{:S(2)}) copy-start(f32[128,1536]{1,0:T(8,128)} %copy-done.24) | copy-start | bytes 2359300
  1464.4 177.2 %copy-start.114 = (f32[128]{0:T(128)S(1)}, f32[128]{0:T(128)}, u32[]{:S(2)}) copy-start(f32[128]{0:T(128)} %copy-done.112) | copy-start | bytes 1540
  (155 other events, 2562.4 us)
Sparse Core Ops, SparseCore 0:
  9.6 143.7 all-gather.11
  158.9 21.5 all-gather.13
  183.0 23.5 all-gather.15
  208.0 89.3 all-gather.17
  298.8 115.2 all-gather.19
  415.5 113.5 all-gather.21
  530.7 113.5 all-gather.23
  685.5 34.7 all-gather.27
  722.8 23.9 all-gather.25
  1207.0 32.3 reduce-scatter.30
  1242.5 35.9 reduce-scatter.34
  1282.1 35.9 reduce-scatter.36
  1321.3 35.9 reduce-scatter.32
  1359.4 20.8 reduce-scatter.38
  1382.4 83.4 reduce-scatter.24
  1468.1 136.7 reduce-scatter.22
  1607.1 111.3 reduce-scatter.40
  1720.6 111.1 reduce-scatter.26
  1834.2 111.2 reduce-scatter.28
  1948.7 69.8 all-reduce.6
where the time goes:
time: 2040 us; the launch traced here: 2030 us
  waiting for transfers between devices  1240 us (61%)
  matrix products  286 us (14%)
  local copies, waits for them, and re-layouts  247 us (12%)
  other arithmetic  117 us (6%)
  blocking collectives  78.5 us (4%)
  starting transfers between devices  39.7 us (2%)
    unnamed x26, waiting for transfers between devices  166 us
    reduce_scatter x1, waiting for transfers between devices, per_device(): lax.psum_scatter(acc_qkv.astype(jnp.bfloat16), 'group', scatter_dimension...  133 us
    all_gather x1, waiting for transfers between devices, per_device(): lax.all_gather(query_key_value_weight, 'group', axis=0, tiled=True)  130 us
    reduce_scatter x1, waiting for transfers between devices, per_device(): lax.psum_scatter(acc_up.astype(jnp.bfloat16), 'group', scatter_dimension=...  110 us
    reduce_scatter x1, waiting for transfers between devices, per_device(): lax.psum_scatter(acc_gate.astype(jnp.bfloat16), 'group', scatter_dimensio...  107 us
    all_gather x1, waiting for transfers between devices, per_device(): lax.all_gather(down_weight, 'group', axis=2, tiled=True)  107 us
    all_to_all x2, waiting for transfers between devices, per_device(): lax.all_to_all(grad_rows.reshape(expert_count, exp_here, slot_cap, MODEL_...  99.5 us
    all_gather x1, waiting for transfers between devices, per_device(): lax.all_gather(up_weight, 'group', axis=1, tiled=True)  74.5 us
  transfers between devices with their start and end apart: 28, of which 21 were waited for; matrix products, arithmetic and copies ran while one was open for 22% of the time, Pallas kernels for 0%

commit v1 on v0

v1 whole, which is shorter than its diff:
```python
import functools

import jax
import jax.numpy as jnp
from jax import lax
from jax.experimental import pallas as pl
from jax.experimental.pallas import tpu as pltpu
from jax.sharding import PartitionSpec as P

QUERY_HEADS = 24
KEY_VALUE_HEADS = 8
HEAD_SIZE = 64
TOPK = 8
CONT = 256
PR_DEV = 64
LANES = 128
SCORE_SCALE = 0.125
NEG_FILL = -1e30
HIGHEST = lax.Precision.HIGHEST
F32 = jnp.float32
BF16 = jnp.bfloat16

NN = (((1,), (0,)), ((), ()))
NT = (((1,), (1,)), ((), ()))
TN = (((0,), (0,)), ((), ()))


def mm(a, b, dims=NN):
    return lax.dot_general(a, b, dims, preferred_element_type=F32)


def swap(x, bit):
    n = lax.axis_size("expert")
    return lax.ppermute(x, "expert", [(i, i ^ bit) for i in range(n)])


def shift(x, step):
    n = lax.axis_size("group")
    return lax.ppermute(x, "group", [(i, (i + step) % n) for i in range(n)])


def turn(x, step, split):
    n = lax.axis_size("group")
    return lax.ppermute(
        x, "group", [((i // split) * split + (i + step) % split, i) for i in range(n)]
    )


def outer_bits(n):
    return [1 << i for i in range(1, n.bit_length() - 1)]


def spread(x, order):
    n = lax.axis_size("expert")
    outer = outer_bits(n)
    if len(outer) == 2:
        a, b = outer
        xa, xb = swap(x, a), swap(x, b)
        slots = {0: x, a: xa, b: xb, a ^ b: swap(xa, b) if order == 0 else swap(xb, a)}
    else:
        slots = {0: x}
        for bit in outer:
            slots.update({r ^ bit: swap(y, bit) for r, y in list(slots.items())})
    if n > 1:
        slots.update({r ^ 1: swap(y, 1) for r, y in list(slots.items())})
    return [slots[r] for r in range(n)]


def plus(a, b):
    return (a.astype(F32) + b.astype(F32)).astype(BF16)


def collect(parts, order):
    n = lax.axis_size("expert")
    outer = outer_bits(n)
    keep = {r: parts[r] for r in range(n)}
    if n > 1:
        keep = {r: plus(keep[r], swap(keep[r ^ 1], 1)) for r in range(0, n, 2)}
    if len(outer) == 2:
        a, b = outer
        if order == 0:
            keep[a] = plus(keep[a], swap(keep[a ^ b], b))
        else:
            keep[b] = plus(keep[b], swap(keep[a ^ b], a))
        return (
            keep[0].astype(F32) + swap(keep[a], a).astype(F32) + swap(keep[b], b).astype(F32)
        )
    for bit in reversed(outer):
        keep = {r: plus(keep[r], swap(keep[r ^ bit], bit)) for r in keep if not r & bit}
    return keep[0].astype(F32)


def full_spec(shape):
    return pl.BlockSpec(shape, lambda *_: (0,) * len(shape))


SMEM_SPEC = pl.BlockSpec(memory_space=pltpu.SMEM)
ANY_SPEC = pl.BlockSpec(memory_space=pl.ANY)


def cost(flops, moved):
    return pl.CostEstimate(flops=int(flops), bytes_accessed=int(moved), transcendentals=0)


def assemble(pieces, place, shape, where):
    count = len(pieces)

    def kernel(at_ref, *refs):
        ins, out, sems = refs[:count], refs[count], refs[count + 1]
        copies = []
        for i in range(count):
            row, column = place(i, at_ref[0], at_ref[1])
            r, c = pieces[i].shape
            copies.append(
                pltpu.make_async_copy(
                    ins[i],
                    out.at[pl.ds(pl.multiple_of(row, 16), r), pl.ds(pl.multiple_of(column, 128), c)],
                    sems.at[i],
                )
            )
        for one in copies:
            one.start()
        for one in copies:
            one.wait()

    return pl.pallas_call(
        kernel,
        grid=(1,),
        in_specs=[SMEM_SPEC] + [ANY_SPEC] * count,
        out_specs=full_spec(shape),
        out_shape=jax.ShapeDtypeStruct(shape, pieces[0].dtype),
        scratch_shapes=[pltpu.SemaphoreType.DMA((count,))],
        cost_estimate=cost(0, 4 * shape[0] * shape[1]),
        name="assemble",
    )(where, *pieces)


def gather_dense(piece, cuts, where):
    groups, n = lax.axis_size("group"), lax.axis_size("expert")
    rows, columns = piece.shape
    own = [piece[:, lo:hi] for lo, hi in cuts]
    far = [[shift(x, s) for x in own] for s in range(1, groups)]
    names, pieces = [], []
    for h, (lo, hi) in enumerate(cuts):
        joined = jnp.concatenate([far[s - 1][h] for s in range(1, groups)], axis=0)
        for r, x in enumerate(spread(own[h], h % 2)):
            names.append((0, r, lo))
            pieces.append(x)
        for r, x in enumerate(spread(joined, h % 2)):
            for s in range(1, groups):
                names.append((s, r, lo))
                pieces.append((x, (s - 1) * rows, rows))
    total = groups * n * rows
    arrays, index = [], []
    for entry in pieces:
        if isinstance(entry, tuple):
            if not arrays or arrays[-1] is not entry[0]:
                arrays.append(entry[0])
            index.append((len(arrays) - 1, entry[1], entry[2]))
        else:
            arrays.append(entry)
            index.append((len(arrays) - 1, 0, rows))
    count, held = len(index), len(arrays)

    def kernel(at_ref, *refs):
        ins, out, sems = refs[:held], refs[held], refs[held + 1]
        copies = []
        for i, (which, start, size) in enumerate(index):
            s, r, lo = names[i]
            z = lax.rem(at_ref[0] - s + groups, groups)
            e = jnp.bitwise_xor(at_ref[1], r)
            row = pl.multiple_of((z * n + e) * rows, 16)
            width = arrays[which].shape[1]
            copies.append(
                pltpu.make_async_copy(
                    ins[which].at[pl.ds(start, size)],
                    out.at[pl.ds(row, rows), pl.ds(lo, width)],
                    sems.at[i],
                )
            )
        for one in copies:
            one.start()
        for one in copies:
            one.wait()

    whole = pl.pallas_call(
        kernel,
        grid=(1,),
        in_specs=[SMEM_SPEC] + [ANY_SPEC] * held,
        out_specs=full_spec((total, columns)),
        out_shape=jax.ShapeDtypeStruct((total, columns), piece.dtype),
        scratch_shapes=[pltpu.SemaphoreType.DMA((count,))],
        cost_estimate=cost(0, 4 * total * columns),
        name="join_rows",
    )(where, *arrays)
    return whole, far


def sliced_outer(a, b, extra, groups, n, where):
    depth = a.shape[1]
    columns = b.shape[1]
    more = 0 if extra is None else extra.shape[1]
    rows = depth // (groups * n)

    def kernel(at_ref, a_ref, b_ref, *refs):
        if more:
            x_ref, refs = refs[0], refs[1:]
        outs, acc = refs[:n], refs[n]
        acc[:, :columns] = mm(a_ref[...], b_ref[...], TN)
        if more:
            acc[:, columns:] = x_ref[...]
        for r in range(n):
            e = jnp.bitwise_xor(at_ref[1], r)
            for s in range(groups):
                z = lax.rem(at_ref[0] + s, groups)
                row = pl.multiple_of((z * n + e) * rows, 16)
                outs[r][s] = acc[pl.ds(row, rows), :].astype(BF16)

    width = columns + more
    return pl.pallas_call(
        kernel,
        grid=(1,),
        in_specs=[SMEM_SPEC, full_spec(a.shape), full_spec(b.shape)]
        + ([full_spec(extra.shape)] if more else []),
        out_specs=[full_spec((groups, rows, width))] * n,
        out_shape=[jax.ShapeDtypeStruct((groups, rows, width), BF16)] * n,
        scratch_shapes=[pltpu.VMEM((depth, width), F32)],
        cost_estimate=cost(2 * a.shape[0] * depth * columns, 2 * depth * width),
        name="sliced_outer",
    )(where, a, b, *([extra] if more else []))


def reduce_dense(parts, order, where):
    groups, n = lax.axis_size("group"), lax.axis_size("expert")
    mine = collect(parts, order)
    total = mine[0]
    low = mine.astype(BF16)
    for s in range(1, groups):
        total = total + shift(low[s], s).astype(F32)
    rows, width = total.shape
    slots = spread(total.astype(BF16), order)

    def kernel(at_ref, *refs):
        out = refs[n]
        for r in range(n):
            e = jnp.bitwise_xor(at_ref[1], r)
            out[pl.ds(pl.multiple_of(e * rows, 16), rows), :] = refs[r][...].astype(F32)

    return pl.pallas_call(
        kernel,
        grid=(1,),
        in_specs=[SMEM_SPEC] + [full_spec((rows, width))] * n,
        out_specs=full_spec((n * rows, width)),
        out_shape=jax.ShapeDtypeStruct((n * rows, width), F32),
        cost_estimate=cost(0, 6 * n * rows * width),
        name="join_sums",
    )(where, *slots)


def attention_masks(n, me):
    shape = (3 * PR_DEV, n * PR_DEV)
    token = lax.rem(lax.broadcasted_iota(jnp.int32, shape, 0), PR_DEV)
    column = lax.broadcasted_iota(jnp.int32, shape, 1)
    key_pos = jnp.bitwise_xor(column // PR_DEV, me) * PR_DEV + lax.rem(column, PR_DEV)
    prompt_ok = key_pos <= me * PR_DEV + token
    slots = CONT // PR_DEV
    shape = (3 * PR_DEV, CONT)
    token = lax.rem(lax.broadcasted_iota(jnp.int32, shape, 0), PR_DEV)
    column = lax.broadcasted_iota(jnp.int32, shape, 1)
    owner = jnp.bitwise_xor(column // PR_DEV, lax.rem(me, slots))
    cont_ok = owner * PR_DEV + lax.rem(column, PR_DEV) <= lax.rem(me, slots) * PR_DEV + token
    return prompt_ok, cont_ok


def head_rows(x, base):
    return jnp.concatenate(
        [x[:, base + i * HEAD_SIZE : base + (i + 1) * HEAD_SIZE] for i in range(3)], axis=0
    )


def row_heads(x):
    return jnp.concatenate([x[i * PR_DEV : (i + 1) * PR_DEV] for i in range(3)], axis=1)


def softmax(scores):
    top = jnp.max(scores, axis=1, keepdims=True)
    weight = jnp.exp(scores - top)
    return weight * (1.0 / jnp.sum(weight, axis=1, keepdims=True))


def load_keys(n, kv_refs, keys):
    for r in range(n):
        keys[r * PR_DEV : (r + 1) * PR_DEV, :] = kv_refs[r][:PR_DEV, :]
    for r in range(CONT // PR_DEV):
        lo = (n + r) * PR_DEV
        keys[lo : lo + PR_DEV, :] = kv_refs[r][PR_DEV:, :]


def group_probs(q_top, q_low, key, prompt_ok, cont_ok, n):
    pr = n * PR_DEV
    top = mm(q_top, key[:pr], NT) * SCORE_SCALE
    top = softmax(jnp.where(prompt_ok, top, NEG_FILL))
    low = mm(q_low, key, NT) * SCORE_SCALE
    low = jnp.concatenate([low[:, :pr], jnp.where(cont_ok, low[:, pr:], NEG_FILL)], axis=1)
    return top, softmax(low)


def attention_forward(query, slots, where):
    n = len(slots)
    width = KEY_VALUE_HEADS * HEAD_SIZE
    tokens = 2 * PR_DEV
    total = n * PR_DEV + CONT

    def kernel(at_ref, q_ref, *refs):
        kv_refs, out_ref, keys = refs[:n], refs[n], refs[n + 1]
        load_keys(n, kv_refs, keys)
        prompt_ok, cont_ok = attention_masks(n, at_ref[1])

        def pair(j, carry):
            q_at = pl.ds(pl.multiple_of(j * 384, 128), 384)
            k_at = pl.ds(pl.multiple_of(j * 128, 128), 128)
            v_at = pl.ds(pl.multiple_of(width + j * 128, 128), 128)
            q_top, q_low = q_ref[:PR_DEV, q_at], q_ref[PR_DEV:, q_at]
            k_two, v_two = keys[:, k_at], keys[:, v_at]
            tops, lows = [], []
            for g in range(2):
                key = k_two[:, g * HEAD_SIZE : (g + 1) * HEAD_SIZE]
                value = v_two[:, g * HEAD_SIZE : (g + 1) * HEAD_SIZE]
                top, low = group_probs(
                    head_rows(q_top, g * 192), head_rows(q_low, g * 192), key, prompt_ok, cont_ok, n
                )
                tops.append(row_heads(mm(top.astype(BF16), value[: n * PR_DEV])))
                lows.append(row_heads(mm(low.astype(BF16), value)))
            out_ref[:PR_DEV, q_at] = jnp.concatenate(tops, axis=1).astype(BF16)
            out_ref[PR_DEV:, q_at] = jnp.concatenate(lows, axis=1).astype(BF16)
            return carry

        lax.fori_loop(0, KEY_VALUE_HEADS // 2, pair, 0)

    return pl.pallas_call(
        kernel,
        grid=(1,),
        in_specs=[SMEM_SPEC, full_spec(query.shape)] + [full_spec((tokens, 2 * width))] * n,
        out_specs=full_spec(query.shape),
        out_shape=jax.ShapeDtypeStruct(query.shape, BF16),
        scratch_shapes=[pltpu.VMEM((total, 2 * width), BF16)],
        cost_estimate=cost(8e9, 4e6),
        name="attention_forward",
    )(where, query, *slots)


def attention_backward(query, slots, d_mixed, where):
    n = len(slots)
    width = KEY_VALUE_HEADS * HEAD_SIZE
    tokens = 2 * PR_DEV
    pr = n * PR_DEV
    total = pr + CONT

    def kernel(at_ref, q_ref, d_ref, *refs):
        kv_refs, refs = refs[:n], refs[n:]
        dq_ref, outs, keys, grads = refs[0], refs[1 : 1 + n], refs[1 + n], refs[2 + n]
        load_keys(n, kv_refs, keys)
        prompt_ok, cont_ok = attention_masks(n, at_ref[1])

        def one_side(prob, d_rows, key, value, q_rows):
            d_prob = mm(d_rows, value, NT)
            delta = jnp.sum(prob * d_prob, axis=1, keepdims=True)
            d_score = (prob * (d_prob - delta)).astype(BF16)
            return (
                mm(d_score, key) * SCORE_SCALE,
                mm(d_score, q_rows, TN) * SCORE_SCALE,
                mm(prob.astype(BF16), d_rows, TN),
            )

        def pair(j, carry):
            q_at = pl.ds(pl.multiple_of(j * 384, 128), 384)
            k_at = pl.ds(pl.multiple_of(j * 128, 128), 128)
            v_at = pl.ds(pl.multiple_of(width + j * 128, 128), 128)
            q_top, q_low = q_ref[:PR_DEV, q_at], q_ref[PR_DEV:, q_at]
            d_top, d_low = d_ref[:PR_DEV, q_at], d_ref[PR_DEV:, q_at]
            k_two, v_two = keys[:, k_at], keys[:, v_at]
            dq_tops, dq_lows, dks, dvs = [], [], [], []
            for g in range(2):
                key = k_two[:, g * HEAD_SIZE : (g + 1) * HEAD_SIZE]
                value = v_two[:, g * HEAD_SIZE : (g + 1) * HEAD_SIZE]
                rows_top, rows_low = head_rows(q_top, g * 192), head_rows(q_low, g * 192)
                top, low = group_probs(rows_top, rows_low, key, prompt_ok, cont_ok, n)
                dq_top, dk_top, dv_top = one_side(
                    top, head_rows(d_top, g * 192), key[:pr], value[:pr], rows_top
                )
                dq_low, dk_low, dv_low = one_side(
                    low, head_rows(d_low, g * 192), key, value, rows_low
                )
                dq_tops.append(row_heads(dq_top))
                dq_lows.append(row_heads(dq_low))
                dks.append(jnp.concatenate([dk_low[:pr] + dk_top, dk_low[pr:]], axis=0))
                dvs.append(jnp.concatenate([dv_low[:pr] + dv_top, dv_low[pr:]], axis=0))
            dq_ref[:PR_DEV, q_at] = jnp.concatenate(dq_tops, axis=1)
            dq_ref[PR_DEV:, q_at] = jnp.concatenate(dq_lows, axis=1)
            grads[:, k_at] = jnp.concatenate(dks, axis=1).astype(BF16)
            grads[:, v_at] = jnp.concatenate(dvs, axis=1).astype(BF16)
            return carry

        lax.fori_loop(0, KEY_VALUE_HEADS // 2, pair, 0)
        for r in range(n):
            outs[r][:PR_DEV, :] = grads[r * PR_DEV : (r + 1) * PR_DEV, :]
            if r < CONT // PR_DEV:
                lo = (n + r) * PR_DEV
                outs[r][PR_DEV:, :] = grads[lo : lo + PR_DEV, :]
            else:
                outs[r][PR_DEV:, :] = jnp.zeros((PR_DEV, 2 * width), BF16)

    out = pl.pallas_call(
        kernel,
        grid=(1,),
        in_specs=[SMEM_SPEC, full_spec(query.shape), full_spec(query.shape)]
        + [full_spec((tokens, 2 * width))] * n,
        out_specs=[full_spec(query.shape)] + [full_spec((tokens, 2 * width))] * n,
        out_shape=[jax.ShapeDtypeStruct(query.shape, F32)]
        + [jax.ShapeDtypeStruct((tokens, 2 * width), BF16)] * n,
        scratch_shapes=[pltpu.VMEM((total, 2 * width), BF16), pltpu.VMEM((total, 2 * width), BF16)],
        cost_estimate=cost(2e10, 8e6),
        name="attention_backward",
    )(where, query, d_mixed, *slots)
    return out[0], out[1:]


def pick(slot_row, cap):
    rows = lax.broadcasted_iota(jnp.int32, (cap, slot_row.shape[1]), 0).astype(F32)
    return jnp.where(slot_row == rows, 1.0, 0.0).astype(BF16)


def dispatch_grads(arrays, at, per, cap, model, buffers, place, blocks_total):
    count = len(arrays)
    split, tokens, width = arrays[0].shape
    blocks = count * split
    first = buffers is None

    def kernel(at_ref, *refs):
        ins = refs[:count]
        out, ranks = refs[-3], refs[-2]
        flags = refs[-1]
        row = lax.broadcasted_iota(jnp.int32, (tokens, tokens), 0)
        col = lax.broadcasted_iota(jnp.int32, (tokens, tokens), 1)
        before = jnp.where(row < col, 1.0, 0.0).astype(BF16)
        for i in range(count):
            for j in range(split):
                b = i * split + j
                payload = ins[i][j]
                flags[...] = payload[:, model:].astype(F32).T
                picked = jnp.concatenate(
                    [flags[pl.ds(at_ref[2] + k, 1), :] for k in range(per)], axis=0
                )
                rank = mm(picked.astype(BF16), before)
                slot = jnp.where(picked > 0.0, rank, -1.0)
                ranks[b] = slot
                for k in range(per):
                    out[k, b * cap : (b + 1) * cap, :] = mm(
                        pick(slot[k : k + 1], cap), payload[:, :model]
                    ).astype(BF16)

    shapes = [
        jax.ShapeDtypeStruct((per, blocks_total * cap, model), BF16),
        jax.ShapeDtypeStruct((blocks_total, per, tokens), F32),
    ]
    return pl.pallas_call(
        kernel,
        grid=(1,),
        in_specs=[SMEM_SPEC]
        + [full_spec(arrays[0].shape)] * count
        + ([] if first else [ANY_SPEC] * 2),
        out_specs=[
            pl.BlockSpec((per, blocks * cap, model), lambda *_: (0, place, 0)),
            pl.BlockSpec((blocks, per, tokens), lambda *_: (place, 0, 0)),
        ],
        out_shape=shapes,
        scratch_shapes=[pltpu.VMEM((LANES, tokens), F32)],
        input_output_aliases={} if first else {1 + count: 0, 2 + count: 1},
        cost_estimate=cost(1e9, 6e6),
        name="dispatch_grads",
    )(at, *arrays, *([] if first else buffers))


def dispatch_rows(arrays, ranks, at, per, cap, model, experts, buffers, place, blocks_total):
    count = len(arrays)
    split, tokens, width = arrays[0].shape
    blocks = count * split
    first = buffers is None

    def kernel(at_ref, rank_ref, *refs):
        ins = refs[:count]
        out, weights = refs[-2], refs[-1]
        lane = lax.broadcasted_iota(jnp.int32, (cap, LANES), 1)
        for i in range(count):
            for j in range(split):
                b = i * split + j
                payload = ins[i][j]
                for k in range(per):
                    got = mm(pick(rank_ref[b, k : k + 1, :], cap), payload)
                    out[k, b * cap : (b + 1) * cap, :] = got[:, :model].astype(BF16)
                    tail = got[:, model:]
                    e = at_ref[2] + k
                    mine = (lane == e) | (lane == e + experts)
                    total = jnp.sum(jnp.where(mine, tail, 0.0), axis=1, keepdims=True)
                    weights[k, b * cap : (b + 1) * cap, :] = jnp.broadcast_to(total, (cap, LANES))

    shapes = [
        jax.ShapeDtypeStruct((per, blocks_total * cap, model), BF16),
        jax.ShapeDtypeStruct((per, blocks_total * cap, LANES), F32),
    ]
    return pl.pallas_call(
        kernel,
        grid=(1,),
        in_specs=[SMEM_SPEC, pl.BlockSpec((blocks, per, tokens), lambda *_: (place, 0, 0))]
        + [full_spec(arrays[0].shape)] * count
        + ([] if first else [ANY_SPEC] * 2),
        out_specs=[
            pl.BlockSpec((per, blocks * cap, model), lambda *_: (0, place, 0)),
            pl.BlockSpec((per, blocks * cap, LANES), lambda *_: (0, place, 0)),
        ],
        out_shape=shapes,
        input_output_aliases={} if first else {2 + count: 0, 3 + count: 1},
        cost_estimate=cost(1e9, 6e6),
        name="dispatch_rows",
    )(at, ranks, *arrays, *([] if first else buffers))


def run_expert(k, at, rows_in, grads_in, weights, gate, up, down, experts, tile, groups, cut):
    per, total, model = rows_in.shape
    ff = gate.shape[1]
    part = model // groups
    steps = total // tile

    def kernel(at_ref, x_ref, d_ref, w_ref, gate_ref, up_ref, down_ref, o_ref, r_ref, *refs):
        outs, (acc_gate, acc_up, acc_down) = refs[:-3], refs[-3:]
        step = pl.program_id(0)
        x, d = x_ref[0], d_ref[0]
        w = w_ref[0, :, 0:1]
        gate_pre = mm(x, gate_ref[...])
        up_pre = mm(x, up_ref[...])
        sig = 1.0 / (1.0 + jnp.exp(-gate_pre))
        silu = gate_pre * sig
        active_wide = silu * up_pre
        active = active_wide.astype(BF16)
        out = mm(active, down_ref[...])
        o_ref[...] = (out * w).astype(BF16)
        d_raw = mm(d, down_ref[...], NT)
        d_gates = jnp.sum(active.astype(F32) * d_raw, axis=1, keepdims=True)
        d_active = d_raw * w
        d_up = (d_active * silu).astype(BF16)
        d_gate = (d_active * up_pre * sig * (1.0 + gate_pre * (1.0 - sig))).astype(BF16)
        d_row = mm(d_gate, gate_ref[...], NT) + mm(d_up, up_ref[...], NT)
        r_ref[:, :model] = d_row.astype(BF16)
        high = d_gates.astype(BF16).astype(F32)
        lane = lax.broadcasted_iota(jnp.int32, (tile, LANES), 1)
        e = at_ref[2] + k
        r_ref[:, model:] = (
            jnp.where(lane == e, high, 0.0) + jnp.where(lane == e + experts, d_gates - high, 0.0)
        ).astype(BF16)
        new_gate = mm(x, d_gate, TN)
        new_up = mm(x, d_up, TN)
        new_down = mm((active_wide * w).astype(BF16), d, TN)

        @pl.when(step == 0)
        def _():
            acc_gate[...] = new_gate
            acc_up[...] = new_up
            acc_down[...] = new_down

        @pl.when(step > 0)
        def _():
            acc_gate[...] += new_gate
            acc_up[...] += new_up
            acc_down[...] += new_down

        @pl.when(step == steps - 1)
        def _():
            if cut:
                for s in range(groups):
                    z = lax.rem(at_ref[0] + s, groups)
                    at_z = pl.ds(pl.multiple_of(z * part, 128), part)
                    outs[s][...] = acc_gate[at_z, :].astype(BF16)
                    outs[groups + s][...] = acc_up[at_z, :].astype(BF16)
                    outs[2 * groups + s][...] = acc_down[:, at_z].astype(BF16)
            else:
                outs[0][...] = acc_gate[...].astype(BF16)
                outs[1][...] = acc_up[...].astype(BF16)
                outs[2][...] = acc_down[...].astype(BF16)

    if cut:
        grads = [(part, ff)] * (2 * groups) + [(ff, part)] * groups
    else:
        grads = [(model, ff)] * 2 + [(ff, model)]
    row_spec = pl.BlockSpec((1, tile, model), lambda t: (k, t, 0))
    held = lambda shape: pl.BlockSpec(shape, lambda t: (0, 0), pipeline_mode=pl.Buffered(1))
    out = pl.pallas_call(
        kernel,
        grid=(steps,),
        in_specs=[
            SMEM_SPEC,
            row_spec,
            row_spec,
            pl.BlockSpec((1, tile, LANES), lambda t: (k, t, 0)),
            held((model, ff)),
            held((model, ff)),
            held((ff, model)),
        ],
        out_specs=[
            pl.BlockSpec((tile, model), lambda t: (t, 0)),
            pl.BlockSpec((tile, model + LANES), lambda t: (t, 0)),
        ]
        + [held(shape) for shape in grads],
        out_shape=[
            jax.ShapeDtypeStruct((total, model), BF16),
            jax.ShapeDtypeStruct((total, model + LANES), BF16),
        ]
        + [jax.ShapeDtypeStruct(shape, BF16) for shape in grads],
        scratch_shapes=[
            pltpu.VMEM((model, ff), F32),
            pltpu.VMEM((model, ff), F32),
            pltpu.VMEM((ff, model), F32),
        ],
        compiler_params=pltpu.CompilerParams(vmem_limit_bytes=62 * 1024 * 1024),
        cost_estimate=cost(18 * total * model * ff, 10 * total * model),
        name="run_expert",
    )(at, rows_in, grads_in, weights, gate, up, down)
    return out[0], out[1], out[2:]


def combine(rows, ranks, count, split, tokens, cap, place):
    per = len(rows)
    width = rows[0].shape[1]
    blocks = count * split

    def kernel(rank_ref, *refs):
        ins, outs = refs[:per], refs[per:]
        for i in range(count):
            for j in range(split):
                b = i * split + j
                total = None
                for k in range(per):
                    one = mm(
                        pick(rank_ref[b, k : k + 1, :], cap), ins[k][b * cap : (b + 1) * cap, :], TN
                    )
                    total = one if total is None else total + one
                outs[i][j] = total.astype(BF16)

    return pl.pallas_call(
        kernel,
        grid=(1,),
        in_specs=[pl.BlockSpec((blocks, per, tokens), lambda *_: (place, 0, 0))]
        + [pl.BlockSpec((blocks * cap, width), lambda *_: (place, 0))] * per,
        out_specs=[full_spec((split, tokens, width))] * count,
        out_shape=[jax.ShapeDtypeStruct((split, tokens, width), BF16)] * count,
        cost_estimate=cost(1e9, 6e6),
        name="combine",
    )(ranks, *rows)


def rope_tables(my_index, prompt_len):
    half = HEAD_SIZE // 2
    local = jnp.arange(2 * PR_DEV, dtype=jnp.int32)
    cont = my_index * PR_DEV + local - PR_DEV
    position = jnp.where(local < PR_DEV, my_index * PR_DEV + local, prompt_len + cont % CONT)
    frequency = 10000.0 ** (-jnp.arange(half, dtype=F32) * (2.0 / HEAD_SIZE))
    angle = position.astype(F32)[:, None] * frequency[None, :]
    return jnp.cos(angle), jnp.sin(angle)


def rotate(x, cosine, sine):
    half = HEAD_SIZE // 2
    column = lax.broadcasted_iota(jnp.int32, x.shape, 1)
    other = jnp.where(column % HEAD_SIZE < half, jnp.roll(x, -half, axis=1), jnp.roll(x, half, axis=1))
    return x * cosine + other * sine


def layer_general(
    tokens,
    cotangent,
    routes,
    norm_one,
    query_key_value_weight,
    out_weight,
    norm_two,
    router_weight,
    gate_weight,
    up_weight,
    down_weight,
):
    n = lax.axis_size("expert")
    groups = lax.axis_size("group")
    me = lax.axis_index("expert")
    z = lax.axis_index("group")
    micro, count, model = tokens.shape
    exp_here, part, ff = gate_weight.shape
    experts = router_weight.shape[1]
    split = 2 if exp_here % 2 == 0 and groups % 2 == 0 else 1
    per = exp_here // split
    query_width = QUERY_HEADS * HEAD_SIZE
    kv_width = KEY_VALUE_HEADS * HEAD_SIZE
    cap = max(2, 3 * TOPK * PR_DEV // experts)
    where = jnp.stack([z, me, me * exp_here + (z % split) * per]).astype(jnp.int32)
    rows_here = part // n if part % n == 0 else 0
    aligned = rows_here > 0 and rows_here % 16 == 0 and part % LANES == 0

    misc = jnp.concatenate(
        [
            norm_one[:, None],
            norm_two[:, None],
            jnp.zeros((part, experts - 2), BF16),
            router_weight,
            jnp.zeros((part, LANES - 2 * experts), BF16),
        ],
        axis=1,
    )
    if aligned:
        first = jnp.concatenate([query_key_value_weight, misc], axis=1)
        cut = lambda x: lax.dynamic_slice_in_dim(x, me * rows_here, rows_here, axis=0)
        width = first.shape[1]
        middle = width // 2 // LANES * LANES
        first_full, far = gather_dense(cut(first), [(0, middle), (middle, width)], where)
        out_full, far_out = gather_dense(
            cut(out_weight), [(0, model // 2), (model // 2, model)], where
        )
        after = (far, far_out)
    else:
        first_full = lax.all_gather(
            jnp.concatenate([query_key_value_weight, misc], axis=1), "group", axis=0, tiled=True
        )
        out_full = lax.all_gather(out_weight, "group", axis=0, tiled=True)
        after = ()
    qkv_columns = query_key_value_weight.shape[1]
    qkv_full = first_full[:, :qkv_columns]
    misc_full = first_full[:, qkv_columns:]
    gain_one = misc_full[:, 0].astype(F32)
    gain_two = misc_full[:, 1].astype(F32)
    router_full = misc_full[:, experts : 2 * experts]

    weights_held = []
    gate_from, up_from, down_from = gate_weight, up_weight, down_weight
    if aligned:
        (gate_from, up_from, down_from), after = lax.optimization_barrier(
            ((gate_weight, up_weight, down_weight), after)
        )
    for k in range(per):
        held = []
        for array, axis in ((gate_from, 0), (up_from, 0), (down_from, 1)):
            if not aligned:
                held.append(lax.all_gather(array[k], "group", axis=axis, tiled=True))
                continue
            pieces = []
            for s in range(groups):
                index = ((z + s) % split) * per + k
                chunk = lax.dynamic_index_in_dim(array, index, 0, keepdims=False)
                pieces.append(shift(chunk, s) if s else chunk)

            def place(i, at_z, at_e, axis=axis):
                start = lax.rem(at_z - i + groups, groups) * part
                return (start, 0) if axis == 0 else (0, start)

            shape = (model, ff) if axis == 0 else (ff, model)
            held.append(assemble(pieces, place, shape, where))
        weights_held.append(held)

    expert_ids = jnp.arange(experts, dtype=jnp.int32)
    named = jnp.any(routes[..., None] == expert_ids, axis=2)
    pad = jnp.zeros((micro, count, LANES - experts), BF16)
    d_payload = jnp.concatenate([cotangent, named.astype(BF16), pad], axis=2)

    def to_experts(payload):
        held = []
        for m in range(micro):
            own = payload[m]
            both = jnp.stack([own] + [turn(own, j, split) for j in range(1, split)])
            held.append(spread(both, m % 2))
        return held

    def to_owners(parts):
        held = []
        for m in range(micro):
            total = collect(parts[m], m % 2)
            mine = total[0]
            for j in range(1, split):
                mine = mine + turn(total[j].astype(BF16), split - j, split).astype(F32)
            held.append(mine)
        return jnp.stack(held)

    slots_per = 2 if n % 2 == 0 else 1
    batches = [list(range(g * slots_per, (g + 1) * slots_per)) for g in range(n // slots_per)]
    blocks_total = n * micro * split

    d_slots = to_experts(d_payload)
    buffers = None
    for g, batch in enumerate(batches):
        buffers = dispatch_grads(
            [d_slots[m][r] for r in batch for m in range(micro)],
            where, per, cap, model, buffers, g, blocks_total,
        )
    grads_in, ranks = buffers

    rows = micro * count
    x = tokens.reshape(rows, model).astype(F32)
    inverse_one = lax.rsqrt(jnp.mean(x * x, axis=-1, keepdims=True) + 1e-05)
    normed = (x * inverse_one * gain_one).astype(BF16)
    cosine, sine = rope_tables(me, PR_DEV * n)
    heads_rope = QUERY_HEADS + KEY_VALUE_HEADS
    cosine = jnp.tile(jnp.concatenate([cosine, cosine], axis=1), (micro, heads_rope))
    sine = jnp.tile(jnp.concatenate([-sine, sine], axis=1), (micro, heads_rope))
    cosine, sine = lax.optimization_barrier((cosine, sine))
    project = mm(normed, qkv_full)
    roped = rotate(project[:, : query_width + kv_width], cosine, sine).astype(BF16)
    query = roped[:, :query_width]
    key_value = jnp.concatenate(
        [roped[:, query_width:], project[:, query_width + kv_width :].astype(BF16)], axis=1
    ).reshape(micro, count, 2 * kv_width)
    query = query.reshape(micro, count, query_width)
    kv_slots = [spread(key_value[m], m % 2) for m in range(micro)]
    mixed = jnp.concatenate(
        [attention_forward(query[m], kv_slots[m], where) for m in range(micro)], axis=0
    )
    hidden = x + mm(mixed, out_full)
    inverse_two = lax.rsqrt(jnp.mean(hidden * hidden, axis=-1, keepdims=True) + 1e-05)
    normed_two = (hidden * inverse_two * gain_two).astype(BF16)
    logits = mm(normed_two, router_full)
    chosen = named.reshape(rows, experts)
    logits = jnp.where(chosen, logits, NEG_FILL)
    top = jnp.max(logits, axis=-1, keepdims=True)
    raised = jnp.where(chosen, jnp.exp(logits - top), 0.0)
    gate_probs = raised / jnp.sum(raised, axis=-1, keepdims=True)

    high = gate_probs.astype(BF16)
    low = (gate_probs - high.astype(F32)).astype(BF16)
    payload = jnp.concatenate(
        [normed_two, high, low, jnp.zeros((rows, LANES - 2 * experts), BF16)], axis=1
    ).reshape(micro, count, model + LANES)
    x_slots = to_experts(payload)
    buffers = None
    for g, batch in enumerate(batches):
        buffers = dispatch_rows(
            [x_slots[m][r] for r in batch for m in range(micro)],
            ranks, where, per, cap, model, experts, buffers, g, blocks_total,
        )
    rows_in, row_weights = buffers
    tile = slots_per * micro * split * cap
    outs, backs, weight_terms = [], [], []
    for k in range(per):
        out_rows, back_rows, terms = run_expert(
            k, where, rows_in, grads_in, row_weights, *weights_held[k], experts, tile, groups, aligned
        )
        outs.append(out_rows)
        backs.append(back_rows)
        weight_terms.append(terms)

    def returned(row_arrays):
        parts = [[None] * n for _ in range(micro)]
        for g in reversed(range(len(batches))):
            got = combine(
                row_arrays, ranks, len(batches[g]) * micro, split, count, cap, g
            )
            for i, (r, m) in enumerate((r, m) for r in batches[g] for m in range(micro)):
                parts[m][r] = got[i]
        return to_owners(parts)

    back = returned(backs).reshape(rows, model + LANES)
    mixture = returned(outs).reshape(rows, model)
    block_out = (hidden + mixture).astype(BF16).reshape(tokens.shape)

    expert_grads = []
    for which in range(3):
        per_class = []
        for k in range(per):
            if not aligned:
                axis = 1 if which == 2 else 0
                per_class.append(
                    [lax.psum_scatter(weight_terms[k][which], "group", scatter_dimension=axis, tiled=True).astype(F32)]
                )
                continue
            sums = [None] * split
            for s in range(groups):
                term = weight_terms[k][which * groups + s]
                term = (shift(term, s) if s else term).astype(F32)
                c = s % split
                sums[c] = term if sums[c] is None else sums[c] + term
            per_class.append(
                [lax.select_n((z - p) % split, *sums) if split > 1 else sums[0] for p in range(split)]
            )
        expert_grads.append(
            jnp.stack([per_class[k][p] for p in range(split) for k in range(per)])
        )

    d_out = cotangent.reshape(rows, model).astype(F32)
    d_gates = back[:, model : model + experts] + back[:, model + experts : model + 2 * experts]
    d_logits = gate_probs * (d_gates - jnp.sum(gate_probs * d_gates, axis=-1, keepdims=True))
    router_grad = lax.dot_general(normed_two.astype(F32), d_logits, TN, precision=HIGHEST)
    d_normed_two = back[:, :model] + lax.dot_general(
        d_logits, router_full.astype(F32), NT, precision=HIGHEST
    )

    def rms_back(inputs, inverse, gain, upstream):
        scaled = gain * upstream
        return inverse * scaled - inputs * inverse * inverse * inverse * jnp.mean(
            scaled * inputs, axis=-1, keepdims=True
        )

    grad_two = jnp.sum(d_normed_two * hidden * inverse_two, axis=0)
    d_hidden = d_out + rms_back(hidden, inverse_two, gain_two, d_normed_two)
    d_attn = d_hidden.astype(BF16)
    d_mixed = mm(d_attn, out_full, NT).astype(BF16).reshape(micro, count, query_width)
    d_query, kv_terms = [], []
    for m in range(micro):
        got, terms = attention_backward(query[m], kv_slots[m], d_mixed[m], where)
        d_query.append(got)
        kv_terms.append(terms)
    d_query = jnp.concatenate(d_query, axis=0)
    q_cos, q_sin = cosine[:, :query_width], sine[:, :query_width]
    d_query_low = rotate(d_query, q_cos, -q_sin).astype(BF16)
    d_kv = jnp.concatenate([collect(kv_terms[m], m % 2) for m in range(micro)], axis=0)
    d_key_low = rotate(d_kv[:, :kv_width], q_cos[:, :kv_width], -q_sin[:, :kv_width]).astype(BF16)
    d_kv_low = jnp.concatenate([d_key_low, d_kv[:, kv_width:].astype(BF16)], axis=1)
    d_normed = mm(d_query_low, qkv_full[:, :query_width], NT) + mm(
        d_kv_low, qkv_full[:, query_width:], NT
    )
    grad_one = jnp.sum(d_normed * x * inverse_one, axis=0)
    input_grad = (d_hidden + rms_back(x, inverse_one, gain_one, d_normed)).reshape(tokens.shape)
    misc_grad = jnp.concatenate(
        [
            grad_one[:, None],
            grad_two[:, None],
            jnp.zeros((model, experts - 2), F32),
            router_grad,
            jnp.zeros((model, LANES - 2 * experts), F32),
        ],
        axis=1,
    )
    if aligned:
        grad_out = reduce_dense(sliced_outer(mixed, d_attn, None, groups, n, where), 0, where)
        grad_q = reduce_dense(sliced_outer(normed, d_query_low, None, groups, n, where), 1, where)
        grad_rest = reduce_dense(
            sliced_outer(normed, d_kv_low, misc_grad, groups, n, where), 0, where
        )
    else:

        def whole(value):
            low = lax.psum_scatter(value.astype(BF16), "group", scatter_dimension=0, tiled=True)
            return lax.psum(low, "expert").astype(F32)

        grad_out = whole(mm(mixed, d_attn, TN))
        grad_q = whole(mm(normed, d_query_low, TN))
        grad_rest = whole(jnp.concatenate([mm(normed, d_kv_low, TN), misc_grad], axis=1))
    grad_qkv = jnp.concatenate([grad_q, grad_rest[:, : 2 * kv_width]], axis=1)
    misc_sum = grad_rest[:, 2 * kv_width :]
    return (
        block_out,
        input_grad,
        misc_sum[:, 0],
        grad_qkv,
        grad_out,
        misc_sum[:, 1],
        misc_sum[:, experts : 2 * experts],
        *expert_grads,
    )


def flip(e, r):
    for bit in (1, 2, 4):
        if r & bit:
            e = e + bit - 2 * bit * lax.rem(e // bit, 2)
    return e


def partner(z):
    return z + 1 - 2 * lax.rem(z, 2)


def remote(src, dst, send, recv, device):
    return pltpu.make_async_remote_copy(
        src_ref=src,
        dst_ref=dst,
        send_sem=send,
        recv_sem=recv,
        device_id=device,
        device_id_type=pl.DeviceIdType.MESH,
    )


def greet(devices):
    barrier = pltpu.get_barrier_semaphore()
    for device in devices:
        pl.semaphore_signal(barrier, inc=1, device_id=device, device_id_type=pl.DeviceIdType.MESH)
    pl.semaphore_wait(barrier, len(devices))


def plane_devices(e):
    return [{"expert": flip(e, bit)} for bit in (1, 2, 4)]


class Gather:
    def __init__(self, e, own, loc, paths, send, recv):
        self.e, self.own, self.loc, self.paths, self.send, self.recv = e, own, loc, paths, send, recv

    def copy(self, r, bit, c):
        q = r ^ bit
        src = self.own(c) if r == 0 else self.loc(r, r, c)
        return remote(
            src, self.loc(r, q, c), self.send.at[q, c], self.recv.at[q, c],
            {"expert": flip(self.e, bit)},
        )

    def begin(self, c):
        for bit in (2, 4, 1):
            self.copy(0, bit, c).start()

    def arrived(self, q, c):
        here = self.loc(q, q, c)
        remote(
            here, here, self.send.at[q, c], self.recv.at[q, c], {"expert": flip(self.e, 1)}
        ).wait_recv()

    def pass_on(self, q, c):
        if q == 2 and self.paths[c] == 0:
            self.copy(2, 4, c).start()
        if q == 4 and self.paths[c] == 1:
            self.copy(4, 2, c).start()
        if q in (2, 4, 6):
            self.copy(q, 1, c).start()

    def finish(self, c):
        for bit in (2, 4, 1):
            self.copy(0, bit, c).wait_send()
        if self.paths[c] == 0:
            self.copy(2, 4, c).wait_send()
        else:
            self.copy(4, 2, c).wait_send()
        for q in (2, 4, 6):
            self.copy(q, 1, c).wait_send()

    def forward_all(self, chunks, use=None):
        for c in chunks:
            for q in (2, 4):
                self.arrived(q, c)
                self.pass_on(q, c)
        if use:
            for c in chunks:
                self.arrived(1, c)
                use(1, c)
                use(2, c)
                use(4, c)
        for c in chunks:
            self.arrived(6, c)
            self.pass_on(6, c)
            if use:
                use(6, c)
        for c in chunks:
            for q in (3, 5, 7) if use else (1, 3, 5, 7):
                self.arrived(q, c)
                if use:
                    use(q, c)


def add_rows(dst, sources, step=16):
    rows = sources[0].shape[0]

    def one(i, carry):
        at = pl.ds(pl.multiple_of(i * step, step), step)
        total = sources[0][at, :].astype(F32)
        for source in sources[1:]:
            total = total + source[at, :].astype(F32)
        dst[at, :] = total.astype(dst.dtype)
        return carry

    lax.fori_loop(0, rows // step, one, 0)


class Reduce:
    def __init__(self, e, part, paths, core, diag, near, acc, send, recv):
        self.e, self.part, self.paths = e, part, paths
        self.core, self.diag, self.near, self.acc = core, diag, near, acc
        self.send, self.recv = send, recv

    def core_copy(self, h, c):
        return remote(
            self.part(2 * h + 1, c), self.core.at[h, c], self.send.at[h, c], self.recv.at[h, c],
            {"expert": flip(self.e, 1)},
        )

    def diag_copy(self, c):
        return remote(
            self.acc.at[2, c], self.diag.at[c], self.send.at[4, c], self.recv.at[4, c],
            {"expert": flip(self.e, 4 if self.paths[c] == 0 else 2)},
        )

    def near_copy(self, i, c):
        return remote(
            self.acc.at[i, c], self.near.at[i, c], self.send.at[5 + i, c], self.recv.at[5 + i, c],
            {"expert": flip(self.e, 2 if i == 0 else 4)},
        )

    def begin(self, r, c):
        self.core_copy(r // 2, c).start()

    def diagonal(self, chunks):
        for c in chunks:
            self.core_copy(3, c).wait_recv()
            add_rows(self.acc.at[2, c], [self.part(6, c), self.core.at[3, c]])
            self.diag_copy(c).start()

    def sides(self, chunks):
        for c in chunks:
            for i in (0, 1) if self.paths[c] == 1 else (1, 0):
                self.core_copy(1 + i, c).wait_recv()
                terms = [self.part(2 + 2 * i, c), self.core.at[1 + i, c]]
                if self.paths[c] == i:
                    self.diag_copy(c).wait_recv()
                    terms.append(self.diag.at[c])
                add_rows(self.acc.at[i, c], terms)
                self.near_copy(i, c).start()

    def total(self, c):
        self.core_copy(0, c).wait_recv()
        self.near_copy(0, c).wait_recv()
        self.near_copy(1, c).wait_recv()
        return [self.part(0, c), self.core.at[0, c], self.near.at[0, c], self.near.at[1, c]]

    def finish(self, c):
        for h in range(4):
            self.core_copy(h, c).wait_send()
        self.diag_copy(c).wait_send()
        for i in range(2):
            self.near_copy(i, c).wait_send()


def reduce_scratch(count, rows, width):
    return [
        pltpu.VMEM((4, count, rows, width), BF16),
        pltpu.VMEM((count, rows, width), BF16),
        pltpu.VMEM((2, count, rows, width), BF16),
        pltpu.VMEM((3, count, rows, width), BF16),
        pltpu.SemaphoreType.DMA((7, count)),
        pltpu.SemaphoreType.DMA((7, count)),
    ]


def params(identity, vmem=62):
    return pltpu.CompilerParams(
        collective_id=identity, has_side_effects=True, vmem_limit_bytes=vmem * 1024 * 1024
    )


def plane_weights(sets):
    groups, n = len(sets[0]), 8
    rows = sets[0][0].shape[0]
    kinds = len(sets)
    count = groups * kinds

    def kernel(*refs):
        ins, outs = refs[:count], refs[count : count + kinds]
        send, recv, local = refs[count + kinds :]
        e, z = lax.axis_index("expert"), lax.axis_index("group")

        def loc(r, q, c):
            s, kind = c // kinds, c % kinds
            row = (lax.rem(z - s + groups, groups) * n + flip(e, r)) * rows
            return outs[kind].at[pl.ds(pl.multiple_of(row, 16), rows), :]

        gather = Gather(e, lambda c: ins[c], loc, [c // kinds % 2 for c in range(count)], send, recv)
        greet(plane_devices(e))
        for c in range(count):
            gather.begin(c)
            pltpu.make_async_copy(ins[c], loc(0, 0, c), local.at[c]).start()
        gather.forward_all(range(count))
        for c in range(count):
            gather.finish(c)
            pltpu.make_async_copy(ins[c], loc(0, 0, c), local.at[c]).wait()

    flat = [sets[kind][s] for s in range(groups) for kind in range(kinds)]
    shapes = [(groups * n * rows, one[0].shape[1]) for one in sets]
    return pl.pallas_call(
        kernel,
        in_specs=[pl.BlockSpec(memory_space=pltpu.VMEM)] * count,
        out_specs=[pl.BlockSpec(memory_space=pltpu.VMEM)] * kinds,
        out_shape=[jax.ShapeDtypeStruct(shape, BF16) for shape in shapes],
        scratch_shapes=[
            pltpu.SemaphoreType.DMA((n, count)),
            pltpu.SemaphoreType.DMA((n, count)),
            pltpu.SemaphoreType.DMA((count,)),
        ],
        compiler_params=params(1),
        cost_estimate=cost(5e10, 6e7),
        name="plane_weights",
    )(*flat)


def attention_pairs(n, at_me, q_ref, keys, out_ref):
    width = KEY_VALUE_HEADS * HEAD_SIZE
    prompt_ok, cont_ok = attention_masks_plain(n, at_me)

    def pair(j, carry):
        q_at = pl.ds(pl.multiple_of(j * 384, 128), 384)
        k_at = pl.ds(pl.multiple_of(j * 128, 128), 128)
        v_at = pl.ds(pl.multiple_of(width + j * 128, 128), 128)
        q_top, q_low = q_ref[:PR_DEV, q_at], q_ref[PR_DEV:, q_at]
        k_two, v_two = keys[:, k_at], keys[:, v_at]
        tops, lows = [], []
        for g in range(2):
            key = k_two[:, g * HEAD_SIZE : (g + 1) * HEAD_SIZE]
            value = v_two[:, g * HEAD_SIZE : (g + 1) * HEAD_SIZE]
            top, low = group_probs(
                head_rows(q_top, g * 192), head_rows(q_low, g * 192), key, prompt_ok, cont_ok, n
            )
            tops.append(row_heads(mm(top.astype(BF16), value[: n * PR_DEV])))
            lows.append(row_heads(mm(low.astype(BF16), value)))
        out_ref[:PR_DEV, q_at] = jnp.concatenate(tops, axis=1).astype(BF16)
        out_ref[PR_DEV:, q_at] = jnp.concatenate(lows, axis=1).astype(BF16)
        return carry

    lax.fori_loop(0, KEY_VALUE_HEADS // 2, pair, 0)


def flip_columns(slot, me, limit):
    bit, total = 1, jnp.zeros_like(slot)
    while bit < limit:
        total = total + bit * lax.rem(slot // bit + me // bit, 2)
        bit *= 2
    return total


def attention_masks_plain(n, me):
    shape = (3 * PR_DEV, n * PR_DEV)
    token = lax.rem(lax.broadcasted_iota(jnp.int32, shape, 0), PR_DEV)
    column = lax.broadcasted_iota(jnp.int32, shape, 1)
    owner = flip_columns(column // PR_DEV, me, n)
    prompt_ok = owner * PR_DEV + lax.rem(column, PR_DEV) <= me * PR_DEV + token
    slots = CONT // PR_DEV
    shape = (3 * PR_DEV, CONT)
    token = lax.rem(lax.broadcasted_iota(jnp.int32, shape, 0), PR_DEV)
    column = lax.broadcasted_iota(jnp.int32, shape, 1)
    local = lax.rem(me, slots)
    owner = flip_columns(column // PR_DEV, local, slots)
    cont_ok = owner * PR_DEV + lax.rem(column, PR_DEV) <= local * PR_DEV + token
    return prompt_ok, cont_ok


def plane_attention(query, key_value):
    micro, tokens, width = key_value.shape
    n = 8

    def kernel(q_ref, kv_ref, out_ref, slots, keys, send, recv, local):
        e = lax.axis_index("expert")
        gather = Gather(
            e, lambda c: kv_ref.at[c], lambda r, q, c: slots.at[q, c], [c % 2 for c in range(micro)],
            send, recv,
        )
        greet(plane_devices(e))
        for c in range(micro):
            gather.begin(c)
            pltpu.make_async_copy(kv_ref.at[c], slots.at[0, c], local.at[c]).start()
        gather.forward_all(range(micro))
        for c in range(micro):
            pltpu.make_async_copy(kv_ref.at[c], slots.at[0, c], local.at[c]).wait()
            load_keys(n, [slots.at[r, c] for r in range(n)], keys)
            attention_pairs(n, e, q_ref.at[c], keys, out_ref.at[c])
        for c in range(micro):
            gather.finish(c)

    vmem = pl.BlockSpec(memory_space=pltpu.VMEM)
    return pl.pallas_call(
        kernel,
        in_specs=[vmem, vmem],
        out_specs=[vmem, vmem],
        out_shape=[
            jax.ShapeDtypeStruct(query.shape, BF16),
            jax.ShapeDtypeStruct((n, micro, tokens, width), BF16),
        ],
        scratch_shapes=[
            pltpu.VMEM((n * PR_DEV + CONT, width), BF16),
            pltpu.SemaphoreType.DMA((n, micro)),
            pltpu.SemaphoreType.DMA((n, micro)),
            pltpu.SemaphoreType.DMA((micro,)),
        ],
        compiler_params=params(2),
        cost_estimate=cost(3e10, 2e7),
        name="plane_attention",
    )(query, key_value)


def plane_attention_backward(query, slots, d_mixed):
    n, micro, tokens, width = slots.shape
    half = width // 2
    pr = n * PR_DEV
    total = pr + CONT

    def kernel(q_ref, d_ref, kv_ref, dq_ref, dkv_ref, keys, grads, parts, *scratch):
        e = lax.axis_index("expert")
        red = Reduce(e, lambda r, c: parts.at[r, c], [c % 2 for c in range(micro)], *scratch)
        greet(plane_devices(e))
        prompt_ok, cont_ok = attention_masks_plain(n, e)

        def one_side(prob, d_rows, key, value, q_rows):
            d_prob = mm(d_rows, value, NT)
            delta = jnp.sum(prob * d_prob, axis=1, keepdims=True)
            d_score = (prob * (d_prob - delta)).astype(BF16)
            return (
                mm(d_score, key) * SCORE_SCALE,
                mm(d_score, q_rows, TN) * SCORE_SCALE,
                mm(prob.astype(BF16), d_rows, TN),
            )

        for c in range(micro):
            load_keys(n, [kv_ref.at[r, c] for r in range(n)], keys)

            def pair(j, carry):
                q_at = pl.ds(pl.multiple_of(j * 384, 128), 384)
                k_at = pl.ds(pl.multiple_of(j * 128, 128), 128)
                v_at = pl.ds(pl.multiple_of(half + j * 128, 128), 128)
                q_top, q_low = q_ref[c, :PR_DEV, q_at], q_ref[c, PR_DEV:, q_at]
                d_top, d_low = d_ref[c, :PR_DEV, q_at], d_ref[c, PR_DEV:, q_at]
                k_two, v_two = keys[:, k_at], keys[:, v_at]
                dq_tops, dq_lows, dks, dvs = [], [], [], []
                for g in range(2):
                    key = k_two[:, g * HEAD_SIZE : (g + 1) * HEAD_SIZE]
                    value = v_two[:, g * HEAD_SIZE : (g + 1) * HEAD_SIZE]
                    rows_top, rows_low = head_rows(q_top, g * 192), head_rows(q_low, g * 192)
                    top, low = group_probs(rows_top, rows_low, key, prompt_ok, cont_ok, n)
                    dq_top, dk_top, dv_top = one_side(
                        top, head_rows(d_top, g * 192), key[:pr], value[:pr], rows_top
                    )
                    dq_low, dk_low, dv_low = one_side(
                        low, head_rows(d_low, g * 192), key, value, rows_low
                    )
                    dq_tops.append(row_heads(dq_top))
                    dq_lows.append(row_heads(dq_low))
                    dks.append(jnp.concatenate([dk_low[:pr] + dk_top, dk_low[pr:]], axis=0))
                    dvs.append(jnp.concatenate([dv_low[:pr] + dv_top, dv_low[pr:]], axis=0))
                dq_ref[c, :PR_DEV, q_at] = jnp.concatenate(dq_tops, axis=1)
                dq_ref[c, PR_DEV:, q_at] = jnp.concatenate(dq_lows, axis=1)
                grads[:, k_at] = jnp.concatenate(dks, axis=1).astype(BF16)
                grads[:, v_at] = jnp.concatenate(dvs, axis=1).astype(BF16)
                return carry

            lax.fori_loop(0, KEY_VALUE_HEADS // 2, pair, 0)
            for r in (7, 5, 3, 1, 6, 2, 4, 0):
                parts[r, c, :PR_DEV, :] = grads[r * PR_DEV : (r + 1) * PR_DEV, :]
                if r < CONT // PR_DEV:
                    lo = (n + r) * PR_DEV
                    parts[r, c, PR_DEV:, :] = grads[lo : lo + PR_DEV, :]
                else:
                    parts[r, c, PR_DEV:, :] = jnp.zeros((PR_DEV, width), BF16)
                if r % 2:
                    red.begin(r, c)
        red.diagonal(range(micro))
        red.sides(range(micro))
        for c in range(micro):
            add_rows(dkv_ref.at[c], red.total(c))
        for c in range(micro):
            red.finish(c)

    vmem = pl.BlockSpec(memory_space=pltpu.VMEM)
    return pl.pallas_call(
        kernel,
        in_specs=[vmem] * 3,
        out_specs=[vmem] * 2,
        out_shape=[
            jax.ShapeDtypeStruct(query.shape, F32),
            jax.ShapeDtypeStruct((micro, tokens, width), F32),
        ],
        scratch_shapes=[
            pltpu.VMEM((total, width), BF16),
            pltpu.VMEM((total, width), BF16),
            pltpu.VMEM((n, micro, tokens, width), BF16),
        ]
        + reduce_scratch(micro, tokens, width),
        compiler_params=params(3),
        cost_estimate=cost(5e10, 2e7),
        name="plane_attention_backward",
    )(query, d_mixed, slots)


def plane_dispatch(payload, ranks, where, per, cap, model, experts):
    micro, tokens, width = payload.shape
    n, split = 8, 2
    count = split * micro

    def kernel(at_ref, own_ref, rank_ref, out, weights, slots, z_send, z_recv, send, recv):
        e, z = lax.axis_index("expert"), lax.axis_index("group")
        lane = lax.broadcasted_iota(jnp.int32, (cap, LANES), 1)

        def own(c):
            return own_ref.at[c] if c < micro else slots.at[0, c]

        gather = Gather(
            e, own, lambda r, q, c: slots.at[q, c], [c % 2 for c in range(count)], send, recv
        )

        def turned(m):
            return remote(
                own_ref.at[m], slots.at[0, micro + m], z_send.at[m], z_recv.at[m],
                {"group": partner(z)},
            )

        def use(r, c):
            rows = own(c)[...] if r == 0 else slots[r, c]
            b = r * count + c
            for k in range(per):
                got = mm(pick(rank_ref[b, k : k + 1, :], cap), rows)
                out[k, b * cap : (b + 1) * cap, :] = got[:, :model].astype(BF16)
                first = at_ref[2] + k
                mine = (lane == first) | (lane == first + experts)
                total = jnp.sum(jnp.where(mine, got[:, model:], 0.0), axis=1, keepdims=True)
                weights[k, b * cap : (b + 1) * cap, :] = jnp.broadcast_to(total, (cap, LANES))

        greet(plane_devices(e) + [{"group": partner(z)}])
        for m in range(micro):
            turned(m).start()
        for m in range(micro):
            gather.begin(m)
        for m in range(micro):
            use(0, m)
        for m in range(micro):
            turned(m).wait_recv()
            gather.begin(micro + m)
            use(0, micro + m)
        gather.forward_all(range(count), use)
        for m in range(micro):
            turned(m).wait_send()
        for c in range(count):
            gather.finish(c)

    vmem = pl.BlockSpec(memory_space=pltpu.VMEM)
    total = n * count * cap
    return pl.pallas_call(
        kernel,
        in_specs=[SMEM_SPEC, vmem, vmem],
        out_specs=[vmem, vmem],
        out_shape=[
            jax.ShapeDtypeStruct((per, total, model), BF16),
            jax.ShapeDtypeStruct((per, total, LANES), F32),
        ],
        scratch_shapes=[
            pltpu.VMEM((n, count, tokens, width), BF16),
            pltpu.SemaphoreType.DMA((micro,)),
            pltpu.SemaphoreType.DMA((micro,)),
            pltpu.SemaphoreType.DMA((n, count)),
            pltpu.SemaphoreType.DMA((n, count)),
        ],
        compiler_params=params(4),
        cost_estimate=cost(6e10, 4e7),
        name="plane_dispatch",
    )(where, payload, ranks)


def plane_return(rows, ranks, micro, tokens, cap):
    per = len(rows)
    width = rows[0].shape[1]
    n, split = 8, 2
    count = split * micro
    chunks = list(range(micro, count)) + list(range(micro))

    def kernel(rank_ref, *refs):
        ins, out, refs = refs[:per], refs[per], refs[per + 1 :]
        parts, z_out, z_in, z_send, z_recv, scratch = *refs[:5], refs[5:]
        e, z = lax.axis_index("expert"), lax.axis_index("group")
        red = Reduce(e, lambda r, c: parts.at[r, c], [c % 2 for c in range(count)], *scratch)

        def produce(r, c):
            b = r * count + c
            total = None
            for k in range(per):
                one = mm(
                    pick(rank_ref[b, k : k + 1, :], cap), ins[k][b * cap : (b + 1) * cap, :], TN
                )
                total = one if total is None else total + one
            parts[r, c] = total.astype(BF16)

        def turned(m):
            return remote(
                z_out.at[m], z_in.at[m], z_send.at[m], z_recv.at[m], {"group": partner(z)}
            )

        greet(plane_devices(e) + [{"group": partner(z)}])
        for r in (7, 3, 5):
            for c in chunks:
                produce(r, c)
                red.begin(r, c)
        for c in chunks:
            produce(6, c)
        red.diagonal(chunks)
        for r in (2, 4):
            for c in chunks:
                produce(r, c)
        red.sides(chunks)
        for c in chunks:
            produce(1, c)
            red.begin(1, c)
        for c in chunks:
            produce(0, c)
        for c in chunks:
            terms = red.total(c)
            if c >= micro:
                add_rows(z_out.at[c - micro], terms)
                turned(c - micro).start()
            else:
                turned(c).wait_recv()
                add_rows(out.at[c], terms + [z_in.at[c]])
        for m in range(micro):
            turned(m).wait_send()
        for c in chunks:
            red.finish(c)

    vmem = pl.BlockSpec(memory_space=pltpu.VMEM)
    return pl.pallas_call(
        kernel,
        in_specs=[vmem] * (1 + per),
        out_specs=vmem,
        out_shape=jax.ShapeDtypeStruct((micro, tokens, width), F32),
        scratch_shapes=[
            pltpu.VMEM((n, count, tokens, width), BF16),
            pltpu.VMEM((micro, tokens, width), BF16),
            pltpu.VMEM((micro, tokens, width), BF16),
            pltpu.SemaphoreType.DMA((micro,)),
            pltpu.SemaphoreType.DMA((micro,)),
        ]
        + reduce_scratch(count, tokens, width),
        compiler_params=params(5),
        cost_estimate=cost(6e10, 4e7),
        name="plane_return",
    )(ranks, *rows)


def plane_gradients(products, extra, groups):
    n = 8
    depth = products[0][0].shape[1]
    widths = [b.shape[1] for a, b in products]
    width = sum(widths) + extra.shape[1]
    rows = depth // (groups * n)
    tile = 512
    flat = [x for pair in products for x in pair]

    def kernel(*refs):
        ins, extra_ref, refs = refs[: len(flat)], refs[len(flat)], refs[len(flat) + 1 :]
        out, wide, parts, z_out, z_in, slots, z_send, z_recv, send, recv, local = refs[:11]
        scratch = refs[11:]
        e, z = lax.axis_index("expert"), lax.axis_index("group")
        red = Reduce(e, lambda r, c: parts.at[r, c], [c % 2 for c in range(groups)], *scratch)
        greet(
            plane_devices(e)
            + [{"group": lax.rem(z + s, groups)} for s in range(1, groups)]
        )

        def cut(lo, size):
            for r in range(n):
                for s in range(groups):
                    row = (lax.rem(z + s, groups) * n + flip(e, r)) * rows
                    at = pl.ds(pl.multiple_of(row, 16), rows)
                    parts[r, s, :, lo : lo + size] = wide[at, :size].astype(BF16)

        lo = 0
        for i, count in enumerate(widths):
            for start in range(0, count, tile):
                size = min(tile, count - start)
                wide[:, :size] = mm(ins[2 * i][...], ins[2 * i + 1][:, start : start + size], TN)
                cut(lo, size)
                lo += size
        wide[:, : extra_ref.shape[1]] = extra_ref[...]
        cut(lo, extra_ref.shape[1])

        chunks = list(range(1, groups)) + [0]
        for r in (7, 3, 5, 1):
            for c in chunks:
                red.begin(r, c)
        red.diagonal(chunks)
        red.sides(chunks)

        def far(s):
            return remote(
                z_out.at[s], z_in.at[s], z_send.at[s], z_recv.at[s],
                {"group": lax.rem(z + s, groups)},
            )

        for c in chunks:
            add_rows(z_out.at[c], red.total(c))
            if c:
                far(c).start()
        for c in range(1, groups):
            far(c).wait_recv()
        add_rows(slots.at[0], [z_out.at[0]] + [z_in.at[c] for c in range(1, groups)])

        middle = width // 2 // LANES * LANES
        spans = [(0, middle), (middle, width)]

        def loc(r, q, c):
            return slots.at[q, :, spans[c][0] : spans[c][1]]

        gather = Gather(e, lambda c: loc(0, 0, c), loc, [0, 1], send, recv)
        for c in range(2):
            gather.begin(c)
        gather.forward_all(range(2))
        for r in range(n):
            row = pl.multiple_of(flip(e, r) * rows, 16)
            out[pl.ds(row, rows), :] = slots[r].astype(F32)
        for c in range(2):
            gather.finish(c)
        for c in range(1, groups):
            far(c).wait_send()
        for c in chunks:
            red.finish(c)

    vmem = pl.BlockSpec(memory_space=pltpu.VMEM)
    return pl.pallas_call(
        kernel,
        in_specs=[vmem] * (len(flat) + 1),
        out_specs=vmem,
        out_shape=jax.ShapeDtypeStruct((n * rows, width), F32),
        scratch_shapes=[
            pltpu.VMEM((depth, tile), F32),
            pltpu.VMEM((n, groups, rows, width), BF16),
            pltpu.VMEM((groups, rows, width), BF16),
            pltpu.VMEM((groups, rows, width), BF16),
            pltpu.VMEM((n, rows, width), BF16),
            pltpu.SemaphoreType.DMA((groups,)),
            pltpu.SemaphoreType.DMA((groups,)),
            pltpu.SemaphoreType.DMA((n, 2)),
            pltpu.SemaphoreType.DMA((n, 2)),
            pltpu.SemaphoreType.DMA((2,)),
        ]
        + reduce_scratch(groups, rows, width),
        compiler_params=params(6),
        cost_estimate=cost(8e10, 4e7),
        name="plane_gradients",
    )(*flat, extra)


def gather_flags(slots, where, per, cap, model):
    n, count, tokens, width = slots.shape

    def kernel(at_ref, in_ref, out, ranks, flags):
        row = lax.broadcasted_iota(jnp.int32, (tokens, tokens), 0)
        col = lax.broadcasted_iota(jnp.int32, (tokens, tokens), 1)
        before = jnp.where(row < col, 1.0, 0.0).astype(BF16)
        for b in range(count):
            payload = in_ref[0, b]
            flags[...] = payload[:, model:].astype(F32).T
            picked = jnp.concatenate(
                [flags[pl.ds(at_ref[2] + k, 1), :] for k in range(per)], axis=0
            )
            slot = jnp.where(picked > 0.0, mm(picked.astype(BF16), before), -1.0)
            ranks[b] = slot
            for k in range(per):
                out[k, b * cap : (b + 1) * cap, :] = mm(
                    pick(slot[k : k + 1], cap), payload[:, :model]
                ).astype(BF16)

    return pl.pallas_call(
        kernel,
        grid_spec=pltpu.PrefetchScalarGridSpec(
            num_scalar_prefetch=1,
            grid=(n,),
            in_specs=[
                pl.BlockSpec(
                    (1, count, tokens, width),
                    lambda r, at: (jnp.bitwise_xor(at[1], r), 0, 0, 0),
                )
            ],
            out_specs=[
                pl.BlockSpec((per, count * cap, model), lambda r, at: (0, r, 0)),
                pl.BlockSpec((count, per, tokens), lambda r, at: (r, 0, 0)),
            ],
            scratch_shapes=[pltpu.VMEM((LANES, tokens), F32)],
        ),
        out_shape=[
            jax.ShapeDtypeStruct((per, n * count * cap, model), BF16),
            jax.ShapeDtypeStruct((n * count, per, tokens), F32),
        ],
        cost_estimate=cost(5e9, 3e7),
        name="gather_flags",
    )(where, slots)


def scatter_rows(rows, ranks, where, n, count, tokens, cap):
    per, width = len(rows), rows[0].shape[1]

    def kernel(at_ref, rank_ref, *refs):
        ins, out = refs[:per], refs[per]
        for b in range(count):
            total = None
            for k in range(per):
                one = mm(
                    pick(rank_ref[b, k : k + 1, :], cap), ins[k][b * cap : (b + 1) * cap, :], TN
                )
                total = one if total is None else total + one
            out[0, b] = total.astype(BF16)

    return pl.pallas_call(
        kernel,
        grid_spec=pltpu.PrefetchScalarGridSpec(
            num_scalar_prefetch=1,
            grid=(n,),
            in_specs=[pl.BlockSpec((count, per, tokens), lambda r, at: (r, 0, 0))]
            + [pl.BlockSpec((count * cap, width), lambda r, at: (r, 0))] * per,
            out_specs=pl.BlockSpec(
                (1, count, tokens, width), lambda r, at: (jnp.bitwise_xor(at[1], r), 0, 0, 0)
            ),
        ),
        out_shape=jax.ShapeDtypeStruct((n, count, tokens, width), BF16),
        cost_estimate=cost(5e9, 3e7),
        name="scatter_rows",
    )(where, ranks, *rows)


def expert_step(k, at, rows_in, grads_in, weights, own, far, experts, tile):
    per, total, model = rows_in.shape
    part, ff = own[0].shape[1:]
    groups = model // part
    steps = total // tile
    held_count = 3 + 2 * (groups - 1)

    def kernel(at_ref, x_ref, d_ref, w_ref, *refs):
        sources, refs = refs[:held_count], refs[held_count:]
        o_ref, r_ref, refs = refs[0], refs[1], refs[2:]
        outs, refs = refs[: 2 * groups], refs[2 * groups :]
        acc_gate, acc_up, acc_down, gate_ref, up_ref, down_ref, sems = refs
        step = pl.program_id(0)

        @pl.when(step == 0)
        def _():
            copies = []
            for s in range(groups):
                z = lax.rem(at_ref[0] - s + groups, groups)
                at_z = pl.ds(pl.multiple_of(z * part, 128), part)
                if s == 0:
                    mine = at_ref[3] + k
                    three = [sources[i].at[mine] for i in range(3)]
                else:
                    pair = sources[3 + 2 * (s - 1)]
                    three = [pair.at[0], pair.at[1], sources[4 + 2 * (s - 1)]]
                for i, dst in enumerate(
                    [gate_ref.at[at_z, :], up_ref.at[at_z, :], down_ref.at[:, at_z]]
                ):
                    copies.append(pltpu.make_async_copy(three[i], dst, sems.at[3 * s + i]))
            for one in copies:
                one.start()
            for one in copies:
                one.wait()

        x, d = x_ref[0], d_ref[0]
        w = w_ref[0, :, 0:1]
        gate_pre = mm(x, gate_ref[...])
        up_pre = mm(x, up_ref[...])
        sig = 1.0 / (1.0 + jnp.exp(-gate_pre))
        silu = gate_pre * sig
        active_wide = silu * up_pre
        active = active_wide.astype(BF16)
        o_ref[...] = (mm(active, down_ref[...]) * w).astype(BF16)
        d_raw = mm(d, down_ref[...], NT)
        d_gates = jnp.sum(active.astype(F32) * d_raw, axis=1, keepdims=True)
        d_active = d_raw * w
        d_up = (d_active * silu).astype(BF16)
        d_gate = (d_active * up_pre * sig * (1.0 + gate_pre * (1.0 - sig))).astype(BF16)
        d_row = mm(d_gate, gate_ref[...], NT) + mm(d_up, up_ref[...], NT)
        r_ref[:, :model] = d_row.astype(BF16)
        high = d_gates.astype(BF16).astype(F32)
        lane = lax.broadcasted_iota(jnp.int32, (tile, LANES), 1)
        e = at_ref[2] + k
        r_ref[:, model:] = (
            jnp.where(lane == e, high, 0.0) + jnp.where(lane == e + experts, d_gates - high, 0.0)
        ).astype(BF16)
        new_gate = mm(x, d_gate, TN)
        new_up = mm(x, d_up, TN)
        new_down = mm((active_wide * w).astype(BF16), d, TN)

        @pl.when(step == 0)
        def _():
            acc_gate[...] = new_gate
            acc_up[...] = new_up
            acc_down[...] = new_down

        @pl.when(step > 0)
        def _():
            acc_gate[...] += new_gate
            acc_up[...] += new_up
            acc_down[...] += new_down

        @pl.when(step == steps - 1)
        def _():
            for s in range(groups):
                z = lax.rem(at_ref[0] + s, groups)
                at_z = pl.ds(pl.multiple_of(z * part, 128), part)
                outs[2 * s][0] = acc_gate[at_z, :].astype(BF16)
                outs[2 * s][1] = acc_up[at_z, :].astype(BF16)
                outs[2 * s + 1][...] = acc_down[:, at_z].astype(BF16)

    def held(shape):
        return pl.BlockSpec(shape, lambda t: (0,) * len(shape), pipeline_mode=pl.Buffered(1))

    grads = [(2, part, ff), (ff, part)] * groups
    row_spec = pl.BlockSpec((1, tile, model), lambda t: (k, t, 0))
    out = pl.pallas_call(
        kernel,
        grid=(steps,),
        in_specs=[SMEM_SPEC, row_spec, row_spec, pl.BlockSpec((1, tile, LANES), lambda t: (k, t, 0))]
        + [ANY_SPEC] * held_count,
        out_specs=[
            pl.BlockSpec((tile, model), lambda t: (t, 0)),
            pl.BlockSpec((tile, model + LANES), lambda t: (t, 0)),
        ]
        + [held(shape) for shape in grads],
        out_shape=[
            jax.ShapeDtypeStruct((total, model), BF16),
            jax.ShapeDtypeStruct((total, model + LANES), BF16),
        ]
        + [jax.ShapeDtypeStruct(shape, BF16) for shape in grads],
        scratch_shapes=[
            pltpu.VMEM((model, ff), F32),
            pltpu.VMEM((model, ff), F32),
            pltpu.VMEM((ff, model), F32),
            pltpu.VMEM((model, ff), BF16),
            pltpu.VMEM((model, ff), BF16),
            pltpu.VMEM((ff, model), BF16),
            pltpu.SemaphoreType.DMA((3 * groups,)),
        ],
        compiler_params=pltpu.CompilerParams(vmem_limit_bytes=62 * 1024 * 1024),
        cost_estimate=cost(36 * total * model * ff, 10 * total * model),
        name="expert_step",
    )(at, rows_in, grads_in, weights, *own, *[x for pair in far for x in pair])
    return out[0], out[1], [(out[2 + 2 * s], out[3 + 2 * s]) for s in range(groups)]


def layer_plane(
    tokens,
    cotangent,
    routes,
    norm_one,
    query_key_value_weight,
    out_weight,
    norm_two,
    router_weight,
    gate_weight,
    up_weight,
    down_weight,
):
    n = lax.axis_size("expert")
    groups = lax.axis_size("group")
    me = lax.axis_index("expert")
    z = lax.axis_index("group")
    micro, count, model = tokens.shape
    exp_here, part, ff = gate_weight.shape
    experts = router_weight.shape[1]
    split = 2
    per = exp_here // split
    query_width = QUERY_HEADS * HEAD_SIZE
    kv_width = KEY_VALUE_HEADS * HEAD_SIZE
    cap = max(2, 3 * TOPK * PR_DEV // experts)
    where = jnp.stack([z, me, me * exp_here + (z % split) * per, (z % split) * per]).astype(jnp.int32)
    rows_here = part // n
    rows = micro * count

    misc = jnp.concatenate(
        [
            norm_one[:, None],
            norm_two[:, None],
            jnp.zeros((part, experts - 2), BF16),
            router_weight,
            jnp.zeros((part, LANES - 2 * experts), BF16),
        ],
        axis=1,
    )
    cut = lambda x: lax.dynamic_slice_in_dim(x, me * rows_here, rows_here, axis=0)
    shares = [cut(query_key_value_weight), jnp.concatenate([cut(out_weight), cut(misc)], axis=1)]
    sets = [[x] + [shift(x, s) for s in range(1, groups)] for x in shares]
    (gate_from, up_from, down_from), sets = lax.optimization_barrier(
        ((gate_weight, up_weight, down_weight), sets)
    )
    weights_far = []
    for k in range(per):
        far = []
        for s in range(1, groups):
            index = ((z + s) % split) * per + k
            take = lambda x: lax.dynamic_index_in_dim(x, index, 0, keepdims=False)
            far.append(
                (shift(jnp.stack([take(gate_from), take(up_from)]), s), shift(take(down_from), s))
            )
        weights_far.append(far)
    qkv_full, rest_full = plane_weights(sets)
    out_full, misc_full = rest_full[:, :model], rest_full[:, model:]
    gain_one = misc_full[:, 0].astype(F32)
    gain_two = misc_full[:, 1].astype(F32)
    router_full = misc_full[:, experts : 2 * experts]

    expert_ids = jnp.arange(experts, dtype=jnp.int32)
    named = jnp.any(routes[..., None] == expert_ids, axis=2)
    pad = jnp.zeros((micro, count, LANES - experts), BF16)
    d_payload = jnp.concatenate([cotangent, named.astype(BF16), pad], axis=2)
    both = jnp.concatenate([d_payload, turn(d_payload, 1, split)], axis=0)
    d_slots = lax.all_gather(both, "expert", axis=0)
    grads_in, ranks = gather_flags(d_slots, where, per, cap, model)

    x = tokens.reshape(rows, model).astype(F32)
    inverse_one = lax.rsqrt(jnp.mean(x * x, axis=-1, keepdims=True) + 1e-05)
    normed = (x * inverse_one * gain_one).astype(BF16)
    cosine, sine = rope_tables(me, PR_DEV * n)
    heads_rope = QUERY_HEADS + KEY_VALUE_HEADS
    cosine = jnp.tile(jnp.concatenate([cosine, cosine], axis=1), (micro, heads_rope))
    sine = jnp.tile(jnp.concatenate([-sine, sine], axis=1), (micro, heads_rope))
    cosine, sine = lax.optimization_barrier((cosine, sine))
    project = mm(normed, qkv_full)
    roped = rotate(project[:, : query_width + kv_width], cosine, sine).astype(BF16)
    query = roped[:, :query_width].reshape(micro, count, query_width)
    key_value = jnp.concatenate(
        [roped[:, query_width:], project[:, query_width + kv_width :].astype(BF16)], axis=1
    ).reshape(micro, count, 2 * kv_width)
    mixed, kv_slots = plane_attention(query, key_value)
    mixed = mixed.reshape(rows, query_width)
    hidden = x + mm(mixed, out_full)
    inverse_two = lax.rsqrt(jnp.mean(hidden * hidden, axis=-1, keepdims=True) + 1e-05)
    normed_two = (hidden * inverse_two * gain_two).astype(BF16)
    logits = mm(normed_two, router_full)
    chosen = named.reshape(rows, experts)
    logits = jnp.where(chosen, logits, NEG_FILL)
    top = jnp.max(logits, axis=-1, keepdims=True)
    raised = jnp.where(chosen, jnp.exp(logits - top), 0.0)
    gate_probs = raised / jnp.sum(raised, axis=-1, keepdims=True)

    high = gate_probs.astype(BF16)
    low = (gate_probs - high.astype(F32)).astype(BF16)
    payload = jnp.concatenate(
        [normed_two, high, low, jnp.zeros((rows, LANES - 2 * experts), BF16)], axis=1
    ).reshape(micro, count, model + LANES)
    rows_in, row_weights = plane_dispatch(payload, ranks, where, per, cap, model, experts)
    tile = 2 * micro * split * cap
    outs, backs, weight_terms = [], [], []
    for k in range(per):
        out_rows, back_rows, terms = expert_step(
            k, where, rows_in, grads_in, row_weights, (gate_weight, up_weight, down_weight),
            weights_far[k], experts, tile,
        )
        outs.append(out_rows)
        backs.append(back_rows)
        weight_terms.append(terms)
    back = plane_return(backs, ranks, micro, count, cap).reshape(rows, model + LANES)

    mixture_parts = scatter_rows(outs, ranks, where, n, micro * split, count, cap)
    mixture_sum = lax.psum_scatter(mixture_parts, "expert", scatter_dimension=0, tiled=False)
    mixture = mixture_sum[:micro].astype(F32) + turn(mixture_sum[micro:], 1, split).astype(F32)
    block_out = (hidden + mixture.reshape(rows, model)).astype(BF16).reshape(tokens.shape)

    sums = [[None, None] for _ in range(split)]
    merged = []
    for k in range(per):
        sums = [None] * split
        for s in range(groups):
            pair, down = weight_terms[k][s]
            got = [(shift(t, s) if s else t).astype(F32) for t in (pair, down)]
            c = s % split
            sums[c] = got if sums[c] is None else [a + b for a, b in zip(sums[c], got)]
        merged.append(
            [
                [lax.select_n((z - p) % split, sums[0][i], sums[1][i]) for i in range(2)]
                for p in range(split)
            ]
        )
    order = [(p, k) for p in range(split) for k in range(per)]
    gate_grad = jnp.stack([merged[k][p][0][0] for p, k in order])
    up_grad = jnp.stack([merged[k][p][0][1] for p, k in order])
    down_grad = jnp.stack([merged[k][p][1] for p, k in order])

    d_out = cotangent.reshape(rows, model).astype(F32)
    d_gates = back[:, model : model + experts] + back[:, model + experts : model + 2 * experts]
    d_logits = gate_probs * (d_gates - jnp.sum(gate_probs * d_gates, axis=-1, keepdims=True))
    router_grad = lax.dot_general(normed_two.astype(F32), d_logits, TN, precision=HIGHEST)
    d_normed_two = back[:, :model] + lax.dot_general(
        d_logits, router_full.astype(F32), NT, precision=HIGHEST
    )

    def rms_back(inputs, inverse, gain, upstream):
        scaled = gain * upstream
        return inverse * scaled - inputs * inverse * inverse * inverse * jnp.mean(
            scaled * inputs, axis=-1, keepdims=True
        )

    grad_two = jnp.sum(d_normed_two * hidden * inverse_two, axis=0)
    d_hidden = d_out + rms_back(hidden, inverse_two, gain_two, d_normed_two)
    d_attn = d_hidden.astype(BF16)
    d_mixed = mm(d_attn, out_full, NT).astype(BF16).reshape(micro, count, query_width)
    d_query, d_kv = plane_attention_backward(query, kv_slots, d_mixed)
    d_query = d_query.reshape(rows, query_width)
    d_kv = d_kv.reshape(rows, 2 * kv_width)
    q_cos, q_sin = cosine[:, :query_width], sine[:, :query_width]
    d_query_low = rotate(d_query, q_cos, -q_sin).astype(BF16)
    d_key_low = rotate(d_kv[:, :kv_width], q_cos[:, :kv_width], -q_sin[:, :kv_width]).astype(BF16)
    d_project = jnp.concatenate(
        [d_query_low, d_key_low, d_kv[:, kv_width:].astype(BF16)], axis=1
    )
    d_normed = mm(d_project, qkv_full, NT)
    grad_one = jnp.sum(d_normed * x * inverse_one, axis=0)
    input_grad = (d_hidden + rms_back(x, inverse_one, gain_one, d_normed)).reshape(tokens.shape)
    misc_grad = jnp.concatenate(
        [
            grad_one[:, None],
            grad_two[:, None],
            jnp.zeros((model, experts - 2), F32),
            router_grad,
            jnp.zeros((model, LANES - 2 * experts), F32),
        ],
        axis=1,
    )
    dense = plane_gradients([(mixed, d_attn), (normed, d_project)], misc_grad, groups)
    misc_sum = dense[:, model + query_width + 2 * kv_width :]
    return (
        block_out,
        input_grad,
        misc_sum[:, 0],
        dense[:, model : model + query_width + 2 * kv_width],
        dense[:, :model],
        misc_sum[:, 1],
        misc_sum[:, experts : 2 * experts],
        gate_grad,
        up_grad,
        down_grad,
    )


def per_device(*arrays):
    n, groups = lax.axis_size("expert"), lax.axis_size("group")
    exp_here, part, ff = arrays[8].shape
    plane = (
        n == 8
        and exp_here % 2 == 0
        and groups % 2 == 0
        and part % (16 * n) == 0
        and part % LANES == 0
        and arrays[0].shape[0] == 2
    )
    return (layer_plane if plane else layer_general)(*arrays)


def solution(mesh):
    rows = P(None, ("group", "expert"), None)
    return jax.shard_map(
        per_device,
        mesh=mesh,
        in_specs=(
            rows,
            rows,
            rows,
            P("group"),
            P("group", None),
            P("group", None),
            P("group"),
            P("group", None),
            P("expert", "group", None),
            P("expert", "group", None),
            P("expert", None, "group"),
        ),
        out_specs=(
            rows,
            rows,
            P("group"),
            P("group", None),
            P("group", None),
            P("group"),
            P("group", None),
            P("expert", "group", None),
            P("expert", "group", None),
            P("expert", None, "group"),
        ),
        check_vma=False,
    )
```

time: 2040 us -> 999 us (0.49)
  waiting for transfers between devices: 1240 us -> 205 us
  Pallas kernels: 0 us -> 557 us
  matrix products: 286 us -> 29.1 us
  local copies, waits for them, and re-layouts: 247 us -> 53.5 us
  other arithmetic: 117 us -> 35.2 us
  blocking collectives: 78.5 us -> 0 us
  starting transfers between devices: 39.7 us -> 94.1 us
    pallas_call x0 -> x10, Pallas kernels: none -> 557 us  [the longest x1 101 us: plane_weights(): pl.pallas_call(kernel, in_specs=[pl.BlockSpec(memory_space=pltpu.VMEM)] *...]
    all_gather x9 -> x1, waiting for transfers between devices: 404 us -> 0.02 us  [layer_plane(): d_slots = lax.all_gather(both, 'expert', axis=0)]
    reduce_scatter x4 -> x1, waiting for transfers between devices: 351 us -> 0.02 us  [layer_plane(): lax.psum_scatter(mixture_parts, 'expert', scatter_dimension=0, tiled=False)]
    dot_general x64 -> x7, matrix products: 286 us -> 29.1 us  [the longest x5 24.1 us: mm(): return lax.dot_general(a, b, dims, preferred_element_type=F32)]
    all_to_all x8 -> x0, waiting for transfers between devices: 253 us -> none  [the longest x2 99.5 us: per_device(): lax.all_to_all(grad_rows.reshape(expert_count, exp_here, slot_cap, MODEL_...]
    ppermute x0 -> x32, waiting for transfers between devices: none -> 205 us  [the longest x30 174 us: shift(): return lax.ppermute(x, 'group', [(i, (i + step) % n) for i in range(n)])]
    unnamed x26 -> x2, waiting for transfers between devices: 166 us -> 0.03 us
    ppermute x0 -> x32, starting transfers between devices: none -> 94.1 us  [the longest x30 73.6 us: shift(): return lax.ppermute(x, 'group', [(i, (i + step) % n) for i in range(n)])]
  transfers between devices with their start and end apart: 28 -> 34, of which waited for: 21 -> 9; matrix products, arithmetic and copies ran while one was open for 22% -> 10% of each run, Pallas kernels for 0% -> 56%
where the time goes in v1:
time: 999 us; the launch traced here: 990 us
  Pallas kernels  557 us (56%)
  waiting for transfers between devices  205 us (21%)
  starting transfers between devices  94.1 us (9%)
  local copies, waits for them, and re-layouts  53.5 us (5%)
  other arithmetic  35.2 us (4%)
  matrix products  29.1 us (3%)
  between operations  15.8 us (2%)
    ppermute x30, waiting for transfers between devices, shift(): return lax.ppermute(x, 'group', [(i, (i + step) % n) for i in range(n)])  174 us
    pallas_call x1, Pallas kernels, plane_weights(): pl.pallas_call(kernel, in_specs=[pl.BlockSpec(memory_space=pltpu.VMEM)] *...  101 us
    pallas_call x1, Pallas kernels, plane_gradients(): pl.pallas_call(kernel, in_specs=[vmem] * (len(flat) + 1), out_specs=vmem,...  98.8 us
    pallas_call x1, Pallas kernels, plane_dispatch(): pl.pallas_call(kernel, in_specs=[SMEM_SPEC, vmem, vmem], out_specs=[vmem,...  77 us
    pallas_call x2, Pallas kernels, expert_step(): pl.pallas_call(kernel, grid=(steps,), in_specs=[SMEM_SPEC, row_spec, row_...  75.6 us
    ppermute x30, starting transfers between devices, shift(): return lax.ppermute(x, 'group', [(i, (i + step) % n) for i in range(n)])  73.6 us
    pallas_call x1, Pallas kernels, plane_attention_backward(): pl.pallas_call(kernel, in_specs=[vmem] * 3, out_specs=[vmem] * 2, out_sha...  70.8 us
    pallas_call x1, Pallas kernels, plane_return(): pl.pallas_call(kernel, in_specs=[vmem] * (1 + per), out_specs=vmem, out_s...  68 us
  transfers between devices with their start and end apart: 34, of which 9 were waited for; matrix products, arithmetic and copies ran while one was open for 10% of the time, Pallas kernels for 56%

profile of v1, /device:TPU:0, one launch (start us, length us, event | category | flops | bytes accessed | tf_op | source)
XLA Modules:
  0.0 989.9 jit_solution(14311071516903150243)
XLA Ops:
  9.5 3.1 collective-permute-start.6
  12.6 18.9 %collective-permute-done.6 = bf16[2,128,1664]{2,1,0:T(8,128)(2,1)S(1)} collective-permute-done((bf16[2,128,1664]{2,1,0:T(8,128)(2,1)S(1)}, bf16[2,128,1664]{2,1,0:T(8,128)(2,1)S(1)}, u32[]{:S(2)}, u32[]{:S(2)}) %collective-permute-start.6) | collective-permute-done | bytes 852000 | tf_op jit(solution)/shard_map/ppermute | solution.py:44
  60.1 6.0 collective-permute-done.5.refs_7_
  67.6 100.6 %plane_weights.1 = (bf16[1536,2560]{1,0:T(8,128)(2,1)}, bf16[1536,1664]{1,0:T(8,128)(2,1)}) custom-call(bf16[48,2560]{1,0:T(8,128)(2,1)} %copy-done.48, bf16[48,1664]{1,0:T(8,128)(2,1)} %copy-done.52, bf16[48,2560]{1,0:T(8,128)(2,1)} %copy-done.79, bf16[48,1664]{1,0:T(8,128)(2,1)} %copy-done.82, bf16[48,2560]{1,0:T(8,128)(2,1)} %copy-done.80, ...), custom_call_target="tpu_custom_call" | custom-call | flops 49999998976 | bytes 60000000 | tf_op jit(solution)/shard_map/plane_weights/pallas_call | solution.py:1177
  170.1 5.7 fusion.74
  184.0 3.4 collective-permute-start.11
  193.7 4.0 collective-permute-start.12
  198.5 36.8 %plane_attention.1 = (bf16[2,128,1536]{2,1,0:T(8,128)(2,1)}, bf16[8,2,128,1024]{3,2,1,0:T(8,128)(2,1)}) custom-call(bf16[2,128,1536]{2,1,0:T(8,128)(2,1)} %bitcast.123, bf16[2,128,1024]{2,1,0:T(8,128)(2,1)} %bitcast.125), custom_call_target="tpu_custom_call" | custom-call | flops 30000001024 | bytes 20000000 | tf_op jit(solution)/shard_map/plane_attention/pallas_call | solution.py:1266
  235.4 4.3 multiply_reduce_fusion.2
  246.2 15.1 %gather_flags.1 = (bf16[2,1536,1536]{2,1,0:T(8,128)(2,1)}, f32[32,2,128]{2,1,0:T(2,128)}) custom-call(s32[4]{0:T(128)} %pad_add_fusion.at_ref, bf16[8,4,128,1664]{3,2,1,0:T(8,128)(2,1)} %bitcast.130), custom_call_target="tpu_custom_call" | custom-call | flops 5000000000 | bytes 30000000 | tf_op jit(solution)/shard_map/gather_flags/pallas_call | solution.py:1652
  261.4 11.8 %collective-permute-done.10.refs_6_ = bf16[512,384]{1,0:T(8,128)(2,1)} collective-permute-done((bf16[512,384]{1,0:T(8,128)(2,1)}, bf16[512,384]{1,0:T(8,128)(2,1)}, u32[]{:S(2)}, u32[]{:S(2)}) %collective-permute-start.10) | collective-permute-done | bytes 393248 | tf_op jit(solution)/shard_map/ppermute | solution.py:39
  273.2 8.7 collective-permute-start.8
  282.1 77.0 %plane_dispatch.1 = (bf16[2,1536,1536]{2,1,0:T(8,128)(2,1)}, f32[2,1536,128]{2,1,0:T(8,128)}) custom-call(s32[4]{0:T(128)} %pad_add_fusion.at_ref, bf16[2,128,1664]{2,1,0:T(8,128)(2,1)} %bitcast.121, f32[32,2,128]{2,1,0:T(2,128)} %get-tuple-element.66.rank_ref), custom_call_target="tpu_custom_call" | custom-call | flops 60000002048 | bytes 40000000 | tf_op jit(solution)/shard_map/plane_dispatch/pallas_call | solution.py:1430
  360.0 3.1 collective-permute-start.17
  366.3 37.5 %expert_step.2 = (bf16[1536,1536]{1,0:T(8,128)(2,1)}, bf16[1536,1664]{1,0:T(8,128)(2,1)}, bf16[2,384,512]{2,1,0:T(8,128)(2,1)}, bf16[512,384]{1,0:T(8,128)(2,1)}...) custom-call(s32[4]{0:T(128)} %pad_add_fusion.at_ref, ...), custom_call_target="tpu_custom_call" | custom-call | flops 43486543872 | bytes 23592960 | tf_op jit(solution)/shard_map/expert_step/pallas_call | solution.py:1796
  403.8 44.0 %collective-permute-done.16.refs_6_ = bf16[512,384]{1,0:T(8,128)(2,1)} collective-permute-done((bf16[512,384]{1,0:T(8,128)(2,1)}, bf16[512,384]{1,0:T(8,128)(2,1)}, u32[]{:S(2)}, u32[]{:S(2)}) %collective-permute-start.16) | collective-permute-done | bytes 393248 | tf_op jit(solution)/shard_map/ppermute | solution.py:39
  447.9 17.4 %collective-permute-start.27 = (bf16[512,384]{1,0:T(8,128)(2,1)}, bf16[512,384]{1,0:T(8,128)(2,1)}, u32[]{:S(2)}, u32[]{:S(2)}) collective-permute-start(bf16[512,384]{1,0:T(8,128)(2,1)} %get-tuple-element.90), channel_id=1, source_target_pairs={{0,8},{8,16},{16,24},{24,0},{1,9},{9,17},{17,25},{25,1},{2,10},{10... | collective-permute-start | bytes 1179656 | tf_op jit(solution)/shard_map/ppermute | solution.py:39
  465.3 38.0 %expert_step.3 = (bf16[1536,1536]{1,0:T(8,128)(2,1)}, bf16[1536,1664]{1,0:T(8,128)(2,1)}, bf16[2,384,512]{2,1,0:T(8,128)(2,1)}, bf16[512,384]{1,0:T(8,128)(2,1)}...) custom-call(s32[4]{0:T(128)} %pad_add_fusion.at_ref, ...), custom_call_target="tpu_custom_call" | custom-call | flops 43486543872 | bytes 23592960 | tf_op jit(solution)/shard_map/expert_step/pallas_call | solution.py:1796
  504.9 68.0 %plane_return.1 = f32[2,128,1664]{2,1,0:T(8,128)} custom-call(f32[32,2,128]{2,1,0:T(2,128)} %get-tuple-element.66.rank_ref, bf16[1536,1664]{1,0:T(8,128)(2,1)} %get-tuple-element.75.refs_0_, bf16[1536,1664]{1,0:T(8,128)(2,1)} %get-tuple-element.76.refs_1_), custom_call_target="tpu_custom_call" | custom-call | flops 60000002048 | bytes 40000000 | tf_op jit(solution)/shard_map/plane_return/pallas_call | solution.py:1510
  577.0 14.0 %scatter_rows.1 = bf16[8,4,128,1536]{3,2,1,0:T(8,128)(2,1)} custom-call(s32[4]{0:T(128)} %pad_add_fusion.at_ref, f32[32,2,128]{2,1,0:T(2,128)} %get-tuple-element.66.rank_ref, bf16[1536,1536]{1,0:T(8,128)(2,1)} %get-tuple-element.73.refs_0_, bf16[1536,1536]{1,0:T(8,128)(2,1)} %get-tuple-element.74.refs_1_), custom_call_target="tpu_custom_call" | custom-call | flops 5000000000 | bytes 30000000 | tf_op jit(solution)/shard_map/scatter_rows/pallas_call | solution.py:1692
  592.8 4.9 fusion.7
  597.7 70.8 %plane_attention_backward.1 = (f32[2,128,1536]{2,1,0:T(8,128)}, f32[2,128,1024]{2,1,0:T(8,128)}) custom-call(bf16[2,128,1536]{2,1,0:T(8,128)(2,1)} %bitcast.124, bf16[2,128,1536]{2,1,0:T(8,128)(2,1)} %bitcast.133, bf16[8,2,128,1024]{3,2,1,0:T(8,128)(2,1)} %get-tuple-element.77.kv_ref), custom_call_target="tpu_custom_call" | custom-call | flops 49999998976 | bytes 20000000 | tf_op jit(solution)/shard_map/plane_attention_backward/pallas_call | solution.py:1358
  676.7 7.5 fusion.19
  689.3 3.6 concatenate.69.refs_4_
  695.1 98.8 %plane_gradients.1 = f32[384,4224]{1,0:T(8,128)} custom-call(bf16[256,1536]{1,0:T(8,128)(2,1)} %bitcast.132, bf16[256,1536]{1,0:T(8,128)(2,1)} %copy-done.44, bf16[256,1536]{1,0:T(8,128)(2,1)} %copy-done.41, bf16[256,2560]{1,0:T(8,128)(2,1)} %pad_maximum_fusion.4.refs_3_, f32[1536,128]{1,0:T(8,128)} %concatenate.69.refs_4_), custom_call_target="tpu_custom_call" | custom-call | flops 80000000000 | bytes 40000000 | tf_op jit(solution)/shard_map/plane_gradients/pallas_call | solution.py:1608
  793.9 4.3 slice.201
  798.2 3.3 slice.202
  816.7 8.4 collective-permute-start.23
  830.7 45.0 %collective-permute-done.20 = bf16[2,384,512]{2,1,0:T(8,128)(2,1)S(1)} collective-permute-done((bf16[2,384,512]{2,1,0:T(8,128)(2,1)}, bf16[2,384,512]{2,1,0:T(8,128)(2,1)S(1)}, u32[]{:S(2)}, u32[]{:S(2)}) %collective-permute-start.20) | collective-permute-done | bytes 786464 | tf_op jit(solution)/shard_map/ppermute | solution.py:39
  878.7 64.3 %collective-permute-done.23 = bf16[2,384,512]{2,1,0:T(8,128)(2,1)S(1)} collective-permute-done((bf16[2,384,512]{2,1,0:T(8,128)(2,1)S(1)}, bf16[2,384,512]{2,1,0:T(8,128)(2,1)S(1)}, u32[]{:S(2)}, u32[]{:S(2)}) %collective-permute-start.23) | collective-permute-done | bytes 786464 | tf_op jit(solution)/shard_map/ppermute | solution.py:39
  944.7 17.4 %collective-permute-start.19 = (bf16[2,128,1536]{2,1,0:T(8,128)(2,1)S(1)}, bf16[2,128,1536]{2,1,0:T(8,128)(2,1)S(1)}, u32[]{:S(2)}, u32[]{:S(2)}) collective-permute-start(bf16[2,128,1536]{2,1,0:T(8,128)(2,1)S(1)} %slice_bitcast_fusion), channel_id=1, source_target_pairs={{8,0},{0,8},{24,16},{16,24},{9,1},{1,9},{25,17},{17,25},{10,2},{2,... | collective-permute-start | bytes 2359304 | tf_op jit(solution)/shard_map/ppermute | solution.py:44
  967.6 12.2 %collective-permute-done.19 = bf16[2,128,1536]{2,1,0:T(8,128)(2,1)S(1)} collective-permute-done((bf16[2,128,1536]{2,1,0:T(8,128)(2,1)S(1)}, bf16[2,128,1536]{2,1,0:T(8,128)(2,1)S(1)}, u32[]{:S(2)}, u32[]{:S(2)}) %collective-permute-start.19) | collective-permute-done | bytes 786464 | tf_op jit(solution)/shard_map/ppermute | solution.py:44
  (319 shorter events, 116.0 us)
Async XLA Ops:
  7.2 239.0 %all-gather.3.cloned.1.call-start = ((), (), s32[]{:S(2)}) async-start(), calls=%async_computation.2 | async-start | bytes 15335424 | tf_op jit(solution)/shard_map/all_gather | solution.py:1893
  9.5 22.1 %collective-permute-start.6 = (bf16[2,128,1664]{2,1,0:T(8,128)(2,1)S(1)}, bf16[2,128,1664]{2,1,0:T(8,128)(2,1)S(1)}, u32[]{:S(2)}, u32[]{:S(2)}) collective-permute-start(bf16[2,128,1664]{2,1,0:T(8,128)(2,1)S(1)} %concatenate.61), channel_id=1, source_target_pairs={{8,0},{0,8},{24,16},{16,24},{9,1},{1,9},{25,17},{17,25},{10,2},{2,... | collective-permute-start | bytes 2555912 | tf_op jit(solution)/shard_map/ppermute | solution.py:44
  33.0 910.5 %reduce-scatter.2.cloned.1.call-start = ((), (), s32[]{:S(2)}) async-start(), calls=%async_computation.1 | async-start | bytes 14155776 | tf_op jit(solution)/shard_map/reduce_scatter | solution.py:1941
  37.0 23.1 %collective-permute-start.4 = (bf16[48,1664]{1,0:T(8,128)(2,1)S(1)}, bf16[48,1664]{1,0:T(8,128)(2,1)}, u32[]{:S(2)}, u32[]{:S(2)}) collective-permute-start(bf16[48,1664]{1,0:T(8,128)(2,1)S(1)} %pad_maximum_fusion.12.refs_1_), channel_id=1, source_target_pairs={{0,16},{8,24},{16,0},{24,8},{1,17},{9,25},{17,1},{25,9},{2,18},{10... | collective-permute-start | bytes 479240 | tf_op jit(solution)/shard_map/ppermute | solution.py:39
  39.7 26.4 %collective-permute-start = (bf16[48,2560]{1,0:T(8,128)(2,1)S(1)}, bf16[48,2560]{1,0:T(8,128)(2,1)S(1)}, u32[]{:S(2)}, u32[]{:S(2)}) collective-permute-start(bf16[48,2560]{1,0:T(8,128)(2,1)S(1)} %constant_dynamic-slice_fusion.14.refs_0_), channel_id=1, source_target_pairs={{0,8},{8,16},{16,24},{24,0},{1,9},{9,17},{17,25},{25,1},{2,10},{10... | collective-permute-start | bytes 737288 | tf_op jit(solution)/shard_map/ppermute | solution.py:39
  39.8 26.3 %collective-permute-start.1 = (bf16[48,2560]{1,0:T(8,128)(2,1)S(1)}, bf16[48,2560]{1,0:T(8,128)(2,1)S(1)}, u32[]{:S(2)}, u32[]{:S(2)}) collective-permute-start(bf16[48,2560]{1,0:T(8,128)(2,1)S(1)} %constant_dynamic-slice_fusion.14.refs_0_), channel_id=1, source_target_pairs={{0,16},{8,24},{16,0},{24,8},{1,17},{9,25},{17,1},{25,9},{2,18},{10... | collective-permute-start | bytes 737288 | tf_op jit(solution)/shard_map/ppermute | solution.py:39
  41.6 24.4 %collective-permute-start.2 = (bf16[48,2560]{1,0:T(8,128)(2,1)S(1)}, bf16[48,2560]{1,0:T(8,128)(2,1)S(1)}, u32[]{:S(2)}, u32[]{:S(2)}) collective-permute-start(bf16[48,2560]{1,0:T(8,128)(2,1)S(1)} %constant_dynamic-slice_fusion.14.refs_0_), channel_id=1, source_target_pairs={{0,24},{8,0},{16,8},{24,16},{1,25},{9,1},{17,9},{25,17},{2,26},{10... | collective-permute-start | bytes 737288 | tf_op jit(solution)/shard_map/ppermute | solution.py:39
  45.7 20.3 %collective-permute-start.5 = (bf16[48,1664]{1,0:T(8,128)(2,1)S(1)}, bf16[48,1664]{1,0:T(8,128)(2,1)S(1)}, u32[]{:S(2)}, u32[]{:S(2)}) collective-permute-start(bf16[48,1664]{1,0:T(8,128)(2,1)S(1)} %pad_maximum_fusion.12.refs_1_), channel_id=1, source_target_pairs={{0,24},{8,0},{16,8},{24,16},{1,25},{9,1},{17,9},{25,17},{2,26},{10... | collective-permute-start | bytes 479240 | tf_op jit(solution)/shard_map/ppermute | solution.py:39
  184.0 176.0 %collective-permute-start.11 = (bf16[2,384,512]{2,1,0:T(8,128)(2,1)}, bf16[2,384,512]{2,1,0:T(8,128)(2,1)}, u32[]{:S(2)}, u32[]{:S(2)}) collective-permute-start(bf16[2,384,512]{2,1,0:T(8,128)(2,1)} %pad_maximum_fusion.7), channel_id=1, source_target_pairs={{0,24},{8,0},{16,8},{24,16},{1,25},{9,1},{17,9},{25,17},{2,26},{10... | collective-permute-start | bytes 2359304 | tf_op jit(solution)/shard_map/ppermute | solution.py:39
  188.4 174.7 %collective-permute-start.7 = (bf16[2,384,512]{2,1,0:T(8,128)(2,1)}, bf16[2,384,512]{2,1,0:T(8,128)(2,1)}, u32[]{:S(2)}, u32[]{:S(2)}) collective-permute-start(bf16[2,384,512]{2,1,0:T(8,128)(2,1)} %pad_maximum_fusion.5), channel_id=1, source_target_pairs={{0,8},{8,16},{16,24},{24,0},{1,9},{9,17},{17,25},{25,1},{2,10},{10... | collective-permute-start | bytes 2359304 | tf_op jit(solution)/shard_map/ppermute | solution.py:39
  189.3 175.8 %collective-permute-start.9 = (bf16[2,384,512]{2,1,0:T(8,128)(2,1)}, bf16[2,384,512]{2,1,0:T(8,128)(2,1)}, u32[]{:S(2)}, u32[]{:S(2)}) collective-permute-start(bf16[2,384,512]{2,1,0:T(8,128)(2,1)} %pad_maximum_fusion.6), channel_id=1, source_target_pairs={{0,16},{8,24},{16,0},{24,8},{1,17},{9,25},{17,1},{25,9},{2,18},{10... | collective-permute-start | bytes 2359304 | tf_op jit(solution)/shard_map/ppermute | solution.py:39
  191.9 81.3 %collective-permute-start.10 = (bf16[512,384]{1,0:T(8,128)(2,1)}, bf16[512,384]{1,0:T(8,128)(2,1)}, u32[]{:S(2)}, u32[]{:S(2)}) collective-permute-start(bf16[512,384]{1,0:T(8,128)(2,1)} %get-tuple-element.177), channel_id=1, source_target_pairs={{0,16},{8,24},{16,0},{24,8},{1,17},{9,25},{17,1},{25,9},{2,18},{10... | collective-permute-start | bytes 1179656 | tf_op jit(solution)/shard_map/ppermute | solution.py:39
  193.7 88.2 %collective-permute-start.12 = (bf16[512,384]{1,0:T(8,128)(2,1)}, bf16[512,384]{1,0:T(8,128)(2,1)}, u32[]{:S(2)}, u32[]{:S(2)}) collective-permute-start(bf16[512,384]{1,0:T(8,128)(2,1)} %get-tuple-element.176), channel_id=1, source_target_pairs={{0,24},{8,0},{16,8},{24,16},{1,25},{9,1},{17,9},{25,17},{2,26},{10... | collective-permute-start | bytes 1179656 | tf_op jit(solution)/shard_map/ppermute | solution.py:39
  273.2 86.0 %collective-permute-start.8 = (bf16[512,384]{1,0:T(8,128)(2,1)}, bf16[512,384]{1,0:T(8,128)(2,1)}, u32[]{:S(2)}, u32[]{:S(2)}) collective-permute-start(bf16[512,384]{1,0:T(8,128)(2,1)} %get-tuple-element.178), channel_id=1, source_target_pairs={{0,8},{8,16},{16,24},{24,0},{1,9},{9,17},{17,25},{25,1},{2,10},{10... | collective-permute-start | bytes 1179656 | tf_op jit(solution)/shard_map/ppermute | solution.py:39
  281.9 77.4 %collective-permute-start.14 = (bf16[512,384]{1,0:T(8,128)(2,1)}, bf16[512,384]{1,0:T(8,128)(2,1)}, u32[]{:S(2)}, u32[]{:S(2)}) collective-permute-start(bf16[512,384]{1,0:T(8,128)(2,1)} %get-tuple-element.175), channel_id=1, source_target_pairs={{0,8},{8,16},{16,24},{24,0},{1,9},{9,17},{17,25},{25,1},{2,10},{10... | collective-permute-start | bytes 1179656 | tf_op jit(solution)/shard_map/ppermute | solution.py:39
  359.2 106.1 %collective-permute-start.13 = (bf16[2,384,512]{2,1,0:T(8,128)(2,1)}, bf16[2,384,512]{2,1,0:T(8,128)(2,1)}, u32[]{:S(2)}, u32[]{:S(2)}) collective-permute-start(bf16[2,384,512]{2,1,0:T(8,128)(2,1)} %pad_maximum_fusion.8), channel_id=1, source_target_pairs={{0,8},{8,16},{16,24},{24,0},{1,9},{9,17},{17,25},{25,1},{2,10},{10... | collective-permute-start | bytes 2359304 | tf_op jit(solution)/shard_map/ppermute | solution.py:39
  359.3 106.0 %collective-permute-start.15 = (bf16[2,384,512]{2,1,0:T(8,128)(2,1)S(1)}, bf16[2,384,512]{2,1,0:T(8,128)(2,1)}, u32[]{:S(2)}, u32[]{:S(2)}) collective-permute-start(bf16[2,384,512]{2,1,0:T(8,128)(2,1)S(1)} %copy-done.40), channel_id=1, source_target_pairs={{0,16},{8,24},{16,0},{24,8},{1,17},{9,25},{17,1},{25,9},{2,18},{10... | collective-permute-start | bytes 2359304 | tf_op jit(solution)/shard_map/ppermute | solution.py:39
  360.0 105.2 %collective-permute-start.17 = (bf16[2,384,512]{2,1,0:T(8,128)(2,1)S(1)}, bf16[2,384,512]{2,1,0:T(8,128)(2,1)}, u32[]{:S(2)}, u32[]{:S(2)}) collective-permute-start(bf16[2,384,512]{2,1,0:T(8,128)(2,1)S(1)} %pad_maximum_fusion.10), channel_id=1, source_target_pairs={{0,24},{8,0},{16,8},{24,16},{1,25},{9,1},{17,9},{25,17},{2,26},{10... | collective-permute-start | bytes 2359304 | tf_op jit(solution)/shard_map/ppermute | solution.py:39
  363.1 84.7 %collective-permute-start.16 = (bf16[512,384]{1,0:T(8,128)(2,1)}, bf16[512,384]{1,0:T(8,128)(2,1)}, u32[]{:S(2)}, u32[]{:S(2)}) collective-permute-start(bf16[512,384]{1,0:T(8,128)(2,1)} %get-tuple-element.174), channel_id=1, source_target_pairs={{0,16},{8,24},{16,0},{24,8},{1,17},{9,25},{17,1},{25,9},{2,18},{10... | collective-permute-start | bytes 1179656 | tf_op jit(solution)/shard_map/ppermute | solution.py:39
  365.1 82.8 %collective-permute-start.18 = (bf16[512,384]{1,0:T(8,128)(2,1)S(1)}, bf16[512,384]{1,0:T(8,128)(2,1)}, u32[]{:S(2)}, u32[]{:S(2)}) collective-permute-start(bf16[512,384]{1,0:T(8,128)(2,1)S(1)} %copy-done.45), channel_id=1, source_target_pairs={{0,24},{8,0},{16,8},{24,16},{1,25},{9,1},{17,9},{25,17},{2,26},{10... | collective-permute-start | bytes 1179656 | tf_op jit(solution)/shard_map/ppermute | solution.py:39
  447.8 356.9 %collective-permute-start.26 = (bf16[512,384]{1,0:T(8,128)(2,1)}, bf16[512,384]{1,0:T(8,128)(2,1)}, u32[]{:S(2)}, u32[]{:S(2)}) collective-permute-start(bf16[512,384]{1,0:T(8,128)(2,1)} %get-tuple-element.89), channel_id=1, source_target_pairs={{0,16},{8,24},{16,0},{24,8},{1,17},{9,25},{17,1},{25,9},{2,18},{10... | collective-permute-start | bytes 1179656 | tf_op jit(solution)/shard_map/ppermute | solution.py:39
  447.9 361.3 %collective-permute-start.27 = (bf16[512,384]{1,0:T(8,128)(2,1)}, bf16[512,384]{1,0:T(8,128)(2,1)}, u32[]{:S(2)}, u32[]{:S(2)}) collective-permute-start(bf16[512,384]{1,0:T(8,128)(2,1)} %get-tuple-element.90), channel_id=1, source_target_pairs={{0,8},{8,16},{16,24},{24,0},{1,9},{9,17},{17,25},{25,1},{2,10},{10... | collective-permute-start | bytes 1179656 | tf_op jit(solution)/shard_map/ppermute | solution.py:39
  465.3 343.9 %collective-permute-start.28 = (bf16[512,384]{1,0:T(8,128)(2,1)}, bf16[512,384]{1,0:T(8,128)(2,1)}, u32[]{:S(2)}, u32[]{:S(2)}) collective-permute-start(bf16[512,384]{1,0:T(8,128)(2,1)} %get-tuple-element.91), channel_id=1, source_target_pairs={{0,24},{8,0},{16,8},{24,16},{1,25},{9,1},{17,9},{25,17},{2,26},{10... | collective-permute-start | bytes 1179656 | tf_op jit(solution)/shard_map/ppermute | solution.py:39
  503.3 307.0 %collective-permute-start.29 = (bf16[512,384]{1,0:T(8,128)(2,1)}, bf16[512,384]{1,0:T(8,128)(2,1)}, u32[]{:S(2)}, u32[]{:S(2)}) collective-permute-start(bf16[512,384]{1,0:T(8,128)(2,1)} %get-tuple-element.93), channel_id=1, source_target_pairs={{0,16},{8,24},{16,0},{24,8},{1,17},{9,25},{17,1},{25,9},{2,18},{10... | collective-permute-start | bytes 1179656 | tf_op jit(solution)/shard_map/ppermute | solution.py:39
  804.7 20.4 %collective-permute-start.31 = (bf16[512,384]{1,0:T(8,128)(2,1)}, bf16[512,384]{1,0:T(8,128)(2,1)S(1)}, u32[]{:S(2)}, u32[]{:S(2)}) collective-permute-start(bf16[512,384]{1,0:T(8,128)(2,1)} %get-tuple-element.95), channel_id=1, source_target_pairs={{0,24},{8,0},{16,8},{24,16},{1,25},{9,1},{17,9},{25,17},{2,26},{10... | collective-permute-start | bytes 1179656 | tf_op jit(solution)/shard_map/ppermute | solution.py:39
  809.1 66.5 %collective-permute-start.20 = (bf16[2,384,512]{2,1,0:T(8,128)(2,1)}, bf16[2,384,512]{2,1,0:T(8,128)(2,1)S(1)}, u32[]{:S(2)}, u32[]{:S(2)}) collective-permute-start(bf16[2,384,512]{2,1,0:T(8,128)(2,1)} %get-tuple-element.81), channel_id=1, source_target_pairs={{0,16},{8,24},{16,0},{24,8},{1,17},{9,25},{17,1},{25,9},{2,18},{10... | collective-permute-start | bytes 2359304 | tf_op jit(solution)/shard_map/ppermute | solution.py:39
  809.2 66.5 %collective-permute-start.21 = (bf16[2,384,512]{2,1,0:T(8,128)(2,1)}, bf16[2,384,512]{2,1,0:T(8,128)(2,1)S(1)}, u32[]{:S(2)}, u32[]{:S(2)}) collective-permute-start(bf16[2,384,512]{2,1,0:T(8,128)(2,1)} %get-tuple-element.82), channel_id=1, source_target_pairs={{0,8},{8,16},{16,24},{24,0},{1,9},{9,17},{17,25},{25,1},{2,10},{10... | collective-permute-start | bytes 2359304 | tf_op jit(solution)/shard_map/ppermute | solution.py:39
  810.4 65.3 %collective-permute-start.22 = (bf16[2,384,512]{2,1,0:T(8,128)(2,1)S(1)}, bf16[2,384,512]{2,1,0:T(8,128)(2,1)S(1)}, u32[]{:S(2)}, u32[]{:S(2)}) collective-permute-start(bf16[2,384,512]{2,1,0:T(8,128)(2,1)S(1)} %copy-done.75), channel_id=1, source_target_pairs={{0,24},{8,0},{16,8},{24,16},{1,25},{9,1},{17,9},{25,17},{2,26},{10... | collective-permute-start | bytes 2359304 | tf_op jit(solution)/shard_map/ppermute | solution.py:39
  816.7 126.3 %collective-permute-start.23 = (bf16[2,384,512]{2,1,0:T(8,128)(2,1)S(1)}, bf16[2,384,512]{2,1,0:T(8,128)(2,1)S(1)}, u32[]{:S(2)}, u32[]{:S(2)}) collective-permute-start(bf16[2,384,512]{2,1,0:T(8,128)(2,1)S(1)} %copy-done.78), channel_id=1, source_target_pairs={{0,16},{8,24},{16,0},{24,8},{1,17},{9,25},{17,1},{25,9},{2,18},{10... | collective-permute-start | bytes 2359304 | tf_op jit(solution)/shard_map/ppermute | solution.py:39
  825.1 117.9 %collective-permute-start.24 = (bf16[2,384,512]{2,1,0:T(8,128)(2,1)S(1)}, bf16[2,384,512]{2,1,0:T(8,128)(2,1)S(1)}, u32[]{:S(2)}, u32[]{:S(2)}) collective-permute-start(bf16[2,384,512]{2,1,0:T(8,128)(2,1)S(1)} %copy-done.77), channel_id=1, source_target_pairs={{0,8},{8,16},{16,24},{24,0},{1,9},{9,17},{17,25},{25,1},{2,10},{10... | collective-permute-start | bytes 2359304 | tf_op jit(solution)/shard_map/ppermute | solution.py:39
  875.7 67.3 %collective-permute-start.25 = (bf16[2,384,512]{2,1,0:T(8,128)(2,1)S(1)}, bf16[2,384,512]{2,1,0:T(8,128)(2,1)S(1)}, u32[]{:S(2)}, u32[]{:S(2)}) collective-permute-start(bf16[2,384,512]{2,1,0:T(8,128)(2,1)S(1)} %copy-done.76), channel_id=1, source_target_pairs={{0,24},{8,0},{16,8},{24,16},{1,25},{9,1},{17,9},{25,17},{2,26},{10... | collective-permute-start | bytes 2359304 | tf_op jit(solution)/shard_map/ppermute | solution.py:39
  944.7 35.1 %collective-permute-start.19 = (bf16[2,128,1536]{2,1,0:T(8,128)(2,1)S(1)}, bf16[2,128,1536]{2,1,0:T(8,128)(2,1)S(1)}, u32[]{:S(2)}, u32[]{:S(2)}) collective-permute-start(bf16[2,128,1536]{2,1,0:T(8,128)(2,1)S(1)} %slice_bitcast_fusion), channel_id=1, source_target_pairs={{8,0},{0,8},{24,16},{16,24},{9,1},{1,9},{25,17},{17,25},{10,2},{2,... | collective-permute-start | bytes 2359304 | tf_op jit(solution)/shard_map/ppermute | solution.py:44
  (87 other events, 1342.3 us)
Sparse Core Ops, SparseCore 0:
  33.1 114.0 all-gather.2
  591.2 110.4 reduce-scatter.1

commit v2 on v1

--- a/solution.py
+++ b/solution.py
@@ -1034,6 +1034,12 @@
         for q in (2, 4, 6):
             self.copy(q, 1, c).wait_send()
 
+    def stage(self, chunks, slots):
+        for c in chunks:
+            for q in slots:
+                self.arrived(q, c)
+                self.pass_on(q, c)
+
     def forward_all(self, chunks, use=None):
         for c in chunks:
             for q in (2, 4):
@@ -1146,15 +1152,17 @@
     )
 
 
-def plane_weights(sets):
-    groups, n = len(sets[0]), 8
-    rows = sets[0][0].shape[0]
-    kinds = len(sets)
+def plane_weights(shares, bank, per):
+    n, split = 8, 2
+    groups = lax.axis_size("group")
+    rows = shares[0].shape[0]
+    kinds = len(shares)
     count = groups * kinds
 
     def kernel(*refs):
-        ins, outs = refs[:count], refs[count : count + kinds]
-        send, recv, local = refs[count + kinds :]
+        ins, bank_ref, refs = refs[:kinds], refs[kinds], refs[kinds + 1 :]
+        outs, far_ref, refs = refs[:kinds], refs[kinds], refs[kinds + 1 :]
+        z_send, z_recv, send, recv, local, b_send, b_recv = refs
         e, z = lax.axis_index("expert"), lax.axis_index("group")
 
         def loc(r, q, c):
@@ -1162,32 +1170,75 @@
             row = (lax.rem(z - s + groups, groups) * n + flip(e, r)) * rows
             return outs[kind].at[pl.ds(pl.multiple_of(row, 16), rows), :]
 
-        gather = Gather(e, lambda c: ins[c], loc, [c // kinds % 2 for c in range(count)], send, recv)
-        greet(plane_devices(e))
-        for c in range(count):
+        def far(c):
+            s, kind = c // kinds, c % kinds
+            return remote(
+                ins[kind], loc(0, 0, kind), z_send.at[c], z_recv.at[c],
+                {"group": lax.rem(z + s, groups)},
+            )
+
+        def landed(c):
+            remote(
+                loc(0, 0, c), loc(0, 0, c), z_send.at[c], z_recv.at[c],
+                {"group": lax.rem(z + c // kinds, groups)},
+            ).wait_recv()
+
+        first = lax.rem(z + 1, split) * per
+        follow = remote(
+            bank_ref.at[pl.ds(first, per)], far_ref, b_send, b_recv, {"group": lax.rem(z + 1, groups)}
+        )
+        gather = Gather(
+            e, lambda c: ins[c] if c < kinds else loc(0, 0, c), loc,
+            [c // kinds % 2 for c in range(count)], send, recv,
+        )
+        near = list(range(kinds))
+        later = list(range(kinds, count))
+        greet(
+            plane_devices(e) + [{"group": lax.rem(z + s, groups)} for s in range(1, groups)]
+        )
+        for c in later:
+            far(c).start()
+        for c in near:
             gather.begin(c)
             pltpu.make_async_copy(ins[c], loc(0, 0, c), local.at[c]).start()
-        gather.forward_all(range(count))
-        for c in range(count):
+        follow.start()
+        gather.stage(near, (2, 4))
+        gather.stage(near, (6,))
+        for c in later:
+            landed(c)
+            gather.begin(c)
+        gather.stage(later, (2, 4))
+        gather.stage(later, (6,))
+        gather.stage(near + later, (1, 3, 5, 7))
+        for c in later:
+            far(c).wait_send()
+        for c in near + later:
             gather.finish(c)
+        for c in near:
             pltpu.make_async_copy(ins[c], loc(0, 0, c), local.at[c]).wait()
-
-    flat = [sets[kind][s] for s in range(groups) for kind in range(kinds)]
-    shapes = [(groups * n * rows, one[0].shape[1]) for one in sets]
+        follow.wait()
+
+    vmem = pl.BlockSpec(memory_space=pltpu.VMEM)
+    shapes = [(groups * n * rows, one.shape[1]) for one in shares]
     return pl.pallas_call(
         kernel,
-        in_specs=[pl.BlockSpec(memory_space=pltpu.VMEM)] * count,
-        out_specs=[pl.BlockSpec(memory_space=pltpu.VMEM)] * kinds,
-        out_shape=[jax.ShapeDtypeStruct(shape, BF16) for shape in shapes],
+        in_specs=[vmem] * kinds + [ANY_SPEC],
+        out_specs=[vmem] * kinds + [ANY_SPEC],
+        out_shape=[jax.ShapeDtypeStruct(shape, BF16) for shape in shapes]
+        + [jax.ShapeDtypeStruct((per,) + bank.shape[1:], BF16)],
         scratch_shapes=[
+            pltpu.SemaphoreType.DMA((count,)),
+            pltpu.SemaphoreType.DMA((count,)),
             pltpu.SemaphoreType.DMA((n, count)),
             pltpu.SemaphoreType.DMA((n, count)),
-            pltpu.SemaphoreType.DMA((count,)),
+            pltpu.SemaphoreType.DMA((kinds,)),
+            pltpu.SemaphoreType.DMA,
+            pltpu.SemaphoreType.DMA,
         ],
         compiler_params=params(1),
-        cost_estimate=cost(5e10, 6e7),
+        cost_estimate=cost(1e9, 1e6),
         name="plane_weights",
-    )(*flat)
+    )(*shares, bank)
 
 
 def attention_pairs(n, at_me, q_ref, keys, out_ref):
@@ -1278,7 +1329,7 @@
             pltpu.SemaphoreType.DMA((micro,)),
         ],
         compiler_params=params(2),
-        cost_estimate=cost(3e10, 2e7),
+        cost_estimate=cost(1e9, 1e6),
         name="plane_attention",
     )(query, key_value)
 
@@ -1370,7 +1421,7 @@
         ]
         + reduce_scratch(micro, tokens, width),
         compiler_params=params(3),
-        cost_estimate=cost(5e10, 2e7),
+        cost_estimate=cost(1e9, 1e6),
         name="plane_attention_backward",
     )(query, d_mixed, slots)
 
@@ -1443,20 +1494,18 @@
             pltpu.SemaphoreType.DMA((n, count)),
         ],
         compiler_params=params(4),
-        cost_estimate=cost(6e10, 4e7),
+        cost_estimate=cost(1e9, 1e6),
         name="plane_dispatch",
     )(where, payload, ranks)
 
 
 def plane_return(rows, ranks, micro, tokens, cap):
-    per = len(rows)
-    width = rows[0].shape[1]
+    per, _, width = rows.shape
     n, split = 8, 2
     count = split * micro
     chunks = list(range(micro, count)) + list(range(micro))
 
-    def kernel(rank_ref, *refs):
-        ins, out, refs = refs[:per], refs[per], refs[per + 1 :]
+    def kernel(rank_ref, in_ref, out, *refs):
         parts, z_out, z_in, z_send, z_recv, scratch = *refs[:5], refs[5:]
         e, z = lax.axis_index("expert"), lax.axis_index("group")
         red = Reduce(e, lambda r, c: parts.at[r, c], [c % 2 for c in range(count)], *scratch)
@@ -1466,7 +1515,7 @@
             total = None
             for k in range(per):
                 one = mm(
-                    pick(rank_ref[b, k : k + 1, :], cap), ins[k][b * cap : (b + 1) * cap, :], TN
+                    pick(rank_ref[b, k : k + 1, :], cap), in_ref[k, b * cap : (b + 1) * cap, :], TN
                 )
                 total = one if total is None else total + one
             parts[r, c] = total.astype(BF16)
@@ -1509,7 +1558,7 @@
     vmem = pl.BlockSpec(memory_space=pltpu.VMEM)
     return pl.pallas_call(
         kernel,
-        in_specs=[vmem] * (1 + per),
+        in_specs=[vmem] * 2,
         out_specs=vmem,
         out_shape=jax.ShapeDtypeStruct((micro, tokens, width), F32),
         scratch_shapes=[
@@ -1521,9 +1570,9 @@
         ]
         + reduce_scratch(count, tokens, width),
         compiler_params=params(5),
-        cost_estimate=cost(6e10, 4e7),
+        cost_estimate=cost(1e9, 1e6),
         name="plane_return",
-    )(ranks, *rows)
+    )(ranks, rows)
 
 
 def plane_gradients(products, extra, groups):
@@ -1624,7 +1673,7 @@
         ]
         + reduce_scratch(groups, rows, width),
         compiler_params=params(6),
-        cost_estimate=cost(8e10, 4e7),
+        cost_estimate=cost(1e9, 1e6),
         name="plane_gradients",
     )(*flat, extra)
 
@@ -1676,15 +1725,14 @@
 
 
 def scatter_rows(rows, ranks, where, n, count, tokens, cap):
-    per, width = len(rows), rows[0].shape[1]
-
-    def kernel(at_ref, rank_ref, *refs):
-        ins, out = refs[:per], refs[per]
+    per, _, width = rows.shape
+
+    def kernel(at_ref, rank_ref, in_ref, out):
         for b in range(count):
             total = None
             for k in range(per):
                 one = mm(
-                    pick(rank_ref[b, k : k + 1, :], cap), ins[k][b * cap : (b + 1) * cap, :], TN
+                    pick(rank_ref[b, k : k + 1, :], cap), in_ref[k, b * cap : (b + 1) * cap, :], TN
                 )
                 total = one if total is None else total + one
             out[0, b] = total.astype(BF16)
@@ -1694,8 +1742,10 @@
         grid_spec=pltpu.PrefetchScalarGridSpec(
             num_scalar_prefetch=1,
             grid=(n,),
-            in_specs=[pl.BlockSpec((count, per, tokens), lambda r, at: (r, 0, 0))]
-            + [pl.BlockSpec((count * cap, width), lambda r, at: (r, 0))] * per,
+            in_specs=[
+                pl.BlockSpec((count, per, tokens), lambda r, at: (r, 0, 0)),
+                pl.BlockSpec((per, count * cap, width), lambda r, at: (0, r, 0)),
+            ],
             out_specs=pl.BlockSpec(
                 (1, count, tokens, width), lambda r, at: (jnp.bitwise_xor(at[1], r), 0, 0, 0)
             ),
@@ -1703,80 +1753,81 @@
         out_shape=jax.ShapeDtypeStruct((n, count, tokens, width), BF16),
         cost_estimate=cost(5e9, 3e7),
         name="scatter_rows",
-    )(where, ranks, *rows)
-
-
-def expert_step(k, at, rows_in, grads_in, weights, own, far, experts, tile):
+    )(where, ranks, rows)
+
+
+def expert_steps(at, rows_in, grads_in, weights, bank, far, experts, tile):
     per, total, model = rows_in.shape
-    part, ff = own[0].shape[1:]
+    part, ff = bank.shape[2:]
     groups = model // part
     steps = total // tile
-    held_count = 3 + 2 * (groups - 1)
 
     def kernel(at_ref, x_ref, d_ref, w_ref, *refs):
-        sources, refs = refs[:held_count], refs[held_count:]
-        o_ref, r_ref, refs = refs[0], refs[1], refs[2:]
-        outs, refs = refs[: 2 * groups], refs[2 * groups :]
-        acc_gate, acc_up, acc_down, gate_ref, up_ref, down_ref, sems = refs
-        step = pl.program_id(0)
-
-        @pl.when(step == 0)
-        def _():
+        sources, o_ref, r_ref, refs = refs[:groups], refs[groups], refs[groups + 1], refs[groups + 2 :]
+        outs, (acc_wide, acc_down, wide_all, down_all, sems) = refs[:groups], refs[groups:]
+        k, step = pl.program_id(0), pl.program_id(1)
+
+        def loads(index):
             copies = []
             for s in range(groups):
                 z = lax.rem(at_ref[0] - s + groups, groups)
                 at_z = pl.ds(pl.multiple_of(z * part, 128), part)
-                if s == 0:
-                    mine = at_ref[3] + k
-                    three = [sources[i].at[mine] for i in range(3)]
-                else:
-                    pair = sources[3 + 2 * (s - 1)]
-                    three = [pair.at[0], pair.at[1], sources[4 + 2 * (s - 1)]]
-                for i, dst in enumerate(
-                    [gate_ref.at[at_z, :], up_ref.at[at_z, :], down_ref.at[:, at_z]]
-                ):
-                    copies.append(pltpu.make_async_copy(three[i], dst, sems.at[3 * s + i]))
-            for one in copies:
-                one.start()
-            for one in copies:
-                one.wait()
-
+                source = sources[s].at[at_ref[3] + index if s == 0 else index]
+                wide, down = wide_all.at[index], down_all.at[index]
+                for i, dst in enumerate([wide.at[at_z, :ff], wide.at[at_z, ff:], down.at[at_z, :]]):
+                    copies.append(
+                        pltpu.make_async_copy(source.at[i], dst, sems.at[index, 3 * s + i])
+                    )
+            return copies
+
+        for index in range(per):
+
+            @pl.when((k == 0) & (step == 0))
+            def _():
+                for one in loads(index):
+                    one.start()
+
+        for index in range(per):
+
+            @pl.when((k == index) & (step == 0))
+            def _():
+                for one in loads(index):
+                    one.wait()
+
+        wide_ref, down_ref = wide_all.at[k], down_all.at[k]
         x, d = x_ref[0], d_ref[0]
         w = w_ref[0, :, 0:1]
-        gate_pre = mm(x, gate_ref[...])
-        up_pre = mm(x, up_ref[...])
+        pre = mm(x, wide_ref[...])
+        gate_pre, up_pre = pre[:, :ff], pre[:, ff:]
         sig = 1.0 / (1.0 + jnp.exp(-gate_pre))
         silu = gate_pre * sig
         active_wide = silu * up_pre
         active = active_wide.astype(BF16)
-        o_ref[...] = (mm(active, down_ref[...]) * w).astype(BF16)
-        d_raw = mm(d, down_ref[...], NT)
+        o_ref[0] = (mm(active, down_ref[...], NT) * w).astype(BF16)
+        d_raw = mm(d, down_ref[...])
         d_gates = jnp.sum(active.astype(F32) * d_raw, axis=1, keepdims=True)
         d_active = d_raw * w
         d_up = (d_active * silu).astype(BF16)
         d_gate = (d_active * up_pre * sig * (1.0 + gate_pre * (1.0 - sig))).astype(BF16)
-        d_row = mm(d_gate, gate_ref[...], NT) + mm(d_up, up_ref[...], NT)
-        r_ref[:, :model] = d_row.astype(BF16)
+        d_both = jnp.concatenate([d_gate, d_up], axis=1)
+        r_ref[0, :, :model] = mm(d_both, wide_ref[...], NT).astype(BF16)
         high = d_gates.astype(BF16).astype(F32)
         lane = lax.broadcasted_iota(jnp.int32, (tile, LANES), 1)
         e = at_ref[2] + k
-        r_ref[:, model:] = (
+        r_ref[0, :, model:] = (
             jnp.where(lane == e, high, 0.0) + jnp.where(lane == e + experts, d_gates - high, 0.0)
         ).astype(BF16)
-        new_gate = mm(x, d_gate, TN)
-        new_up = mm(x, d_up, TN)
+        new_wide = mm(x, d_both, TN)
         new_down = mm((active_wide * w).astype(BF16), d, TN)
 
         @pl.when(step == 0)
         def _():
-            acc_gate[...] = new_gate
-            acc_up[...] = new_up
+            acc_wide[...] = new_wide
             acc_down[...] = new_down
 
         @pl.when(step > 0)
         def _():
-            acc_gate[...] += new_gate
-            acc_up[...] += new_up
+            acc_wide[...] += new_wide
             acc_down[...] += new_down
 
         @pl.when(step == steps - 1)
@@ -1784,44 +1835,68 @@
             for s in range(groups):
                 z = lax.rem(at_ref[0] + s, groups)
                 at_z = pl.ds(pl.multiple_of(z * part, 128), part)
-                outs[2 * s][0] = acc_gate[at_z, :].astype(BF16)
-                outs[2 * s][1] = acc_up[at_z, :].astype(BF16)
-                outs[2 * s + 1][...] = acc_down[:, at_z].astype(BF16)
-
-    def held(shape):
-        return pl.BlockSpec(shape, lambda t: (0,) * len(shape), pipeline_mode=pl.Buffered(1))
-
-    grads = [(2, part, ff), (ff, part)] * groups
-    row_spec = pl.BlockSpec((1, tile, model), lambda t: (k, t, 0))
+                outs[s][0, 0] = acc_wide[at_z, :ff].astype(BF16)
+                outs[s][0, 1] = acc_wide[at_z, ff:].astype(BF16)
+                outs[s][0, 2] = acc_down[:, at_z].T.astype(BF16)
+
+    grad = pl.BlockSpec((1, 3, part, ff), lambda k, t: (k, 0, 0, 0), pipeline_mode=pl.Buffered(1))
+    rows = lambda width: pl.BlockSpec((1, tile, width), lambda k, t: (k, t, 0))
     out = pl.pallas_call(
         kernel,
-        grid=(steps,),
-        in_specs=[SMEM_SPEC, row_spec, row_spec, pl.BlockSpec((1, tile, LANES), lambda t: (k, t, 0))]
-        + [ANY_SPEC] * held_count,
-        out_specs=[
-            pl.BlockSpec((tile, model), lambda t: (t, 0)),
-            pl.BlockSpec((tile, model + LANES), lambda t: (t, 0)),
+        grid=(per, steps),
+        in_specs=[SMEM_SPEC, rows(model), rows(model), rows(LANES)] + [ANY_SPEC] * groups,
+        out_specs=[rows(model), rows(model + LANES)] + [grad] * groups,
+        out_shape=[
+            jax.ShapeDtypeStruct((per, total, model), BF16),
+            jax.ShapeDtypeStruct((per, total, model + LANES), BF16),
         ]
-        + [held(shape) for shape in grads],
-        out_shape=[
-            jax.ShapeDtypeStruct((total, model), BF16),
-            jax.ShapeDtypeStruct((total, model + LANES), BF16),
-        ]
-        + [jax.ShapeDtypeStruct(shape, BF16) for shape in grads],
+        + [jax.ShapeDtypeStruct((per, 3, part, ff), BF16)] * groups,
         scratch_shapes=[
-            pltpu.VMEM((model, ff), F32),
-            pltpu.VMEM((model, ff), F32),
+            pltpu.VMEM((model, 2 * ff), F32),
             pltpu.VMEM((ff, model), F32),
-            pltpu.VMEM((model, ff), BF16),
-            pltpu.VMEM((model, ff), BF16),
-            pltpu.VMEM((ff, model), BF16),
-            pltpu.SemaphoreType.DMA((3 * groups,)),
+            pltpu.VMEM((per, model, 2 * ff), BF16),
+            pltpu.VMEM((per, model, ff), BF16),
+            pltpu.SemaphoreType.DMA((per, 3 * groups)),
         ],
         compiler_params=pltpu.CompilerParams(vmem_limit_bytes=62 * 1024 * 1024),
-        cost_estimate=cost(36 * total * model * ff, 10 * total * model),
-        name="expert_step",
-    )(at, rows_in, grads_in, weights, *own, *[x for pair in far for x in pair])
-    return out[0], out[1], [(out[2 + 2 * s], out[3 + 2 * s]) for s in range(groups)]
+        cost_estimate=cost(18 * per * total * model * ff, 10 * per * total * model),
+        name="expert_steps",
+    )(at, rows_in, grads_in, weights, bank, *far)
+    return out[0], out[1], list(out[2:])
+
+
+def merge_grads(which, at, terms):
+    per, _, part, ff = terms[0].shape
+    split = 2
+    tile = LANES
+
+    def kernel(at_ref, *refs):
+        ins, out = refs[: len(terms)], refs[len(terms)]
+        for k in range(per):
+            for parity in range(split):
+                value = None
+                for one in ins[parity::split]:
+                    more = one[k, 0].astype(F32)
+                    value = more if value is None else value + more
+                index = lax.rem(at_ref[0] + parity, split) * per + k
+                out[index] = value.T if which == 2 else value
+
+    if which == 2:
+        spec = pl.BlockSpec((split * per, ff, tile), lambda t: (0, 0, t))
+        shape = (split * per, ff, part)
+    else:
+        spec = pl.BlockSpec((split * per, tile, ff), lambda t: (0, t, 0))
+        shape = (split * per, part, ff)
+    return pl.pallas_call(
+        kernel,
+        grid=(part // tile,),
+        in_specs=[SMEM_SPEC]
+        + [pl.BlockSpec((per, 1, tile, ff), lambda t: (0, which, t, 0))] * len(terms),
+        out_specs=spec,
+        out_shape=jax.ShapeDtypeStruct(shape, F32),
+        cost_estimate=cost(1e8, 6e6),
+        name="merge_grads",
+    )(at, *terms)
 
 
 def layer_plane(
@@ -1865,32 +1940,29 @@
     )
     cut = lambda x: lax.dynamic_slice_in_dim(x, me * rows_here, rows_here, axis=0)
     shares = [cut(query_key_value_weight), jnp.concatenate([cut(out_weight), cut(misc)], axis=1)]
-    sets = [[x] + [shift(x, s) for s in range(1, groups)] for x in shares]
-    (gate_from, up_from, down_from), sets = lax.optimization_barrier(
-        ((gate_weight, up_weight, down_weight), sets)
+    bank = jnp.stack([gate_weight, up_weight, jnp.swapaxes(down_weight, 1, 2)], axis=1)
+
+    expert_ids = jnp.arange(experts, dtype=jnp.int32)
+    named = jnp.any(routes[..., None] == expert_ids, axis=2)
+    pad = jnp.zeros((micro, count, LANES - experts), BF16)
+    d_payload = jnp.concatenate([cotangent, named.astype(BF16), pad], axis=2)
+    d_turned = turn(d_payload, 1, split)
+
+    qkv_full, rest_full, far_one = plane_weights(shares, bank, per)
+    (bank_late, d_payload, d_turned), qkv_full = lax.optimization_barrier(
+        ((bank, d_payload, d_turned), qkv_full)
     )
-    weights_far = []
-    for k in range(per):
-        far = []
-        for s in range(1, groups):
-            index = ((z + s) % split) * per + k
-            take = lambda x: lax.dynamic_index_in_dim(x, index, 0, keepdims=False)
-            far.append(
-                (shift(jnp.stack([take(gate_from), take(up_from)]), s), shift(take(down_from), s))
-            )
-        weights_far.append(far)
-    qkv_full, rest_full = plane_weights(sets)
+    weights_far = [far_one]
+    for s in range(2, groups):
+        first = ((z + s) % split) * per
+        weights_far.append(shift(lax.dynamic_slice_in_dim(bank_late, first, per, axis=0), s))
+    both = jnp.concatenate([d_payload, d_turned], axis=0)
+    d_slots = lax.all_gather(both, "expert", axis=0)
     out_full, misc_full = rest_full[:, :model], rest_full[:, model:]
     gain_one = misc_full[:, 0].astype(F32)
     gain_two = misc_full[:, 1].astype(F32)
     router_full = misc_full[:, experts : 2 * experts]
 
-    expert_ids = jnp.arange(experts, dtype=jnp.int32)
-    named = jnp.any(routes[..., None] == expert_ids, axis=2)
-    pad = jnp.zeros((micro, count, LANES - experts), BF16)
-    d_payload = jnp.concatenate([cotangent, named.astype(BF16), pad], axis=2)
-    both = jnp.concatenate([d_payload, turn(d_payload, 1, split)], axis=0)
-    d_slots = lax.all_gather(both, "expert", axis=0)
     grads_in, ranks = gather_flags(d_slots, where, per, cap, model)
 
     x = tokens.reshape(rows, model).astype(F32)
@@ -1926,15 +1998,9 @@
     ).reshape(micro, count, model + LANES)
     rows_in, row_weights = plane_dispatch(payload, ranks, where, per, cap, model, experts)
     tile = 2 * micro * split * cap
-    outs, backs, weight_terms = [], [], []
-    for k in range(per):
-        out_rows, back_rows, terms = expert_step(
-            k, where, rows_in, grads_in, row_weights, (gate_weight, up_weight, down_weight),
-            weights_far[k], experts, tile,
-        )
-        outs.append(out_rows)
-        backs.append(back_rows)
-        weight_terms.append(terms)
+    outs, backs, weight_terms = expert_steps(
+        where, rows_in, grads_in, row_weights, bank, weights_far, experts, tile
+    )
     back = plane_return(backs, ranks, micro, count, cap).reshape(rows, model + LANES)
 
     mixture_parts = scatter_rows(outs, ranks, where, n, micro * split, count, cap)
@@ -1942,25 +2008,8 @@
     mixture = mixture_sum[:micro].astype(F32) + turn(mixture_sum[micro:], 1, split).astype(F32)
     block_out = (hidden + mixture.reshape(rows, model)).astype(BF16).reshape(tokens.shape)
 
-    sums = [[None, None] for _ in range(split)]
-    merged = []
-    for k in range(per):
-        sums = [None] * split
-        for s in range(groups):
-            pair, down = weight_terms[k][s]
-            got = [(shift(t, s) if s else t).astype(F32) for t in (pair, down)]
-            c = s % split
-            sums[c] = got if sums[c] is None else [a + b for a, b in zip(sums[c], got)]
-        merged.append(
-            [
-                [lax.select_n((z - p) % split, sums[0][i], sums[1][i]) for i in range(2)]
-                for p in range(split)
-            ]
-        )
-    order = [(p, k) for p in range(split) for k in range(per)]
-    gate_grad = jnp.stack([merged[k][p][0][0] for p, k in order])
-    up_grad = jnp.stack([merged[k][p][0][1] for p, k in order])
-    down_grad = jnp.stack([merged[k][p][1] for p, k in order])
+    terms = weight_terms[:1] + [shift(weight_terms[s], s) for s in range(1, groups)]
+    gate_grad, up_grad, down_grad = [merge_grads(which, where, terms) for which in range(3)]
 
     d_out = cotangent.reshape(rows, model).astype(F32)
     d_gates = back[:, model : model + experts] + back[:, model + experts : model + 2 * experts]
@@ -2024,7 +2073,7 @@
     plane = (
         n == 8
         and exp_here % 2 == 0
-        and groups % 2 == 0
+        and groups == 4
         and part % (16 * n) == 0
         and part % LANES == 0
         and arrays[0].shape[0] == 2

time: 999 us -> 861 us (0.86)
  waiting for transfers between devices: 205 us -> 0.07 us
  Pallas kernels: 557 us -> 670 us
  starting transfers between devices: 94.1 us -> 62.4 us
  other arithmetic: 35.2 us -> 24.5 us
    ppermute x30 -> x5, waiting for transfers between devices: 174 us -> 0.01 us  [shift(): return lax.ppermute(x, 'group', [(i, (i + step) % n) for i in range(n)])]
    pallas_call x4 -> x6, Pallas kernels: 244 us -> 354 us  [the longest x1 172 us: plane_return(): pl.pallas_call(kernel, in_specs=[vmem] * 2, out_specs=vmem, out_shape=jax...]
    ppermute x2, waiting for transfers between devices: 31.1 us -> 0.01 us  [turn(): lax.ppermute(x, 'group', [(i // split * split + (i + step) % split, i) fo...]
    pallas_call x1, Pallas kernels: 36.8 us -> 63 us  [plane_attention(): pl.pallas_call(kernel, in_specs=[vmem, vmem], out_specs=[vmem, vmem], out...]
    pallas_call x1, Pallas kernels: 70.8 us -> 50.3 us  [plane_attention_backward(): pl.pallas_call(kernel, in_specs=[vmem] * 3, out_specs=[vmem] * 2, out_sha...]
    ppermute x2, starting transfers between devices: 20.5 us -> 3.05 us  [turn(): lax.ppermute(x, 'group', [(i // split * split + (i + step) % split, i) fo...]
    ppermute x30 -> x5, starting transfers between devices: 73.6 us -> 59.2 us  [shift(): return lax.ppermute(x, 'group', [(i, (i + step) % n) for i in range(n)])]
  transfers between devices with their start and end apart: 34 -> 9, of which waited for: 9 -> 0; matrix products, arithmetic and copies ran while one was open for 10% -> 10% of each run, Pallas kernels for 56% -> 68%
where the time goes in v2:
time: 861 us; the launch traced here: 852 us
  Pallas kernels  670 us (78%)
  starting transfers between devices  62.4 us (7%)
  local copies, waits for them, and re-layouts  50.7 us (6%)
  matrix products  29.3 us (3%)
  other arithmetic  24.5 us (3%)
  between operations  15.3 us (2%)
    pallas_call x1, Pallas kernels, plane_return(): pl.pallas_call(kernel, in_specs=[vmem] * 2, out_specs=vmem, out_shape=jax...  172 us
    pallas_call x1, Pallas kernels, plane_gradients(): pl.pallas_call(kernel, in_specs=[vmem] * (len(flat) + 1), out_specs=vmem,...  105 us
    pallas_call x1, Pallas kernels, plane_weights(): pl.pallas_call(kernel, in_specs=[vmem] * kinds + [ANY_SPEC], out_specs=[v...  95.7 us
    pallas_call x1, Pallas kernels, expert_steps(): pl.pallas_call(kernel, grid=(per, steps), in_specs=[SMEM_SPEC, rows(model...  72.2 us
    pallas_call x1, Pallas kernels, plane_dispatch(): pl.pallas_call(kernel, in_specs=[SMEM_SPEC, vmem, vmem], out_specs=[vmem,...  68.7 us
    pallas_call x1, Pallas kernels, plane_attention(): pl.pallas_call(kernel, in_specs=[vmem, vmem], out_specs=[vmem, vmem], out...  63 us
    ppermute x5, starting transfers between devices, shift(): return lax.ppermute(x, 'group', [(i, (i + step) % n) for i in range(n)])  59.2 us
    pallas_call x1, Pallas kernels, plane_attention_backward(): pl.pallas_call(kernel, in_specs=[vmem] * 3, out_specs=[vmem] * 2, out_sha...  50.3 us
  transfers between devices with their start and end apart: 9, of which 0 were waited for; matrix products, arithmetic and copies ran while one was open for 10% of the time, Pallas kernels for 68%

profile of v2, /device:TPU:0, one launch (start us, length us, event | category | flops | bytes accessed | tf_op | source)
XLA Modules:
  0.0 852.3 jit_solution(5563876686626254891)
XLA Ops:
  8.3 2.0 concatenate.56
  10.3 3.1 collective-permute-start
  17.3 3.8 pad_maximum_fusion.refs_2_.refs_0_
  21.9 95.7 %plane_weights.1 = (bf16[1536,2560]{1,0:T(8,128)(2,1)}, bf16[1536,1664]{1,0:T(8,128)(2,1)}, bf16[2,3,384,512]{3,2,1,0:T(8,128)(2,1)}) custom-call(bf16[48,2560]{1,0:T(8,128)(2,1)} %constant_dynamic-slice_fusion.4.refs_0_, bf16[48,1664]{1,0:T(8,128)(2,1)} %pad_maximum_fusion.4.refs_1_, bf16[4,3,384,512]{3,2,1,0:T(8,128)(2,1)} %pad_maximum_fusion.refs_2_.refs_0_), custom_call_target="tpu_custom_call" | custom-call | flops 1000000000 | bytes 1000000 | tf_op jit(solution)/shard_map/plane_weights/pallas_call | solution.py:1223
  117.6 2.8 pad_maximum_fusion.1
  125.6 2.9 copy.64
  128.5 3.0 copy.65
  134.5 5.7 fusion.66
  144.8 2.5 constant_dynamic-slice_fusion
  148.9 19.4 %collective-permute-start.2 = (bf16[2,3,384,512]{3,2,1,0:T(8,128)(2,1)}, bf16[2,3,384,512]{3,2,1,0:T(8,128)(2,1)}, u32[]{:S(2)}, u32[]{:S(2)}) collective-permute-start(bf16[2,3,384,512]{3,2,1,0:T(8,128)(2,1)} %get-tuple-element.107), channel_id=1, source_target_pairs={{0,24},{8,0},{16,8},{24,16},{1,25},{9,1},{17,9},{25,17},{2,26},{10... | collective-permute-start | bytes 7077896 | tf_op jit(solution)/shard_map/ppermute | solution.py:39
  169.1 63.0 %plane_attention.1 = (bf16[2,128,1536]{2,1,0:T(8,128)(2,1)}, bf16[8,2,128,1024]{3,2,1,0:T(8,128)(2,1)}) custom-call(bf16[2,128,1536]{2,1,0:T(8,128)(2,1)} %bitcast.108, bf16[2,128,1024]{2,1,0:T(8,128)(2,1)} %bitcast.121), custom_call_target="tpu_custom_call" | custom-call | flops 1000000000 | bytes 1000000 | tf_op jit(solution)/shard_map/plane_attention/pallas_call | solution.py:1317
  232.1 4.5 multiply_reduce_fusion.2
  240.2 15.2 %gather_flags.1 = (bf16[2,1536,1536]{2,1,0:T(8,128)(2,1)}, f32[32,2,128]{2,1,0:T(2,128)}) custom-call(s32[4]{0:T(128)} %pad_add_fusion.at_ref, bf16[8,4,128,1664]{3,2,1,0:T(8,128)(2,1)} %bitcast.123), custom_call_target="tpu_custom_call" | custom-call | flops 5000000000 | bytes 30000000 | tf_op jit(solution)/shard_map/gather_flags/pallas_call | solution.py:1701
  255.3 68.7 %plane_dispatch.1 = (bf16[2,1536,1536]{2,1,0:T(8,128)(2,1)}, f32[2,1536,128]{2,1,0:T(8,128)}) custom-call(s32[4]{0:T(128)} %pad_add_fusion.at_ref, bf16[2,128,1664]{2,1,0:T(8,128)(2,1)} %bitcast.116, f32[32,2,128]{2,1,0:T(2,128)} %get-tuple-element.41.rank_ref), custom_call_target="tpu_custom_call" | custom-call | flops 1000000000 | bytes 1000000 | tf_op jit(solution)/shard_map/plane_dispatch/pallas_call | solution.py:1481
  324.1 72.2 %expert_steps.1 = (bf16[2,1536,1536]{2,1,0:T(8,128)(2,1)}, bf16[2,1536,1664]{2,1,0:T(8,128)(2,1)}, bf16[2,3,384,512]{3,2,1,0:T(8,128)(2,1)}, bf16[2,3,384,512]{3...) custom-call(s32[4]{0:T(128)} %pad_add_fusion.at_ref, ...), custom_call_target="tpu_custom_call" | custom-call | flops 43486543872 | bytes 47185920 | tf_op jit(solution)/shard_map/expert_steps/pallas_call | solution.py:1844
  396.3 14.1 %scatter_rows.1 = bf16[8,4,128,1536]{3,2,1,0:T(8,128)(2,1)} custom-call(s32[4]{0:T(128)} %pad_add_fusion.at_ref, f32[32,2,128]{2,1,0:T(2,128)} %get-tuple-element.41.rank_ref, bf16[2,1536,1536]{2,1,0:T(8,128)(2,1)} %get-tuple-element.47.in_ref), custom_call_target="tpu_custom_call" | custom-call | flops 5000000000 | bytes 30000000 | tf_op jit(solution)/shard_map/scatter_rows/pallas_call | solution.py:1740
  412.2 36.9 %collective-permute-start.5 = (bf16[2,3,384,512]{3,2,1,0:T(8,128)(2,1)}, bf16[2,3,384,512]{3,2,1,0:T(8,128)(2,1)}, u32[]{:S(2)}, u32[]{:S(2)}) collective-permute-start(bf16[2,3,384,512]{3,2,1,0:T(8,128)(2,1)} %get-tuple-element.54), channel_id=1, source_target_pairs={{0,16},{8,24},{16,0},{24,8},{1,17},{9,25},{17,1},{25,9},{2,18},{10... | collective-permute-start | bytes 7077896 | tf_op jit(solution)/shard_map/ppermute | solution.py:39
  449.1 172.2 %plane_return.1 = f32[2,128,1664]{2,1,0:T(8,128)} custom-call(f32[32,2,128]{2,1,0:T(2,128)} %get-tuple-element.41.rank_ref, bf16[2,1536,1664]{2,1,0:T(8,128)(2,1)} %get-tuple-element.48.in_ref), custom_call_target="tpu_custom_call" | custom-call | flops 1000000000 | bytes 1000000 | tf_op jit(solution)/shard_map/plane_return/pallas_call | solution.py:1559
  622.5 3.0 multiply_reduce_fusion
  627.3 4.9 fusion.7
  632.3 50.3 %plane_attention_backward.1 = (f32[2,128,1536]{2,1,0:T(8,128)}, f32[2,128,1024]{2,1,0:T(8,128)}) custom-call(bf16[2,128,1536]{2,1,0:T(8,128)(2,1)} %bitcast.109, bf16[2,128,1536]{2,1,0:T(8,128)(2,1)} %bitcast.118, bf16[8,2,128,1024]{3,2,1,0:T(8,128)(2,1)} %get-tuple-element.49.kv_ref), custom_call_target="tpu_custom_call" | custom-call | flops 1000000000 | bytes 1000000 | tf_op jit(solution)/shard_map/plane_attention_backward/pallas_call | solution.py:1409
  689.9 7.3 fusion.19
  698.3 2.1 fusion.65
  701.4 3.7 concatenate.69.refs_4_
  705.1 2.1 slice_bitcast_fusion
  708.4 104.8 %plane_gradients.1 = f32[384,4224]{1,0:T(8,128)} custom-call(bf16[256,1536]{1,0:T(8,128)(2,1)} %bitcast.120, bf16[256,1536]{1,0:T(8,128)(2,1)} %copy-done.22, bf16[256,1536]{1,0:T(8,128)(2,1)} %copy-done.21, bf16[256,2560]{1,0:T(8,128)(2,1)} %pad_maximum_fusion.2.refs_3_, f32[1536,128]{1,0:T(8,128)} %concatenate.69.refs_4_), custom_call_target="tpu_custom_call" | custom-call | flops 1000000000 | bytes 1000000 | tf_op jit(solution)/shard_map/plane_gradients/pallas_call | solution.py:1657
  813.2 4.3 slice.177
  817.5 3.2 slice.178
  824.9 4.8 merge_grads.5
  829.8 4.4 merge_grads.4
  834.2 4.6 merge_grads.3
  841.0 4.1 fusion.26
  (167 shorter events, 45.8 us)
Async XLA Ops:
  7.2 14.0 %copy-start = (bf16[384,2560]{1,0:T(8,128)(2,1)S(1)}, bf16[384,2560]{1,0:T(8,128)(2,1)}, u32[]{:S(2)}) copy-start(bf16[384,2560]{1,0:T(8,128)(2,1)} %param.15) | copy-start | bytes 5898244
  7.2 6.1 copy-start.34
  7.2 6.3 copy-start.35
  7.2 6.4 copy-start.28
  7.2 232.9 %all-gather.3.cloned.1.call-start = ((), (), s32[]{:S(2)}) async-start(), calls=%async_computation.2 | async-start | bytes 15335424 | tf_op jit(solution)/shard_map/all_gather | solution.py:1960
  10.3 107.3 %collective-permute-start = (bf16[2,128,1664]{2,1,0:T(8,128)(2,1)}, bf16[2,128,1664]{2,1,0:T(8,128)(2,1)}, u32[]{:S(2)}, u32[]{:S(2)}) collective-permute-start(bf16[2,128,1664]{2,1,0:T(8,128)(2,1)} %concatenate.56), channel_id=1, source_target_pairs={{8,0},{0,8},{24,16},{16,24},{9,1},{1,9},{25,17},{17,25},{10,2},{2,... | collective-permute-start | bytes 2555912 | tf_op jit(solution)/shard_map/ppermute | solution.py:44
  120.4 584.7 %reduce-scatter.2.cloned.1.call-start = ((), (), s32[]{:S(2)}) async-start(), calls=%async_computation.1 | async-start | bytes 14155776 | tf_op jit(solution)/shard_map/reduce_scatter | solution.py:2007
  128.5 5.2 copy-start.11
  134.5 5.7 copy-start.21
  140.4 2.2 copy-start.6
  141.1 3.6 slice-start
  147.3 176.8 %collective-permute-start.1 = (bf16[2,3,384,512]{3,2,1,0:T(8,128)(2,1)}, bf16[2,3,384,512]{3,2,1,0:T(8,128)(2,1)}, u32[]{:S(2)}, u32[]{:S(2)}) collective-permute-start(bf16[2,3,384,512]{3,2,1,0:T(8,128)(2,1)} %get-tuple-element.108), channel_id=1, source_target_pairs={{0,16},{8,24},{16,0},{24,8},{1,17},{9,25},{17,1},{25,9},{2,18},{10... | collective-permute-start | bytes 7077896 | tf_op jit(solution)/shard_map/ppermute | solution.py:39
  148.9 175.2 %collective-permute-start.2 = (bf16[2,3,384,512]{3,2,1,0:T(8,128)(2,1)}, bf16[2,3,384,512]{3,2,1,0:T(8,128)(2,1)}, u32[]{:S(2)}, u32[]{:S(2)}) collective-permute-start(bf16[2,3,384,512]{3,2,1,0:T(8,128)(2,1)} %get-tuple-element.107), channel_id=1, source_target_pairs={{0,24},{8,0},{16,8},{24,16},{1,25},{9,1},{17,9},{25,17},{2,26},{10... | collective-permute-start | bytes 7077896 | tf_op jit(solution)/shard_map/ppermute | solution.py:39
  236.6 389.0 %copy-start.2 = (f32[256,1536]{1,0:T(8,128)}, f32[256,1536]{1,0:T(8,128)S(1)}, u32[]{:S(2)}) copy-start(f32[256,1536]{1,0:T(8,128)S(1)} %get-tuple-element.127) | copy-start | bytes 4718596
  236.6 389.0 %copy-start.26 = (f32[256]{0:T(256)}, f32[256]{0:T(256)S(1)}, u32[]{:S(2)}) copy-start(f32[256]{0:T(256)S(1)} %add_rsqrt_fusion) | copy-start | bytes 3076
  236.8 3.3 copy-start.14
  410.9 414.0 %collective-permute-start.4 = (bf16[2,3,384,512]{3,2,1,0:T(8,128)(2,1)}, bf16[2,3,384,512]{3,2,1,0:T(8,128)(2,1)}, u32[]{:S(2)}, u32[]{:S(2)}) collective-permute-start(bf16[2,3,384,512]{3,2,1,0:T(8,128)(2,1)} %get-tuple-element.53), channel_id=1, source_target_pairs={{0,8},{8,16},{16,24},{24,0},{1,9},{9,17},{17,25},{25,1},{2,10},{10... | collective-permute-start | bytes 7077896 | tf_op jit(solution)/shard_map/ppermute | solution.py:39
  412.2 412.7 %collective-permute-start.5 = (bf16[2,3,384,512]{3,2,1,0:T(8,128)(2,1)}, bf16[2,3,384,512]{3,2,1,0:T(8,128)(2,1)}, u32[]{:S(2)}, u32[]{:S(2)}) collective-permute-start(bf16[2,3,384,512]{3,2,1,0:T(8,128)(2,1)} %get-tuple-element.54), channel_id=1, source_target_pairs={{0,16},{8,24},{16,0},{24,8},{1,17},{9,25},{17,1},{25,9},{2,18},{10... | collective-permute-start | bytes 7077896 | tf_op jit(solution)/shard_map/ppermute | solution.py:39
  449.1 375.8 %collective-permute-start.6 = (bf16[2,3,384,512]{3,2,1,0:T(8,128)(2,1)}, bf16[2,3,384,512]{3,2,1,0:T(8,128)(2,1)}, u32[]{:S(2)}, u32[]{:S(2)}) collective-permute-start(bf16[2,3,384,512]{3,2,1,0:T(8,128)(2,1)} %get-tuple-element.55), channel_id=1, source_target_pairs={{0,24},{8,0},{16,8},{24,16},{1,25},{9,1},{17,9},{25,17},{2,26},{10... | collective-permute-start | bytes 7077896 | tf_op jit(solution)/shard_map/ppermute | solution.py:39
  622.5 3.1 copy-start.32
  622.5 4.2 copy-start.16
  627.3 4.9 copy-start.22
  682.6 2.3 copy-start.18
  682.6 2.5 copy-start.8
  685.2 2.2 copy-start.7
  688.7 8.5 copy-start.24
  707.2 131.6 %collective-permute-start.3 = (bf16[2,128,1536]{2,1,0:T(8,128)(2,1)}, bf16[2,128,1536]{2,1,0:T(8,128)(2,1)}, u32[]{:S(2)}, u32[]{:S(2)}) collective-permute-start(bf16[2,128,1536]{2,1,0:T(8,128)(2,1)} %slice_bitcast_fusion), channel_id=1, source_target_pairs={{8,0},{0,8},{24,16},{16,24},{9,1},{1,9},{25,17},{17,25},{10,2},{2,... | collective-permute-start | bytes 2359304 | tf_op jit(solution)/shard_map/ppermute | solution.py:44
  817.5 6.9 copy-start.36
  834.2 4.7 copy-start.23
  834.2 6.2 copy-start.13
  834.2 6.2 copy-start.17
  841.0 4.1 copy-start.1
  (17 other events, 26.2 us)
Sparse Core Ops, SparseCore 0:
  120.5 114.9 all-gather.2
  410.5 163.2 reduce-scatter.1

commit v3 on v2

--- a/solution.py
+++ b/solution.py
@@ -1291,38 +1291,69 @@
     return prompt_ok, cont_ok
 
 
-def plane_attention(query, key_value):
-    micro, tokens, width = key_value.shape
-    n = 8
-
-    def kernel(q_ref, kv_ref, out_ref, slots, keys, send, recv, local):
+def turn_heads(x, cosine, sine):
+    half = HEAD_SIZE // 2
+    lane = lax.broadcasted_iota(jnp.int32, cosine.shape, 1)
+    first = lax.rem(lane, HEAD_SIZE) < half
+    blocks = []
+    for lo in range(0, x.shape[1], LANES):
+        one = x[:, lo : lo + LANES]
+        other = jnp.where(first, pltpu.roll(one, LANES - half, 1), pltpu.roll(one, half, 1))
+        blocks.append(one * cosine + other * sine)
+    return jnp.concatenate(blocks, axis=1)
+
+
+def plane_attention(normed, weight, cosine, sine, micro):
+    rows, model = normed.shape
+    tokens = rows // micro
+    width = 2 * KEY_VALUE_HEADS * HEAD_SIZE
+    query_width = QUERY_HEADS * HEAD_SIZE
+    n, tile = 8, 512
+
+    def kernel(x_ref, w_ref, cos_ref, sin_ref, out_ref, q_ref, slots, own, keys, send, recv, local):
         e = lax.axis_index("expert")
         gather = Gather(
-            e, lambda c: kv_ref.at[c], lambda r, q, c: slots.at[q, c], [c % 2 for c in range(micro)],
+            e, lambda c: own.at[c], lambda r, q, c: slots.at[q, c], [c % 2 for c in range(micro)],
             send, recv,
         )
+
+        def project(lo, turned):
+            wide = mm(x_ref[...], w_ref[:, lo : lo + tile])
+            for c in range(micro):
+                part = wide[c * tokens : (c + 1) * tokens]
+                if turned:
+                    part = turn_heads(part, cos_ref[...], sin_ref[...])
+                yield c, part.astype(BF16)
+
+        for lo in range(0, width, tile):
+            for c, part in project(query_width + lo, lo < width // 2):
+                own[c, :, lo : lo + tile] = part
         greet(plane_devices(e))
         for c in range(micro):
             gather.begin(c)
-            pltpu.make_async_copy(kv_ref.at[c], slots.at[0, c], local.at[c]).start()
-        gather.forward_all(range(micro))
+            pltpu.make_async_copy(own.at[c], slots.at[0, c], local.at[c]).start()
+        for lo in range(0, query_width, tile):
+            for c, part in project(lo, True):
+                q_ref[c, :, lo : lo + tile] = part
+        gather.stage(range(micro), (2, 4))
+        gather.stage(range(micro), (6,))
         for c in range(micro):
-            pltpu.make_async_copy(kv_ref.at[c], slots.at[0, c], local.at[c]).wait()
+            gather.stage([c], (1, 3, 5, 7))
+            pltpu.make_async_copy(own.at[c], slots.at[0, c], local.at[c]).wait()
             load_keys(n, [slots.at[r, c] for r in range(n)], keys)
             attention_pairs(n, e, q_ref.at[c], keys, out_ref.at[c])
         for c in range(micro):
             gather.finish(c)
 
     vmem = pl.BlockSpec(memory_space=pltpu.VMEM)
+    shape = jax.ShapeDtypeStruct((micro, tokens, query_width), BF16)
     return pl.pallas_call(
         kernel,
-        in_specs=[vmem, vmem],
-        out_specs=[vmem, vmem],
-        out_shape=[
-            jax.ShapeDtypeStruct(query.shape, BF16),
-            jax.ShapeDtypeStruct((n, micro, tokens, width), BF16),
-        ],
+        in_specs=[vmem] * 4,
+        out_specs=[vmem] * 3,
+        out_shape=[shape, shape, jax.ShapeDtypeStruct((n, micro, tokens, width), BF16)],
         scratch_shapes=[
+            pltpu.VMEM((micro, tokens, width), BF16),
             pltpu.VMEM((n * PR_DEV + CONT, width), BF16),
             pltpu.SemaphoreType.DMA((n, micro)),
             pltpu.SemaphoreType.DMA((n, micro)),
@@ -1331,16 +1362,17 @@
         compiler_params=params(2),
         cost_estimate=cost(1e9, 1e6),
         name="plane_attention",
-    )(query, key_value)
-
-
-def plane_attention_backward(query, slots, d_mixed):
+    )(normed, weight, cosine, sine)
+
+
+def plane_attention_backward(query, slots, d_mixed, cosine, sine):
     n, micro, tokens, width = slots.shape
     half = width // 2
+    query_width = query.shape[2]
     pr = n * PR_DEV
     total = pr + CONT
 
-    def kernel(q_ref, d_ref, kv_ref, dq_ref, dkv_ref, keys, grads, parts, *scratch):
+    def kernel(q_ref, d_ref, kv_ref, cos_ref, sin_ref, out_ref, keys, grads, parts, *scratch):
         e = lax.axis_index("expert")
         red = Reduce(e, lambda r, c: parts.at[r, c], [c % 2 for c in range(micro)], *scratch)
         greet(plane_devices(e))
@@ -1382,8 +1414,12 @@
                     dq_lows.append(row_heads(dq_low))
                     dks.append(jnp.concatenate([dk_low[:pr] + dk_top, dk_low[pr:]], axis=0))
                     dvs.append(jnp.concatenate([dv_low[:pr] + dv_top, dv_low[pr:]], axis=0))
-                dq_ref[c, :PR_DEV, q_at] = jnp.concatenate(dq_tops, axis=1)
-                dq_ref[c, PR_DEV:, q_at] = jnp.concatenate(dq_lows, axis=1)
+                for lo, found in ((0, dq_tops), (PR_DEV, dq_lows)):
+                    there = slice(lo, lo + PR_DEV)
+                    turned = turn_heads(
+                        jnp.concatenate(found, axis=1), cos_ref[there, :], sin_ref[there, :]
+                    )
+                    out_ref[c, there, q_at] = turned.astype(BF16)
                 grads[:, k_at] = jnp.concatenate(dks, axis=1).astype(BF16)
                 grads[:, v_at] = jnp.concatenate(dvs, axis=1).astype(BF16)
                 return carry
@@ -1400,20 +1436,30 @@
                     red.begin(r, c)
         red.diagonal(range(micro))
         red.sides(range(micro))
+        step = 16
         for c in range(micro):
-            add_rows(dkv_ref.at[c], red.total(c))
+            terms = red.total(c)
+
+            def last(i, carry):
+                at = pl.ds(pl.multiple_of(i * step, step), step)
+                total = terms[0][at, :].astype(F32)
+                for term in terms[1:]:
+                    total = total + term[at, :].astype(F32)
+                turned = turn_heads(total[:, :half], cos_ref[at, :], sin_ref[at, :])
+                out_ref[c, at, query_width : query_width + half] = turned.astype(BF16)
+                out_ref[c, at, query_width + half :] = total[:, half:].astype(BF16)
+                return carry
+
+            lax.fori_loop(0, tokens // step, last, 0)
         for c in range(micro):
             red.finish(c)
 
     vmem = pl.BlockSpec(memory_space=pltpu.VMEM)
     return pl.pallas_call(
         kernel,
-        in_specs=[vmem] * 3,
-        out_specs=[vmem] * 2,
-        out_shape=[
-            jax.ShapeDtypeStruct(query.shape, F32),
-            jax.ShapeDtypeStruct((micro, tokens, width), F32),
-        ],
+        in_specs=[vmem] * 5,
+        out_specs=vmem,
+        out_shape=jax.ShapeDtypeStruct((micro, tokens, query_width + width), BF16),
         scratch_shapes=[
             pltpu.VMEM((total, width), BF16),
             pltpu.VMEM((total, width), BF16),
@@ -1423,15 +1469,19 @@
         compiler_params=params(3),
         cost_estimate=cost(1e9, 1e6),
         name="plane_attention_backward",
-    )(query, d_mixed, slots)
-
-
-def plane_dispatch(payload, ranks, where, per, cap, model, experts):
+    )(query, d_mixed, slots, cosine, sine)
+
+
+def plane_dispatch(payload, ranks, bank, where, per, cap, model, experts):
     micro, tokens, width = payload.shape
     n, split = 8, 2
+    groups = lax.axis_size("group")
     count = split * micro
 
-    def kernel(at_ref, own_ref, rank_ref, out, weights, slots, z_send, z_recv, send, recv):
+    def kernel(
+        at_ref, own_ref, rank_ref, bank_ref, out, weights, far_ref,
+        slots, z_send, z_recv, send, recv, b_send, b_recv,
+    ):
         e, z = lax.axis_index("expert"), lax.axis_index("group")
         lane = lax.broadcasted_iota(jnp.int32, (cap, LANES), 1)
 
@@ -1459,9 +1509,16 @@
                 total = jnp.sum(jnp.where(mine, got[:, model:], 0.0), axis=1, keepdims=True)
                 weights[k, b * cap : (b + 1) * cap, :] = jnp.broadcast_to(total, (cap, LANES))
 
-        greet(plane_devices(e) + [{"group": partner(z)}])
+        last = groups - 1
+        first = lax.rem(z + last, split) * per
+        follow = remote(
+            bank_ref.at[pl.ds(first, per)], far_ref, b_send, b_recv,
+            {"group": lax.rem(z + last, groups)},
+        )
+        greet(plane_devices(e) + [{"group": lax.rem(z + s, groups)} for s in (1, last)])
         for m in range(micro):
             turned(m).start()
+        follow.start()
         for m in range(micro):
             gather.begin(m)
         for m in range(micro):
@@ -1475,16 +1532,18 @@
             turned(m).wait_send()
         for c in range(count):
             gather.finish(c)
+        follow.wait()
 
     vmem = pl.BlockSpec(memory_space=pltpu.VMEM)
     total = n * count * cap
     return pl.pallas_call(
         kernel,
-        in_specs=[SMEM_SPEC, vmem, vmem],
-        out_specs=[vmem, vmem],
+        in_specs=[SMEM_SPEC, vmem, vmem, ANY_SPEC],
+        out_specs=[vmem, vmem, ANY_SPEC],
         out_shape=[
             jax.ShapeDtypeStruct((per, total, model), BF16),
             jax.ShapeDtypeStruct((per, total, LANES), F32),
+            jax.ShapeDtypeStruct((per,) + bank.shape[1:], BF16),
         ],
         scratch_shapes=[
             pltpu.VMEM((n, count, tokens, width), BF16),
@@ -1492,21 +1551,24 @@
             pltpu.SemaphoreType.DMA((micro,)),
             pltpu.SemaphoreType.DMA((n, count)),
             pltpu.SemaphoreType.DMA((n, count)),
+            pltpu.SemaphoreType.DMA,
+            pltpu.SemaphoreType.DMA,
         ],
         compiler_params=params(4),
         cost_estimate=cost(1e9, 1e6),
         name="plane_dispatch",
-    )(where, payload, ranks)
-
-
-def plane_return(rows, ranks, micro, tokens, cap):
+    )(where, payload, ranks, bank)
+
+
+def plane_return(rows, ranks, term, micro, tokens, cap):
     per, _, width = rows.shape
     n, split = 8, 2
+    groups = lax.axis_size("group")
     count = split * micro
     chunks = list(range(micro, count)) + list(range(micro))
 
-    def kernel(rank_ref, in_ref, out, *refs):
-        parts, z_out, z_in, z_send, z_recv, scratch = *refs[:5], refs[5:]
+    def kernel(rank_ref, in_ref, term_ref, out, far_ref, *refs):
+        parts, z_out, z_in, z_send, z_recv, t_send, t_recv, scratch = *refs[:7], refs[7:]
         e, z = lax.axis_index("expert"), lax.axis_index("group")
         red = Reduce(e, lambda r, c: parts.at[r, c], [c % 2 for c in range(count)], *scratch)
 
@@ -1525,7 +1587,9 @@
                 z_out.at[m], z_in.at[m], z_send.at[m], z_recv.at[m], {"group": partner(z)}
             )
 
-        greet(plane_devices(e) + [{"group": partner(z)}])
+        follow = remote(term_ref, far_ref, t_send, t_recv, {"group": lax.rem(z + 1, groups)})
+        greet(plane_devices(e) + [{"group": lax.rem(z + s, groups)} for s in (1, groups - 1)])
+        follow.start()
         for r in (7, 3, 5):
             for c in chunks:
                 produce(r, c)
@@ -1554,46 +1618,58 @@
             turned(m).wait_send()
         for c in chunks:
             red.finish(c)
+        follow.wait()
 
     vmem = pl.BlockSpec(memory_space=pltpu.VMEM)
     return pl.pallas_call(
         kernel,
-        in_specs=[vmem] * 2,
-        out_specs=vmem,
-        out_shape=jax.ShapeDtypeStruct((micro, tokens, width), F32),
+        in_specs=[vmem, vmem, ANY_SPEC],
+        out_specs=[vmem, ANY_SPEC],
+        out_shape=[
+            jax.ShapeDtypeStruct((micro, tokens, width), F32),
+            jax.ShapeDtypeStruct(term.shape, BF16),
+        ],
         scratch_shapes=[
             pltpu.VMEM((n, count, tokens, width), BF16),
             pltpu.VMEM((micro, tokens, width), BF16),
             pltpu.VMEM((micro, tokens, width), BF16),
             pltpu.SemaphoreType.DMA((micro,)),
             pltpu.SemaphoreType.DMA((micro,)),
+            pltpu.SemaphoreType.DMA,
+            pltpu.SemaphoreType.DMA,
         ]
         + reduce_scratch(count, tokens, width),
         compiler_params=params(5),
         cost_estimate=cost(1e9, 1e6),
         name="plane_return",
-    )(ranks, rows)
-
-
-def plane_gradients(products, extra, groups):
+    )(ranks, rows, term)
+
+
+def plane_gradients(products, router, gains, term, groups):
     n = 8
     depth = products[0][0].shape[1]
     widths = [b.shape[1] for a, b in products]
-    width = sum(widths) + extra.shape[1]
+    width = sum(widths) + LANES
+    experts = router.shape[1]
     rows = depth // (groups * n)
     tile = 512
     flat = [x for pair in products for x in pair]
 
     def kernel(*refs):
-        ins, extra_ref, refs = refs[: len(flat)], refs[len(flat)], refs[len(flat) + 1 :]
-        out, wide, parts, z_out, z_in, slots, z_send, z_recv, send, recv, local = refs[:11]
-        scratch = refs[11:]
+        ins, refs = refs[: len(flat)], refs[len(flat) :]
+        router_ref, gains_ref, term_ref, out, far_ref, *refs = refs
+        wide, parts, z_out, z_in, z_send, z_recv, send, recv, t_send, t_recv = refs[:10]
+        scratch = refs[10:]
         e, z = lax.axis_index("expert"), lax.axis_index("group")
         red = Reduce(e, lambda r, c: parts.at[r, c], [c % 2 for c in range(groups)], *scratch)
         greet(
             plane_devices(e)
             + [{"group": lax.rem(z + s, groups)} for s in range(1, groups)]
         )
+        follow = remote(
+            term_ref, far_ref, t_send, t_recv, {"group": lax.rem(z + groups - 1, groups)}
+        )
+        follow.start()
 
         def cut(lo, size):
             for r in range(n):
@@ -1609,8 +1685,10 @@
                 wide[:, :size] = mm(ins[2 * i][...], ins[2 * i + 1][:, start : start + size], TN)
                 cut(lo, size)
                 lo += size
-        wide[:, : extra_ref.shape[1]] = extra_ref[...]
-        cut(lo, extra_ref.shape[1])
+        wide[:, :LANES] = jnp.zeros((depth, LANES), F32)
+        wide[:, experts : 2 * experts] = router_ref[...]
+        wide[:, : gains.shape[0]] = gains_ref[...].T
+        cut(lo, LANES)
 
         chunks = list(range(1, groups)) + [0]
         for r in (7, 3, 5, 1):
@@ -1631,23 +1709,24 @@
                 far(c).start()
         for c in range(1, groups):
             far(c).wait_recv()
-        add_rows(slots.at[0], [z_out.at[0]] + [z_in.at[c] for c in range(1, groups)])
-
+        def place(r):
+            return out.at[pl.ds(pl.multiple_of(flip(e, r) * rows, 16), rows), :]
+
+        add_rows(place(0), [z_out.at[0]] + [z_in.at[c] for c in range(1, groups)])
         middle = width // 2 // LANES * LANES
         spans = [(0, middle), (middle, width)]
 
         def loc(r, q, c):
-            return slots.at[q, :, spans[c][0] : spans[c][1]]
+            row = pl.multiple_of(flip(e, r) * rows, 16)
+            return out.at[pl.ds(row, rows), spans[c][0] : spans[c][1]]
 
         gather = Gather(e, lambda c: loc(0, 0, c), loc, [0, 1], send, recv)
         for c in range(2):
             gather.begin(c)
         gather.forward_all(range(2))
-        for r in range(n):
-            row = pl.multiple_of(flip(e, r) * rows, 16)
-            out[pl.ds(row, rows), :] = slots[r].astype(F32)
         for c in range(2):
             gather.finish(c)
+        follow.wait()
         for c in range(1, groups):
             far(c).wait_send()
         for c in chunks:
@@ -1656,26 +1735,29 @@
     vmem = pl.BlockSpec(memory_space=pltpu.VMEM)
     return pl.pallas_call(
         kernel,
-        in_specs=[vmem] * (len(flat) + 1),
-        out_specs=vmem,
-        out_shape=jax.ShapeDtypeStruct((n * rows, width), F32),
+        in_specs=[vmem] * (len(flat) + 2) + [ANY_SPEC],
+        out_specs=[vmem, ANY_SPEC],
+        out_shape=[
+            jax.ShapeDtypeStruct((n * rows, width), BF16),
+            jax.ShapeDtypeStruct(term.shape, BF16),
+        ],
         scratch_shapes=[
             pltpu.VMEM((depth, tile), F32),
             pltpu.VMEM((n, groups, rows, width), BF16),
             pltpu.VMEM((groups, rows, width), BF16),
             pltpu.VMEM((groups, rows, width), BF16),
-            pltpu.VMEM((n, rows, width), BF16),
             pltpu.SemaphoreType.DMA((groups,)),
             pltpu.SemaphoreType.DMA((groups,)),
             pltpu.SemaphoreType.DMA((n, 2)),
             pltpu.SemaphoreType.DMA((n, 2)),
-            pltpu.SemaphoreType.DMA((2,)),
+            pltpu.SemaphoreType.DMA,
+            pltpu.SemaphoreType.DMA,
         ]
         + reduce_scratch(groups, rows, width),
         compiler_params=params(6),
         cost_estimate=cost(1e9, 1e6),
         name="plane_gradients",
-    )(*flat, extra)
+    )(*flat, router, gains, term)
 
 
 def gather_flags(slots, where, per, cap, model):
@@ -1948,14 +2030,12 @@
     d_payload = jnp.concatenate([cotangent, named.astype(BF16), pad], axis=2)
     d_turned = turn(d_payload, 1, split)
 
+    bank_two = lax.dynamic_slice_in_dim(bank, (z % split) * per, per, axis=0)
     qkv_full, rest_full, far_one = plane_weights(shares, bank, per)
-    (bank_late, d_payload, d_turned), qkv_full = lax.optimization_barrier(
-        ((bank, d_payload, d_turned), qkv_full)
+    (bank_two, d_payload, d_turned), qkv_full = lax.optimization_barrier(
+        ((bank_two, d_payload, d_turned), qkv_full)
     )
-    weights_far = [far_one]
-    for s in range(2, groups):
-        first = ((z + s) % split) * per
-        weights_far.append(shift(lax.dynamic_slice_in_dim(bank_late, first, per, axis=0), s))
+    far_two = shift(bank_two, 2)
     both = jnp.concatenate([d_payload, d_turned], axis=0)
     d_slots = lax.all_gather(both, "expert", axis=0)
     out_full, misc_full = rest_full[:, :model], rest_full[:, model:]
@@ -1969,17 +2049,9 @@
     inverse_one = lax.rsqrt(jnp.mean(x * x, axis=-1, keepdims=True) + 1e-05)
     normed = (x * inverse_one * gain_one).astype(BF16)
     cosine, sine = rope_tables(me, PR_DEV * n)
-    heads_rope = QUERY_HEADS + KEY_VALUE_HEADS
-    cosine = jnp.tile(jnp.concatenate([cosine, cosine], axis=1), (micro, heads_rope))
-    sine = jnp.tile(jnp.concatenate([-sine, sine], axis=1), (micro, heads_rope))
-    cosine, sine = lax.optimization_barrier((cosine, sine))
-    project = mm(normed, qkv_full)
-    roped = rotate(project[:, : query_width + kv_width], cosine, sine).astype(BF16)
-    query = roped[:, :query_width].reshape(micro, count, query_width)
-    key_value = jnp.concatenate(
-        [roped[:, query_width:], project[:, query_width + kv_width :].astype(BF16)], axis=1
-    ).reshape(micro, count, 2 * kv_width)
-    mixed, kv_slots = plane_attention(query, key_value)
+    cosine = jnp.concatenate([cosine] * 4, axis=1)
+    sine = jnp.concatenate([-sine, sine] * 2, axis=1)
+    mixed, query, kv_slots = plane_attention(normed, qkv_full, cosine, sine, micro)
     mixed = mixed.reshape(rows, query_width)
     hidden = x + mm(mixed, out_full)
     inverse_two = lax.rsqrt(jnp.mean(hidden * hidden, axis=-1, keepdims=True) + 1e-05)
@@ -1996,20 +2068,21 @@
     payload = jnp.concatenate(
         [normed_two, high, low, jnp.zeros((rows, LANES - 2 * experts), BF16)], axis=1
     ).reshape(micro, count, model + LANES)
-    rows_in, row_weights = plane_dispatch(payload, ranks, where, per, cap, model, experts)
+    rows_in, row_weights, far_three = plane_dispatch(
+        payload, ranks, bank, where, per, cap, model, experts
+    )
+    weights_far = [far_one, far_two, far_three]
     tile = 2 * micro * split * cap
     outs, backs, weight_terms = expert_steps(
         where, rows_in, grads_in, row_weights, bank, weights_far, experts, tile
     )
-    back = plane_return(backs, ranks, micro, count, cap).reshape(rows, model + LANES)
-
+    back, term_one = plane_return(backs, ranks, weight_terms[1], micro, count, cap)
+    back = back.reshape(rows, model + LANES)
+
+    outs, back, late = lax.optimization_barrier((outs, back, weight_terms[2]))
     mixture_parts = scatter_rows(outs, ranks, where, n, micro * split, count, cap)
     mixture_sum = lax.psum_scatter(mixture_parts, "expert", scatter_dimension=0, tiled=False)
-    mixture = mixture_sum[:micro].astype(F32) + turn(mixture_sum[micro:], 1, split).astype(F32)
-    block_out = (hidden + mixture.reshape(rows, model)).astype(BF16).reshape(tokens.shape)
-
-    terms = weight_terms[:1] + [shift(weight_terms[s], s) for s in range(1, groups)]
-    gate_grad, up_grad, down_grad = [merge_grads(which, where, terms) for which in range(3)]
+    term_two = shift(late, 2)
 
     d_out = cotangent.reshape(rows, model).astype(F32)
     d_gates = back[:, model : model + experts] + back[:, model + experts : model + 2 * experts]
@@ -2029,36 +2102,27 @@
     d_hidden = d_out + rms_back(hidden, inverse_two, gain_two, d_normed_two)
     d_attn = d_hidden.astype(BF16)
     d_mixed = mm(d_attn, out_full, NT).astype(BF16).reshape(micro, count, query_width)
-    d_query, d_kv = plane_attention_backward(query, kv_slots, d_mixed)
-    d_query = d_query.reshape(rows, query_width)
-    d_kv = d_kv.reshape(rows, 2 * kv_width)
-    q_cos, q_sin = cosine[:, :query_width], sine[:, :query_width]
-    d_query_low = rotate(d_query, q_cos, -q_sin).astype(BF16)
-    d_key_low = rotate(d_kv[:, :kv_width], q_cos[:, :kv_width], -q_sin[:, :kv_width]).astype(BF16)
-    d_project = jnp.concatenate(
-        [d_query_low, d_key_low, d_kv[:, kv_width:].astype(BF16)], axis=1
-    )
+    d_project = plane_attention_backward(query, kv_slots, d_mixed, cosine, -sine)
+    d_project = d_project.reshape(rows, query_width + 2 * kv_width)
     d_normed = mm(d_project, qkv_full, NT)
     grad_one = jnp.sum(d_normed * x * inverse_one, axis=0)
     input_grad = (d_hidden + rms_back(x, inverse_one, gain_one, d_normed)).reshape(tokens.shape)
-    misc_grad = jnp.concatenate(
-        [
-            grad_one[:, None],
-            grad_two[:, None],
-            jnp.zeros((model, experts - 2), F32),
-            router_grad,
-            jnp.zeros((model, LANES - 2 * experts), F32),
-        ],
-        axis=1,
+    gains = jnp.concatenate([grad_one[None], grad_two[None], jnp.zeros((6, model), F32)], axis=0)
+    dense, term_three = plane_gradients(
+        [(mixed, d_attn), (normed, d_project)], router_grad, gains, weight_terms[3], groups
     )
-    dense = plane_gradients([(mixed, d_attn), (normed, d_project)], misc_grad, groups)
-    misc_sum = dense[:, model + query_width + 2 * kv_width :]
+    mixture_sum, dense = lax.optimization_barrier((mixture_sum, dense))
+    mixture = mixture_sum[:micro].astype(F32) + turn(mixture_sum[micro:], 1, split).astype(F32)
+    block_out = (hidden + mixture.reshape(rows, model)).astype(BF16).reshape(tokens.shape)
+    terms = [weight_terms[0], term_one, term_two, term_three]
+    gate_grad, up_grad, down_grad = [merge_grads(which, where, terms) for which in range(3)]
+    misc_sum = dense[:, model + query_width + 2 * kv_width :].astype(F32)
     return (
         block_out,
         input_grad,
         misc_sum[:, 0],
-        dense[:, model : model + query_width + 2 * kv_width],
-        dense[:, :model],
+        dense[:, model : model + query_width + 2 * kv_width].astype(F32),
+        dense[:, :model].astype(F32),
         misc_sum[:, 1],
         misc_sum[:, experts : 2 * experts],
         gate_grad,

time: 861 us -> 772 us (0.90)
  Pallas kernels: 670 us -> 583 us
  waiting for transfers between devices: 0.07 us -> 73.1 us
  starting transfers between devices: 62.4 us -> 19.8 us
  local copies, waits for them, and re-layouts: 50.7 us -> 18 us
    pallas_call x5, Pallas kernels: 459 us -> 376 us  [the longest x1 108 us: plane_gradients(): pl.pallas_call(kernel, in_specs=[vmem] * (len(flat) + 2) + [ANY_SPEC], ou...]
    all_gather x1, waiting for transfers between devices: 0.01 us -> 59.8 us  [layer_plane(): d_slots = lax.all_gather(both, 'expert', axis=0)]
    ppermute x5 -> x2, starting transfers between devices: 59.2 us -> 7.23 us  [shift(): return lax.ppermute(x, 'group', [(i, (i + step) % n) for i in range(n)])]
    ppermute x2, waiting for transfers between devices: 0.01 us -> 13.2 us  [turn(): lax.ppermute(x, 'group', [(i // split * split + (i + step) % split, i) fo...]
    slice x12 -> x0, local copies, waits for them, and re-layouts: 12.4 us -> none  [the longest x1 4.29 us: layer_plane(): dense[:, model:model + query_width + 2 * kv_width]]
    ppermute x2, starting transfers between devices: 3.05 us -> 12.5 us  [turn(): lax.ppermute(x, 'group', [(i // split * split + (i + step) % split, i) fo...]
    dot_general x5 -> x4, matrix products: 24.2 us -> 19.4 us  [mm(): return lax.dot_general(a, b, dims, preferred_element_type=F32)]
  transfers between devices with their start and end apart: 9 -> 6, of which waited for: 0 -> 2; matrix products, arithmetic and copies ran while one was open for 10% -> 8% of each run, Pallas kernels for 68% -> 54%
where the time goes in v3:
time: 772 us; the launch traced here: 763 us
  Pallas kernels  583 us (76%)
  waiting for transfers between devices  73.1 us (9%)
  other arithmetic  28.1 us (4%)
  matrix products  26.1 us (3%)
  starting transfers between devices  19.8 us (3%)
  local copies, waits for them, and re-layouts  18 us (2%)
  between operations  15 us (2%)
    pallas_call x1, Pallas kernels, plane_gradients(): pl.pallas_call(kernel, in_specs=[vmem] * (len(flat) + 2) + [ANY_SPEC], ou...  108 us
    pallas_call x1, Pallas kernels, plane_weights(): pl.pallas_call(kernel, in_specs=[vmem] * kinds + [ANY_SPEC], out_specs=[v...  90.6 us
    pallas_call x1, Pallas kernels, plane_return(): pl.pallas_call(kernel, in_specs=[vmem, vmem, ANY_SPEC], out_specs=[vmem,...  80.7 us
    pallas_call x1, Pallas kernels, plane_dispatch(): pl.pallas_call(kernel, in_specs=[SMEM_SPEC, vmem, vmem, ANY_SPEC], out_sp...  78.6 us
    pallas_call x1, Pallas kernels, expert_steps(): pl.pallas_call(kernel, grid=(per, steps), in_specs=[SMEM_SPEC, rows(model...  72.2 us
    pallas_call x1, Pallas kernels, plane_attention_backward(): pl.pallas_call(kernel, in_specs=[vmem] * 5, out_specs=vmem, out_shape=jax...  67.6 us
    all_gather x1, waiting for transfers between devices, layer_plane(): d_slots = lax.all_gather(both, 'expert', axis=0)  59.8 us
    pallas_call x1, Pallas kernels, plane_attention(): pl.pallas_call(kernel, in_specs=[vmem] * 4, out_specs=[vmem] * 3, out_sha...  41 us
  transfers between devices with their start and end apart: 6, of which 2 were waited for; matrix products, arithmetic and copies ran while one was open for 8% of the time, Pallas kernels for 54%

profile of v3, /device:TPU:0, one launch (start us, length us, event | category | flops | bytes accessed | tf_op | source)
XLA Modules:
  0.0 762.6 jit_solution(12271411685544294748)
XLA Ops:
  8.3 2.0 concatenate.26
  10.3 3.1 collective-permute-start
  13.3 1.7 copy.55
  19.7 3.7 pad_maximum_fusion.refs_2_.bank_ref.refs_0_
  24.7 1.6 pad_maximum_fusion.2.refs_1_
  27.0 90.6 %plane_weights.1 = (bf16[1536,2560]{1,0:T(8,128)(2,1)}, bf16[1536,1664]{1,0:T(8,128)(2,1)}, bf16[2,3,384,512]{3,2,1,0:T(8,128)(2,1)}) custom-call(bf16[48,2560]{1,0:T(8,128)(2,1)} %constant_dynamic-slice_fusion.3.refs_0_, bf16[48,1664]{1,0:T(8,128)(2,1)} %pad_maximum_fusion.2.refs_1_, bf16[4,3,384,512]{3,2,1,0:T(8,128)(2,1)} %pad_maximum_fusion.refs_2_.bank_ref.refs_0_), custom_call_target="tpu_custom_call" | custom-call | flops 1000000000 | bytes 1000000 | tf_op jit(solution)/shard_map/plane_weights/pallas_call | solution.py:1223
  117.6 3.4 constant_dynamic-slice_fusion
  120.9 2.8 pad_maximum_fusion.1
  128.7 6.7 collective-permute-start.1
  135.3 41.0 %plane_attention.1 = (bf16[2,128,1536]{2,1,0:T(8,128)(2,1)}, bf16[2,128,1536]{2,1,0:T(8,128)(2,1)}, bf16[8,2,128,1024]{3,2,1,0:T(8,128)(2,1)}) custom-call(bf16[256,1536]{1,0:T(8,128)(2,1)} %fusion.16.x_ref.refs_2_, bf16[1536,2560]{1,0:T(8,128)(2,1)} %get-tuple-element.42.w_ref, f32[128,128]{1,0:T(8,128)} %get-tuple-element.144.cos_ref, ...), custom_call_target="tpu_custom_call" | custom-call | flops 1000000000 | bytes 1000000 | tf_op jit(solution)/shard_map/plane_attention/pallas_call | solution.py:1350
  176.4 4.3 multiply_reduce_fusion.2
  180.9 1.9 fusion.34
  184.2 59.8 %all-gather.3.cloned.1.call-done = bf16[32,128,1664]{2,1,0:T(8,128)(2,1)} async-done(((bf16[4,128,1664]{2,1,0:T(8,128)(2,1)}), bf16[32,128,1664]{2,1,0:T(8,128)(2,1)}) %all-gather.3.cloned.1.call-update) | async-done | bytes 13631504 | tf_op jit(solution)/shard_map/all_gather | solution.py:2040
  244.0 15.3 %gather_flags.1 = (bf16[2,1536,1536]{2,1,0:T(8,128)(2,1)}, f32[32,2,128]{2,1,0:T(2,128)}) custom-call(s32[4]{0:T(128)} %pad_add_fusion.at_ref, bf16[8,4,128,1664]{3,2,1,0:T(8,128)(2,1)} %bitcast.87), custom_call_target="tpu_custom_call" | custom-call | flops 5000000000 | bytes 30000000 | tf_op jit(solution)/shard_map/gather_flags/pallas_call | solution.py:1783
  259.3 78.6 %plane_dispatch.1 = (bf16[2,1536,1536]{2,1,0:T(8,128)(2,1)}, f32[2,1536,128]{2,1,0:T(8,128)}, bf16[2,3,384,512]{3,2,1,0:T(8,128)(2,1)}) custom-call(s32[4]{0:T(128)} %pad_add_fusion.at_ref, bf16[2,128,1664]{2,1,0:T(8,128)(2,1)} %bitcast.73, f32[32,2,128]{2,1,0:T(2,128)} %get-tuple-element.46.rank_ref, ...), custom_call_target="tpu_custom_call" | custom-call | flops 1000000000 | bytes 1000000 | tf_op jit(solution)/shard_map/plane_dispatch/pallas_call | solution.py:1539
  338.0 72.2 %expert_steps.1 = (bf16[2,1536,1536]{2,1,0:T(8,128)(2,1)}, bf16[2,1536,1664]{2,1,0:T(8,128)(2,1)}, bf16[2,3,384,512]{3,2,1,0:T(8,128)(2,1)}, bf16[2,3,384,512]{3...) custom-call(s32[4]{0:T(128)} %pad_add_fusion.at_ref, ...), custom_call_target="tpu_custom_call" | custom-call | flops 43486543872 | bytes 47185920 | tf_op jit(solution)/shard_map/expert_steps/pallas_call | solution.py:1926
  410.2 80.7 %plane_return.1 = (f32[2,128,1664]{2,1,0:T(8,128)}, bf16[2,3,384,512]{3,2,1,0:T(8,128)(2,1)}) custom-call(f32[32,2,128]{2,1,0:T(2,128)} %get-tuple-element.46.rank_ref, bf16[2,1536,1664]{2,1,0:T(8,128)(2,1)} %get-tuple-element.54.in_ref, bf16[2,3,384,512]{3,2,1,0:T(8,128)(2,1)} %get-tuple-element.55.term_ref), custom_call_target="tpu_custom_call" | custom-call | flops 1000000000 | bytes 1000000 | tf_op jit(solution)/shard_map/plane_return/pallas_call | solution.py:1624
  490.9 14.1 %scatter_rows.1 = bf16[8,4,128,1536]{3,2,1,0:T(8,128)(2,1)} custom-call(s32[4]{0:T(128)} %pad_add_fusion.at_ref, f32[32,2,128]{2,1,0:T(2,128)} %get-tuple-element.46.rank_ref, bf16[2,1536,1536]{2,1,0:T(8,128)(2,1)} %get-tuple-element.58.in_ref), custom_call_target="tpu_custom_call" | custom-call | flops 5000000000 | bytes 30000000 | tf_op jit(solution)/shard_map/scatter_rows/pallas_call | solution.py:1822
  506.8 3.8 multiply_reduce_fusion
  512.4 6.1 fusion.7
  518.5 67.6 %plane_attention_backward.1 = bf16[2,128,2560]{2,1,0:T(8,128)(2,1)} custom-call(bf16[2,128,1536]{2,1,0:T(8,128)(2,1)} %get-tuple-element.60.q_ref, bf16[2,128,1536]{2,1,0:T(8,128)(2,1)} %bitcast.80, bf16[8,2,128,1024]{3,2,1,0:T(8,128)(2,1)} %get-tuple-element.61.kv_ref, f32[128,128]{1,0:T(8,128)} %get-tuple-element.144.cos_ref, ...), custom_call_target="tpu_custom_call" | custom-call | flops 1000000000 | bytes 1000000 | tf_op jit(solution)/shard_map/plane_attention_backward/pallas_call | solution.py:1458
  586.1 7.2 fusion.13
  593.3 2.9 fusion.35.refs_4_
  597.0 108.5 %plane_gradients.1 = (bf16[384,4224]{1,0:T(8,128)(2,1)}, bf16[2,3,384,512]{3,2,1,0:T(8,128)(2,1)}) custom-call(bf16[256,1536]{1,0:T(8,128)(2,1)} %bitcast.82, bf16[256,1536]{1,0:T(8,128)(2,1)} %copy-done.13, bf16[256,1536]{1,0:T(8,128)(2,1)} %fusion.16.x_ref.refs_2_, bf16[256,2560]{1,0:T(8,128)(2,1)} %bitcast.72, f32[1536,32]{1,0:T(8,128)} %fusion.35.refs_4_, ...), custom_call_target="tpu_custom_call" | custom-call | flops 1000000000 | bytes 1000000 | tf_op jit(solution)/shard_map/plane_gradients/pallas_call | solution.py:1736
  706.0 4.8 merge_grads.5
  710.9 4.4 merge_grads.4
  715.3 4.6 merge_grads.3
  720.0 3.1 slice_convert_fusion.1
  725.0 9.4 %collective-permute-start.2 = (bf16[2,128,1536]{2,1,0:T(8,128)(2,1)S(1)}, bf16[2,128,1536]{2,1,0:T(8,128)(2,1)S(1)}, u32[]{:S(2)}, u32[]{:S(2)}) collective-permute-start(bf16[2,128,1536]{2,1,0:T(8,128)(2,1)S(1)} %slice.57), channel_id=1, source_target_pairs={{8,0},{0,8},{24,16},{16,24},{9,1},{1,9},{25,17},{17,25},{10,2},{2,... | collective-permute-start | bytes 2359304 | tf_op jit(solution)/shard_map/ppermute | solution.py:44
  735.1 4.1 slice_convert_fusion
  739.3 13.2 %collective-permute-done.2 = bf16[2,128,1536]{2,1,0:T(8,128)(2,1)S(1)} collective-permute-done((bf16[2,128,1536]{2,1,0:T(8,128)(2,1)S(1)}, bf16[2,128,1536]{2,1,0:T(8,128)(2,1)S(1)}, u32[]{:S(2)}, u32[]{:S(2)}) %collective-permute-start.2) | collective-permute-done | bytes 786464 | tf_op jit(solution)/shard_map/ppermute | solution.py:44
  752.8 2.5 fusion.20
  (103 shorter events, 21.9 us)
Async XLA Ops:
  7.2 19.1 %copy-start = (bf16[384,2560]{1,0:T(8,128)(2,1)S(1)}, bf16[384,2560]{1,0:T(8,128)(2,1)}, u32[]{:S(2)}) copy-start(bf16[384,2560]{1,0:T(8,128)(2,1)} %param.15) | copy-start | bytes 5898244
  7.2 236.8 %all-gather.3.cloned.1.call-start = ((), (), s32[]{:S(2)}) async-start(), calls=%async_computation.2 | async-start | bytes 15335424 | tf_op jit(solution)/shard_map/all_gather | solution.py:2040
  10.3 110.7 %collective-permute-start = (bf16[2,128,1664]{2,1,0:T(8,128)(2,1)}, bf16[2,128,1664]{2,1,0:T(8,128)(2,1)}, u32[]{:S(2)}, u32[]{:S(2)}) collective-permute-start(bf16[2,128,1664]{2,1,0:T(8,128)(2,1)} %concatenate.26), channel_id=1, source_target_pairs={{8,0},{0,8},{24,16},{16,24},{9,1},{1,9},{25,17},{17,25},{10,2},{2,... | collective-permute-start | bytes 2555912 | tf_op jit(solution)/shard_map/ppermute | solution.py:44
  13.3 1.8 copy-start.23
  13.3 2.5 copy-start.24
  123.7 3.6 copy-start.6
  123.7 596.2 %reduce-scatter.2.cloned.1.call-start = ((), (), s32[]{:S(2)}) async-start(), calls=%async_computation.1 | async-start | bytes 14155776 | tf_op jit(solution)/shard_map/reduce_scatter | solution.py:2084
  127.5 458.6 %copy-start.20 = (f32[256]{0:T(256)}, f32[256]{0:T(256)S(1)}, u32[]{:S(2)}) copy-start(f32[256]{0:T(256)S(1)} %rsqrt_bitcast_fusion) | copy-start | bytes 3076
  128.7 209.3 %collective-permute-start.1 = (bf16[2,3,384,512]{3,2,1,0:T(8,128)(2,1)}, bf16[2,3,384,512]{3,2,1,0:T(8,128)(2,1)}, u32[]{:S(2)}, u32[]{:S(2)}) collective-permute-start(bf16[2,3,384,512]{3,2,1,0:T(8,128)(2,1)} %constant_dynamic-slice_fusion), channel_id=1, source_target_pairs={{0,16},{8,24},{16,0},{24,8},{1,17},{9,25},{17,1},{25,9},{2,18},{10... | collective-permute-start | bytes 7077896 | tf_op jit(solution)/shard_map/ppermute | solution.py:39
  180.6 330.0 %copy-start.2 = (f32[256,1536]{1,0:T(8,128)}, f32[256,1536]{1,0:T(8,128)S(1)}, u32[]{:S(2)}) copy-start(f32[256,1536]{1,0:T(8,128)S(1)} %get-tuple-element.139) | copy-start | bytes 4718596
  180.7 330.0 %copy-start.16 = (f32[256]{0:T(256)}, f32[256]{0:T(256)S(1)}, u32[]{:S(2)}) copy-start(f32[256]{0:T(256)S(1)} %add_rsqrt_fusion) | copy-start | bytes 3076
  180.9 3.3 copy-start.9
  505.1 200.9 %collective-permute-start.3 = (bf16[2,3,384,512]{3,2,1,0:T(8,128)(2,1)}, bf16[2,3,384,512]{3,2,1,0:T(8,128)(2,1)}, u32[]{:S(2)}, u32[]{:S(2)}) collective-permute-start(bf16[2,3,384,512]{3,2,1,0:T(8,128)(2,1)} %get-tuple-element.68), channel_id=1, source_target_pairs={{0,16},{8,24},{16,0},{24,8},{1,17},{9,25},{17,1},{25,9},{2,18},{10... | collective-permute-start | bytes 7077896 | tf_op jit(solution)/shard_map/ppermute | solution.py:39
  506.8 4.9 copy-start.11
  510.6 1.2 copy-start.4
  510.6 1.8 copy-start.18
  512.4 6.2 copy-start.13
  518.5 67.6 %copy-start.7 = (bf16[2,128,1536]{2,1,0:T(8,128)(2,1)S(1)}, bf16[2,128,1536]{2,1,0:T(8,128)(2,1)}, u32[]{:S(2)}) copy-start(bf16[2,128,1536]{2,1,0:T(8,128)(2,1)} %param.11) | copy-start | bytes 2359300
  586.1 7.2 copy-start.10
  719.9 5.0 copy-start.15
  725.0 27.5 %collective-permute-start.2 = (bf16[2,128,1536]{2,1,0:T(8,128)(2,1)S(1)}, bf16[2,128,1536]{2,1,0:T(8,128)(2,1)S(1)}, u32[]{:S(2)}, u32[]{:S(2)}) collective-permute-start(bf16[2,128,1536]{2,1,0:T(8,128)(2,1)S(1)} %slice.57), channel_id=1, source_target_pairs={{8,0},{0,8},{24,16},{16,24},{9,1},{1,9},{25,17},{17,25},{10,2},{2,... | collective-permute-start | bytes 2359304 | tf_op jit(solution)/shard_map/ppermute | solution.py:44
  735.1 17.6 %copy-start.8 = (bf16[2,128,1536]{2,1,0:T(8,128)(2,1)S(1)}, bf16[2,128,1536]{2,1,0:T(8,128)(2,1)}, u32[]{:S(2)}) copy-start(bf16[2,128,1536]{2,1,0:T(8,128)(2,1)} %param.11) | copy-start | bytes 2359300
  735.1 17.6 %copy-start.12 = (bf16[2,128,1536]{2,1,0:T(8,128)(2,1)S(1)}, bf16[2,128,1536]{2,1,0:T(8,128)(2,1)}, u32[]{:S(2)}) copy-start(bf16[2,128,1536]{2,1,0:T(8,128)(2,1)} %param.12) | copy-start | bytes 2359300
  735.1 17.6 %copy-start.14 = (f32[256,1536]{1,0:T(8,128)S(1)}, f32[256,1536]{1,0:T(8,128)}, u32[]{:S(2)}) copy-start(f32[256,1536]{1,0:T(8,128)} %get-tuple-element.143) | copy-start | bytes 4718596
  735.1 17.6 %copy-start.19 = (f32[256]{0:T(256)S(1)}, f32[256]{0:T(256)}, u32[]{:S(2)}) copy-start(f32[256]{0:T(256)} %copy-done.18) | copy-start | bytes 3076
  735.1 17.6 %copy-start.21 = (f32[256]{0:T(256)S(1)}, f32[256]{0:T(256)}, u32[]{:S(2)}) copy-start(f32[256]{0:T(256)} %copy-done.20) | copy-start | bytes 3076
  735.1 17.6 %copy-start.22 = (f32[256]{0:T(256)S(1)}, f32[256]{0:T(256)}, u32[]{:S(2)}) copy-start(f32[256]{0:T(256)} %broadcast_multiply_fusion) | copy-start | bytes 3076
  739.3 13.5 %copy-start.3 = (f32[256,1536]{1,0:T(8,128)S(1)}, f32[256,1536]{1,0:T(8,128)}, u32[]{:S(2)}) copy-start(f32[256,1536]{1,0:T(8,128)} %copy-done.2) | copy-start | bytes 4718596
  739.3 13.5 %copy-start.5 = (f32[256,1536]{1,0:T(8,128)S(1)}, f32[256,1536]{1,0:T(8,128)}, u32[]{:S(2)}) copy-start(f32[256,1536]{1,0:T(8,128)} %copy-done.4) | copy-start | bytes 4718596
  739.3 13.5 %copy-start.17 = (f32[256]{0:T(256)S(1)}, f32[256]{0:T(256)}, u32[]{:S(2)}) copy-start(f32[256]{0:T(256)} %copy-done.16) | copy-start | bytes 3076
  752.8 2.5 copy-start.1
Sparse Core Ops, SparseCore 0:
  123.8 120.1 all-gather.2
  505.1 106.3 reduce-scatter.1

commit v4 on v3

--- a/solution.py
+++ b/solution.py
@@ -1236,7 +1236,7 @@
             pltpu.SemaphoreType.DMA,
         ],
         compiler_params=params(1),
-        cost_estimate=cost(1e9, 1e6),
+        cost_estimate=cost(1e4, 1e3),
         name="plane_weights",
     )(*shares, bank)
 
@@ -1360,7 +1360,7 @@
             pltpu.SemaphoreType.DMA((micro,)),
         ],
         compiler_params=params(2),
-        cost_estimate=cost(1e9, 1e6),
+        cost_estimate=cost(1e4, 1e3),
         name="plane_attention",
     )(normed, weight, cosine, sine)
 
@@ -1467,7 +1467,7 @@
         ]
         + reduce_scratch(micro, tokens, width),
         compiler_params=params(3),
-        cost_estimate=cost(1e9, 1e6),
+        cost_estimate=cost(1e4, 1e3),
         name="plane_attention_backward",
     )(query, d_mixed, slots, cosine, sine)
 
@@ -1555,7 +1555,7 @@
             pltpu.SemaphoreType.DMA,
         ],
         compiler_params=params(4),
-        cost_estimate=cost(1e9, 1e6),
+        cost_estimate=cost(1e4, 1e3),
         name="plane_dispatch",
     )(where, payload, ranks, bank)
 
@@ -1640,7 +1640,7 @@
         ]
         + reduce_scratch(count, tokens, width),
         compiler_params=params(5),
-        cost_estimate=cost(1e9, 1e6),
+        cost_estimate=cost(1e4, 1e3),
         name="plane_return",
     )(ranks, rows, term)
 
@@ -1755,7 +1755,7 @@
         ]
         + reduce_scratch(groups, rows, width),
         compiler_params=params(6),
-        cost_estimate=cost(1e9, 1e6),
+        cost_estimate=cost(1e4, 1e3),
         name="plane_gradients",
     )(*flat, router, gains, term)
 
@@ -1833,7 +1833,7 @@
             ),
         ),
         out_shape=jax.ShapeDtypeStruct((n, count, tokens, width), BF16),
-        cost_estimate=cost(5e9, 3e7),
+        cost_estimate=cost(1e4, 1e3),
         name="scatter_rows",
     )(where, ranks, rows)
 
@@ -1976,7 +1976,7 @@
         + [pl.BlockSpec((per, 1, tile, ff), lambda t: (0, which, t, 0))] * len(terms),
         out_specs=spec,
         out_shape=jax.ShapeDtypeStruct(shape, F32),
-        cost_estimate=cost(1e8, 6e6),
+        cost_estimate=cost(1e5, 1e4),
         name="merge_grads",
     )(at, *terms)
 
@@ -2031,13 +2031,19 @@
     d_turned = turn(d_payload, 1, split)
 
     bank_two = lax.dynamic_slice_in_dim(bank, (z % split) * per, per, axis=0)
+    x = tokens.reshape(rows, model).astype(F32)
+    inverse_one = lax.rsqrt(jnp.mean(x * x, axis=-1, keepdims=True) + 1e-05)
+    cosine, sine = rope_tables(me, PR_DEV * n)
+    cosine = jnp.concatenate([cosine] * 4, axis=1)
+    sine = jnp.concatenate([-sine, sine] * 2, axis=1)
+    both = jnp.concatenate([d_payload, d_turned], axis=0)
+    both, bank_two, inverse_one, cosine, sine, shares = lax.optimization_barrier(
+        (both, bank_two, inverse_one, cosine, sine, shares)
+    )
+    d_slots = lax.all_gather(both, "expert", axis=0)
     qkv_full, rest_full, far_one = plane_weights(shares, bank, per)
-    (bank_two, d_payload, d_turned), qkv_full = lax.optimization_barrier(
-        ((bank_two, d_payload, d_turned), qkv_full)
-    )
+    bank_two, qkv_full = lax.optimization_barrier((bank_two, qkv_full))
     far_two = shift(bank_two, 2)
-    both = jnp.concatenate([d_payload, d_turned], axis=0)
-    d_slots = lax.all_gather(both, "expert", axis=0)
     out_full, misc_full = rest_full[:, :model], rest_full[:, model:]
     gain_one = misc_full[:, 0].astype(F32)
     gain_two = misc_full[:, 1].astype(F32)
@@ -2045,12 +2051,7 @@
 
     grads_in, ranks = gather_flags(d_slots, where, per, cap, model)
 
-    x = tokens.reshape(rows, model).astype(F32)
-    inverse_one = lax.rsqrt(jnp.mean(x * x, axis=-1, keepdims=True) + 1e-05)
     normed = (x * inverse_one * gain_one).astype(BF16)
-    cosine, sine = rope_tables(me, PR_DEV * n)
-    cosine = jnp.concatenate([cosine] * 4, axis=1)
-    sine = jnp.concatenate([-sine, sine] * 2, axis=1)
     mixed, query, kv_slots = plane_attention(normed, qkv_full, cosine, sine, micro)
     mixed = mixed.reshape(rows, query_width)
     hidden = x + mm(mixed, out_full)
@@ -2079,9 +2080,7 @@
     back, term_one = plane_return(backs, ranks, weight_terms[1], micro, count, cap)
     back = back.reshape(rows, model + LANES)
 
-    outs, back, late = lax.optimization_barrier((outs, back, weight_terms[2]))
-    mixture_parts = scatter_rows(outs, ranks, where, n, micro * split, count, cap)
-    mixture_sum = lax.psum_scatter(mixture_parts, "expert", scatter_dimension=0, tiled=False)
+    late, back = lax.optimization_barrier((weight_terms[2], back))
     term_two = shift(late, 2)
 
     d_out = cotangent.reshape(rows, model).astype(F32)
@@ -2101,6 +2100,9 @@
     grad_two = jnp.sum(d_normed_two * hidden * inverse_two, axis=0)
     d_hidden = d_out + rms_back(hidden, inverse_two, gain_two, d_normed_two)
     d_attn = d_hidden.astype(BF16)
+    outs, d_attn = lax.optimization_barrier((outs, d_attn))
+    mixture_parts = scatter_rows(outs, ranks, where, n, micro * split, count, cap)
+    mixture_sum = lax.psum_scatter(mixture_parts, "expert", scatter_dimension=0, tiled=False)
     d_mixed = mm(d_attn, out_full, NT).astype(BF16).reshape(micro, count, query_width)
     d_project = plane_attention_backward(query, kv_slots, d_mixed, cosine, -sine)
     d_project = d_project.reshape(rows, query_width + 2 * kv_width)
@@ -2112,7 +2114,8 @@
         [(mixed, d_attn), (normed, d_project)], router_grad, gains, weight_terms[3], groups
     )
     mixture_sum, dense = lax.optimization_barrier((mixture_sum, dense))
-    mixture = mixture_sum[:micro].astype(F32) + turn(mixture_sum[micro:], 1, split).astype(F32)
+    mixture_far, dense = lax.optimization_barrier((turn(mixture_sum[micro:], 1, split), dense))
+    mixture = mixture_sum[:micro].astype(F32) + mixture_far.astype(F32)
     block_out = (hidden + mixture.reshape(rows, model)).astype(BF16).reshape(tokens.shape)
     terms = [weight_terms[0], term_one, term_two, term_three]
     gate_grad, up_grad, down_grad = [merge_grads(which, where, terms) for which in range(3)]

time: 772 us -> 795 us (1.030)
  Pallas kernels: 583 us -> 675 us
  waiting for transfers between devices: 73.1 us -> 9.75 us
    all_gather x1, waiting for transfers between devices: 59.8 us -> 0.01 us  [layer_plane(): d_slots = lax.all_gather(both, 'expert', axis=0)]
    pallas_call x1, Pallas kernels: 78.6 us -> 113 us  [plane_dispatch(): pl.pallas_call(kernel, in_specs=[SMEM_SPEC, vmem, vmem, ANY_SPEC], out_sp...]
    pallas_call x1, Pallas kernels: 80.7 us -> 111 us  [plane_return(): pl.pallas_call(kernel, in_specs=[vmem, vmem, ANY_SPEC], out_specs=[vmem,...]
    pallas_call x1, Pallas kernels: 90.6 us -> 112 us  [plane_weights(): pl.pallas_call(kernel, in_specs=[vmem] * kinds + [ANY_SPEC], out_specs=[v...]
  transfers between devices with their start and end apart: 6 -> 6, of which waited for: 2 -> 2; matrix products, arithmetic and copies ran while one was open for 8% -> 5% of each run, Pallas kernels for 54% -> 61%
where the time goes in v4:
time: 795 us; the launch traced here: 785 us
  Pallas kernels  675 us (85%)
  other arithmetic  30.6 us (4%)
  matrix products  24.8 us (3%)
  local copies, waits for them, and re-layouts  17 us (2%)
  between operations  14.9 us (2%)
  starting transfers between devices  13.2 us (2%)
  waiting for transfers between devices  9.75 us (1%)
    pallas_call x1, Pallas kernels, plane_dispatch(): pl.pallas_call(kernel, in_specs=[SMEM_SPEC, vmem, vmem, ANY_SPEC], out_sp...  113 us
    pallas_call x1, Pallas kernels, plane_weights(): pl.pallas_call(kernel, in_specs=[vmem] * kinds + [ANY_SPEC], out_specs=[v...  112 us
    pallas_call x1, Pallas kernels, plane_return(): pl.pallas_call(kernel, in_specs=[vmem, vmem, ANY_SPEC], out_specs=[vmem,...  111 us
    pallas_call x1, Pallas kernels, plane_gradients(): pl.pallas_call(kernel, in_specs=[vmem] * (len(flat) + 2) + [ANY_SPEC], ou...  111 us
    pallas_call x1, Pallas kernels, plane_attention_backward(): pl.pallas_call(kernel, in_specs=[vmem] * 5, out_specs=vmem, out_shape=jax...  72.6 us
    pallas_call x1, Pallas kernels, expert_steps(): pl.pallas_call(kernel, grid=(per, steps), in_specs=[SMEM_SPEC, rows(model...  72.2 us
    pallas_call x1, Pallas kernels, plane_attention(): pl.pallas_call(kernel, in_specs=[vmem] * 4, out_specs=[vmem] * 3, out_sha...  40.4 us
    dot_general x4, matrix products, mm(): return lax.dot_general(a, b, dims, preferred_element_type=F32)  18.8 us
  transfers between devices with their start and end apart: 6, of which 2 were waited for; matrix products, arithmetic and copies ran while one was open for 5% of the time, Pallas kernels for 61%

profile of v4, /device:TPU:0, one launch (start us, length us, event | category | flops | bytes accessed | tf_op | source)
XLA Modules:
  0.0 785.1 jit_solution(9767896362782471040)
XLA Ops:
  8.3 2.0 concatenate.24
  10.3 3.1 collective-permute-start
  13.4 2.7 copy.53
  16.7 2.6 pad_maximum_fusion.refs_2_.bank_ref.refs_0_
  19.3 2.1 copy-done.2
  21.4 1.6 constant_dynamic-slice_fusion.3
  26.7 5.8 collective-permute-done
  32.6 2.8 pad_maximum_fusion.1
  36.2 111.8 %plane_weights.1 = (bf16[1536,2560]{1,0:T(8,128)(2,1)}, bf16[1536,1664]{1,0:T(8,128)(2,1)}, bf16[2,3,384,512]{3,2,1,0:T(8,128)(2,1)}) custom-call(bf16[48,2560]{1,0:T(8,128)(2,1)} %constant_dynamic-slice_fusion.2.refs_0_, bf16[48,1664]{1,0:T(8,128)(2,1)} %pad_maximum_fusion.2.refs_1_, bf16[4,3,384,512]{3,2,1,0:T(8,128)(2,1)} %copy-done.2), custom_call_target="tpu_custom_call" | custom-call | flops 10000 | bytes 1000 | tf_op jit(solution)/shard_map/plane_weights/pallas_call | solution.py:1223
  148.1 1.6 convert_reduce_fusion
  150.8 40.4 %plane_attention.1 = (bf16[2,128,1536]{2,1,0:T(8,128)(2,1)}, bf16[2,128,1536]{2,1,0:T(8,128)(2,1)}, bf16[8,2,128,1024]{3,2,1,0:T(8,128)(2,1)}) custom-call(bf16[256,1536]{1,0:T(8,128)(2,1)} %fusion.16.x_ref.refs_2_, bf16[1536,2560]{1,0:T(8,128)(2,1)} %get-tuple-element.54.w_ref, f32[128,128]{1,0:T(8,128)} %get-tuple-element.55.cos_ref, ...), custom_call_target="tpu_custom_call" | custom-call | flops 10000 | bytes 1000 | tf_op jit(solution)/shard_map/plane_attention/pallas_call | solution.py:1350
  191.2 4.3 multiply_reduce_fusion.2
  195.7 1.9 fusion.33
  199.0 15.3 %gather_flags.1 = (bf16[2,1536,1536]{2,1,0:T(8,128)(2,1)}, f32[32,2,128]{2,1,0:T(2,128)}) custom-call(s32[4]{0:T(128)} %pad_add_fusion.at_ref, bf16[8,4,128,1664]{3,2,1,0:T(8,128)(2,1)} %bitcast.90), custom_call_target="tpu_custom_call" | custom-call | flops 5000000000 | bytes 30000000 | tf_op jit(solution)/shard_map/gather_flags/pallas_call | solution.py:1783
  214.3 112.7 %plane_dispatch.1 = (bf16[2,1536,1536]{2,1,0:T(8,128)(2,1)}, f32[2,1536,128]{2,1,0:T(8,128)}, bf16[2,3,384,512]{3,2,1,0:T(8,128)(2,1)}) custom-call(s32[4]{0:T(128)} %pad_add_fusion.at_ref, bf16[2,128,1664]{2,1,0:T(8,128)(2,1)} %bitcast.73, f32[32,2,128]{2,1,0:T(2,128)} %get-tuple-element.59.rank_ref, bf16[4,3,384,512]{3,2,1,0:T(8,128)(2,1)} %copy-done.2), custom_call_target="tpu_custom_call" | custom-call | flops 10000 | bytes 1000 | tf_op jit(solution)/shard_map/plane_dispatch/pallas_call | solution.py:1539
  327.0 72.2 %expert_steps.1 = (bf16[2,1536,1536]{2,1,0:T(8,128)(2,1)}, bf16[2,1536,1664]{2,1,0:T(8,128)(2,1)}, bf16[2,3,384,512]{3,2,1,0:T(8,128)(2,1)}, bf16[2,3,384,512]{3...) custom-call(s32[4]{0:T(128)} %pad_add_fusion.at_ref, ...), custom_call_target="tpu_custom_call" | custom-call | flops 43486543872 | bytes 47185920 | tf_op jit(solution)/shard_map/expert_steps/pallas_call | solution.py:1926
  399.2 111.3 %plane_return.1 = (f32[2,128,1664]{2,1,0:T(8,128)}, bf16[2,3,384,512]{3,2,1,0:T(8,128)(2,1)}) custom-call(f32[32,2,128]{2,1,0:T(2,128)} %get-tuple-element.59.rank_ref, bf16[2,1536,1664]{2,1,0:T(8,128)(2,1)} %get-tuple-element.68.in_ref, bf16[2,3,384,512]{3,2,1,0:T(8,128)(2,1)} %get-tuple-element.69.term_ref), custom_call_target="tpu_custom_call" | custom-call | flops 10000 | bytes 1000 | tf_op jit(solution)/shard_map/plane_return/pallas_call | solution.py:1624
  511.7 3.0 multiply_reduce_fusion
  515.9 14.0 %scatter_rows.1 = bf16[8,4,128,1536]{3,2,1,0:T(8,128)(2,1)} custom-call(s32[4]{0:T(128)} %pad_add_fusion.at_ref, f32[32,2,128]{2,1,0:T(2,128)} %get-tuple-element.59.rank_ref, bf16[2,1536,1536]{2,1,0:T(8,128)(2,1)} %get-tuple-element.72.in_ref), custom_call_target="tpu_custom_call" | custom-call | flops 10000 | bytes 1000 | tf_op jit(solution)/shard_map/scatter_rows/pallas_call | solution.py:1822
  532.0 5.5 fusion.7
  537.5 72.6 %plane_attention_backward.1 = bf16[2,128,2560]{2,1,0:T(8,128)(2,1)} custom-call(bf16[2,128,1536]{2,1,0:T(8,128)(2,1)} %get-tuple-element.74.q_ref, bf16[2,128,1536]{2,1,0:T(8,128)(2,1)} %bitcast.80, bf16[8,2,128,1024]{3,2,1,0:T(8,128)(2,1)} %get-tuple-element.75.kv_ref, f32[128,128]{1,0:T(8,128)} %get-tuple-element.55.cos_ref, f32[128,128]{1,0:T(8,128)} %neg.15.sin_ref), custom_call_target="tpu_custom_call" | custom-call | flops 10000 | bytes 1000 | tf_op jit(solution)/shard_map/plane_attention_backward/pallas_call | solution.py:1458
  610.1 7.2 fusion.13
  617.3 2.9 fusion.34.refs_4_
  621.0 110.9 %plane_gradients.1 = (bf16[384,4224]{1,0:T(8,128)(2,1)}, bf16[2,3,384,512]{3,2,1,0:T(8,128)(2,1)}) custom-call(bf16[256,1536]{1,0:T(8,128)(2,1)} %bitcast.82, bf16[256,1536]{1,0:T(8,128)(2,1)} %copy-done.12, bf16[256,1536]{1,0:T(8,128)(2,1)} %fusion.16.x_ref.refs_2_, bf16[256,2560]{1,0:T(8,128)(2,1)} %bitcast.72, f32[1536,32]{1,0:T(8,128)} %fusion.34.refs_4_, ...), custom_call_target="tpu_custom_call" | custom-call | flops 10000 | bytes 1000 | tf_op jit(solution)/shard_map/plane_gradients/pallas_call | solution.py:1736
  733.0 9.4 %collective-permute-start.2 = (bf16[2,128,1536]{2,1,0:T(8,128)(2,1)S(1)}, bf16[2,128,1536]{2,1,0:T(8,128)(2,1)S(1)}, u32[]{:S(2)}, u32[]{:S(2)}) collective-permute-start(bf16[2,128,1536]{2,1,0:T(8,128)(2,1)S(1)} %slice.57), channel_id=1, source_target_pairs={{8,0},{0,8},{24,16},{16,24},{9,1},{1,9},{25,17},{17,25},{10,2},{2,... | collective-permute-start | bytes 2359304 | tf_op jit(solution)/shard_map/ppermute | solution.py:44
  743.0 4.8 merge_grads.5
  747.9 4.4 merge_grads.4
  752.3 4.4 merge_grads.3
  756.7 3.8 collective-permute-done.2
  761.4 4.0 slice_convert_fusion
  765.4 3.1 slice_convert_fusion.1
  772.5 5.4 fusion.20
  (100 shorter events, 20.8 us)
Async XLA Ops:
  7.2 18.8 %copy-start = (bf16[384,2560]{1,0:T(8,128)(2,1)S(1)}, bf16[384,2560]{1,0:T(8,128)(2,1)}, u32[]{:S(2)}) copy-start(bf16[384,2560]{1,0:T(8,128)(2,1)} %param.15) | copy-start | bytes 5898244
  7.2 191.8 %all-gather.3.cloned.1.call-start = ((), (), s32[]{:S(2)}) async-start(), calls=%async_computation.2 | async-start | bytes 15335424 | tf_op jit(solution)/shard_map/all_gather | solution.py:2043
  10.3 22.3 %collective-permute-start = (bf16[2,128,1664]{2,1,0:T(8,128)(2,1)}, bf16[2,128,1664]{2,1,0:T(8,128)(2,1)}, u32[]{:S(2)}, u32[]{:S(2)}) collective-permute-start(bf16[2,128,1664]{2,1,0:T(8,128)(2,1)} %concatenate.24), channel_id=1, source_target_pairs={{8,0},{0,8},{24,16},{16,24},{9,1},{1,9},{25,17},{17,25},{10,2},{2,... | collective-permute-start | bytes 2555912 | tf_op jit(solution)/shard_map/ppermute | solution.py:44
  13.3 2.7 copy-start.21
  13.3 2.8 copy-start.22
  13.3 2.9 copy-start.18
  13.3 3.1 copy-start.6
  16.7 593.4 %copy-start.20 = (f32[2,128]{1,0:T(2,128)}, f32[2,128]{1,0:T(2,128)S(1)}, u32[]{:S(2)}) copy-start(f32[2,128]{1,0:T(2,128)S(1)} %add_rsqrt_fusion.1) | copy-start | bytes 3076
  19.3 2.1 copy-start.2
  35.4 696.5 %reduce-scatter.2.cloned.1.call-start = ((), (), s32[]{:S(2)}) async-start(), calls=%async_computation.1 | async-start | bytes 14155776 | tf_op jit(solution)/shard_map/reduce_scatter | solution.py:2105
  36.2 113.5 %copy-start.7 = (bf16[2,128,1536]{2,1,0:T(8,128)(2,1)S(1)}, bf16[2,128,1536]{2,1,0:T(8,128)(2,1)}, u32[]{:S(2)}) copy-start(bf16[2,128,1536]{2,1,0:T(8,128)(2,1)} %param.11) | copy-start | bytes 2359300
  148.0 179.0 %collective-permute-start.1 = (bf16[2,3,384,512]{3,2,1,0:T(8,128)(2,1)}, bf16[2,3,384,512]{3,2,1,0:T(8,128)(2,1)}, u32[]{:S(2)}, u32[]{:S(2)}) collective-permute-start(bf16[2,3,384,512]{3,2,1,0:T(8,128)(2,1)} %constant_dynamic-slice_fusion.3), channel_id=1, source_target_pairs={{0,16},{8,24},{16,0},{24,8},{1,17},{9,25},{17,1},{25,9},{2,18},{10... | collective-permute-start | bytes 7077896 | tf_op jit(solution)/shard_map/ppermute | solution.py:39
  195.4 319.4 %copy-start.3 = (f32[256,1536]{1,0:T(8,128)}, f32[256,1536]{1,0:T(8,128)S(1)}, u32[]{:S(2)}) copy-start(f32[256,1536]{1,0:T(8,128)S(1)} %get-tuple-element.153) | copy-start | bytes 4718596
  195.4 319.4 %copy-start.17 = (f32[256]{0:T(256)}, f32[256]{0:T(256)S(1)}, u32[]{:S(2)}) copy-start(f32[256]{0:T(256)S(1)} %add_rsqrt_fusion) | copy-start | bytes 3076
  195.6 3.3 copy-start.9
  511.7 3.1 copy-start.11
  514.8 1.2 copy-start.5
  514.8 1.2 copy-start.19
  515.9 16.1 %copy-start.12 = (bf16[256,1536]{1,0:T(8,128)(2,1)}, bf16[256,1536]{1,0:T(8,128)(2,1)S(1)}, u32[]{:S(2)}) copy-start(bf16[256,1536]{1,0:T(8,128)(2,1)S(1)} %fusion.31.refs_1_) | copy-start | bytes 2359300
  530.0 0.8 copy-start.16
  531.4 211.6 %collective-permute-start.3 = (bf16[2,3,384,512]{3,2,1,0:T(8,128)(2,1)}, bf16[2,3,384,512]{3,2,1,0:T(8,128)(2,1)}, u32[]{:S(2)}, u32[]{:S(2)}) collective-permute-start(bf16[2,3,384,512]{3,2,1,0:T(8,128)(2,1)} %get-tuple-element.84), channel_id=1, source_target_pairs={{0,16},{8,24},{16,0},{24,8},{1,17},{9,25},{17,1},{25,9},{2,18},{10... | collective-permute-start | bytes 7077896 | tf_op jit(solution)/shard_map/ppermute | solution.py:39
  537.5 72.6 %copy-start.8 = (bf16[2,128,1536]{2,1,0:T(8,128)(2,1)S(1)}, bf16[2,128,1536]{2,1,0:T(8,128)(2,1)}, u32[]{:S(2)}) copy-start(bf16[2,128,1536]{2,1,0:T(8,128)(2,1)} %param.11) | copy-start | bytes 2359300
  610.1 7.2 copy-start.10
  733.0 27.5 %collective-permute-start.2 = (bf16[2,128,1536]{2,1,0:T(8,128)(2,1)S(1)}, bf16[2,128,1536]{2,1,0:T(8,128)(2,1)S(1)}, u32[]{:S(2)}, u32[]{:S(2)}) collective-permute-start(bf16[2,128,1536]{2,1,0:T(8,128)(2,1)S(1)} %slice.57), channel_id=1, source_target_pairs={{8,0},{0,8},{24,16},{16,24},{9,1},{1,9},{25,17},{17,25},{10,2},{2,... | collective-permute-start | bytes 2359304 | tf_op jit(solution)/shard_map/ppermute | solution.py:44
  760.6 0.9 copy-start.14
  765.4 5.0 copy-start.13
  765.4 5.0 copy-start.15
  770.4 2.1 copy-start.4
  772.5 5.4 copy-start.1
Sparse Core Ops, SparseCore 0:
  35.5 115.8 all-gather.2
  530.1 106.3 reduce-scatter.1

commit v5 on v3

--- a/solution.py
+++ b/solution.py
@@ -1512,7 +1512,7 @@
         last = groups - 1
         first = lax.rem(z + last, split) * per
         follow = remote(
-            bank_ref.at[pl.ds(first, per)], far_ref, b_send, b_recv,
+            bank_ref.at[pl.ds(first, 1)], far_ref, b_send, b_recv,
             {"group": lax.rem(z + last, groups)},
         )
         greet(plane_devices(e) + [{"group": lax.rem(z + s, groups)} for s in (1, last)])
@@ -1543,7 +1543,7 @@
         out_shape=[
             jax.ShapeDtypeStruct((per, total, model), BF16),
             jax.ShapeDtypeStruct((per, total, LANES), F32),
-            jax.ShapeDtypeStruct((per,) + bank.shape[1:], BF16),
+            jax.ShapeDtypeStruct((1,) + bank.shape[1:], BF16),
         ],
         scratch_shapes=[
             pltpu.VMEM((n, count, tokens, width), BF16),
@@ -1560,14 +1560,14 @@
     )(where, payload, ranks, bank)
 
 
-def plane_return(rows, ranks, term, micro, tokens, cap):
+def plane_return(rows, ranks, next_term, last_terms, micro, tokens, cap):
     per, _, width = rows.shape
     n, split = 8, 2
     groups = lax.axis_size("group")
     count = split * micro
     chunks = list(range(micro, count)) + list(range(micro))
 
-    def kernel(rank_ref, in_ref, term_ref, out, far_ref, *refs):
+    def kernel(rank_ref, in_ref, next_ref, last_ref, out, next_far, last_far, *refs):
         parts, z_out, z_in, z_send, z_recv, t_send, t_recv, scratch = *refs[:7], refs[7:]
         e, z = lax.axis_index("expert"), lax.axis_index("group")
         red = Reduce(e, lambda r, c: parts.at[r, c], [c % 2 for c in range(count)], *scratch)
@@ -1587,9 +1587,18 @@
                 z_out.at[m], z_in.at[m], z_send.at[m], z_recv.at[m], {"group": partner(z)}
             )
 
-        follow = remote(term_ref, far_ref, t_send, t_recv, {"group": lax.rem(z + 1, groups)})
+        follow = [
+            remote(
+                next_ref, next_far, t_send.at[0], t_recv.at[0], {"group": lax.rem(z + 1, groups)}
+            ),
+            remote(
+                last_ref.at[0], last_far, t_send.at[1], t_recv.at[1],
+                {"group": lax.rem(z + groups - 1, groups)},
+            ),
+        ]
         greet(plane_devices(e) + [{"group": lax.rem(z + s, groups)} for s in (1, groups - 1)])
-        follow.start()
+        for one in follow:
+            one.start()
         for r in (7, 3, 5):
             for c in chunks:
                 produce(r, c)
@@ -1618,16 +1627,18 @@
             turned(m).wait_send()
         for c in chunks:
             red.finish(c)
-        follow.wait()
+        for one in follow:
+            one.wait()
 
     vmem = pl.BlockSpec(memory_space=pltpu.VMEM)
     return pl.pallas_call(
         kernel,
-        in_specs=[vmem, vmem, ANY_SPEC],
-        out_specs=[vmem, ANY_SPEC],
+        in_specs=[vmem, vmem, ANY_SPEC, ANY_SPEC],
+        out_specs=[vmem, ANY_SPEC, ANY_SPEC],
         out_shape=[
             jax.ShapeDtypeStruct((micro, tokens, width), F32),
-            jax.ShapeDtypeStruct(term.shape, BF16),
+            jax.ShapeDtypeStruct(next_term.shape, BF16),
+            jax.ShapeDtypeStruct(next_term.shape, BF16),
         ],
         scratch_shapes=[
             pltpu.VMEM((n, count, tokens, width), BF16),
@@ -1635,17 +1646,17 @@
             pltpu.VMEM((micro, tokens, width), BF16),
             pltpu.SemaphoreType.DMA((micro,)),
             pltpu.SemaphoreType.DMA((micro,)),
-            pltpu.SemaphoreType.DMA,
-            pltpu.SemaphoreType.DMA,
+            pltpu.SemaphoreType.DMA((2,)),
+            pltpu.SemaphoreType.DMA((2,)),
         ]
         + reduce_scratch(count, tokens, width),
         compiler_params=params(5),
         cost_estimate=cost(1e9, 1e6),
         name="plane_return",
-    )(ranks, rows, term)
-
-
-def plane_gradients(products, router, gains, term, groups):
+    )(ranks, rows, next_term, last_terms)
+
+
+def plane_gradients(products, router, gains, terms, groups):
     n = 8
     depth = products[0][0].shape[1]
     widths = [b.shape[1] for a, b in products]
@@ -1667,7 +1678,7 @@
             + [{"group": lax.rem(z + s, groups)} for s in range(1, groups)]
         )
         follow = remote(
-            term_ref, far_ref, t_send, t_recv, {"group": lax.rem(z + groups - 1, groups)}
+            term_ref.at[1], far_ref, t_send, t_recv, {"group": lax.rem(z + groups - 1, groups)}
         )
         follow.start()
 
@@ -1739,7 +1750,7 @@
         out_specs=[vmem, ANY_SPEC],
         out_shape=[
             jax.ShapeDtypeStruct((n * rows, width), BF16),
-            jax.ShapeDtypeStruct(term.shape, BF16),
+            jax.ShapeDtypeStruct(terms.shape[1:], BF16),
         ],
         scratch_shapes=[
             pltpu.VMEM((depth, tile), F32),
@@ -1757,7 +1768,7 @@
         compiler_params=params(6),
         cost_estimate=cost(1e9, 1e6),
         name="plane_gradients",
-    )(*flat, router, gains, term)
+    )(*flat, router, gains, terms)
 
 
 def gather_flags(slots, where, per, cap, model):
@@ -1838,43 +1849,73 @@
     )(where, ranks, rows)
 
 
-def expert_steps(at, rows_in, grads_in, weights, bank, far, experts, tile):
+def expert_steps(rows_in, grads_in, weights, bank, far, experts, tile):
     per, total, model = rows_in.shape
     part, ff = bank.shape[2:]
     groups = model // part
     steps = total // tile
-
-    def kernel(at_ref, x_ref, d_ref, w_ref, *refs):
+    split = 2
+    here = bank.shape[0]
+    last = groups - 1
+
+    def kernel(x_ref, d_ref, w_ref, *refs):
         sources, o_ref, r_ref, refs = refs[:groups], refs[groups], refs[groups + 1], refs[groups + 2 :]
-        outs, (acc_wide, acc_down, wide_all, down_all, sems) = refs[:groups], refs[groups:]
+        outs, got_ref, refs = refs[:groups], refs[groups], refs[groups + 1 :]
+        acc_wide, acc_down, wide_all, down_all, early, sems, w_send, w_recv, g_send, g_recv = refs
         k, step = pl.program_id(0), pl.program_id(1)
+        me, mine_z = lax.axis_index("expert"), lax.axis_index("group")
+        own_first = lax.rem(mine_z, split) * per
+
+        def rows_of(index, z):
+            at_z = pl.ds(pl.multiple_of(z * part, 128), part)
+            wide, down = wide_all.at[index], down_all.at[index]
+            return [wide.at[at_z, :ff], wide.at[at_z, ff:], down.at[at_z, :]]
 
         def loads(index):
             copies = []
-            for s in range(groups):
-                z = lax.rem(at_ref[0] - s + groups, groups)
-                at_z = pl.ds(pl.multiple_of(z * part, 128), part)
-                source = sources[s].at[at_ref[3] + index if s == 0 else index]
-                wide, down = wide_all.at[index], down_all.at[index]
-                for i, dst in enumerate([wide.at[at_z, :ff], wide.at[at_z, ff:], down.at[at_z, :]]):
+            for s in range(groups - index):
+                source = sources[s].at[own_first + index if s == 0 else index]
+                there = rows_of(index, lax.rem(mine_z - s + groups, groups))
+                for i, dst in enumerate(there):
                     copies.append(
                         pltpu.make_async_copy(source.at[i], dst, sems.at[index, 3 * s + i])
                     )
             return copies
 
-        for index in range(per):
-
-            @pl.when((k == 0) & (step == 0))
-            def _():
+        def late_weights(z):
+            source = sources[0].at[lax.rem(mine_z + last, split) * per + 1]
+            return [
+                remote(
+                    source.at[i], dst, w_send.at[i], w_recv.at[i],
+                    {"group": lax.rem(mine_z + last, groups)},
+                )
+                for i, dst in enumerate(rows_of(1, z))
+            ]
+
+        early_term = remote(
+            early, got_ref, g_send, g_recv, {"group": lax.rem(mine_z + 1, groups)}
+        )
+
+        @pl.when((k == 0) & (step == 0))
+        def _():
+            for index in range(per):
                 for one in loads(index):
                     one.start()
-
-        for index in range(per):
-
-            @pl.when((k == index) & (step == 0))
-            def _():
-                for one in loads(index):
-                    one.wait()
+            greet([{"group": lax.rem(mine_z + s, groups)} for s in (1, last)])
+            for one in late_weights(mine_z):
+                one.start()
+            for one in loads(0):
+                one.wait()
+
+        @pl.when((k == 1) & (step == 0))
+        def _():
+            early_term.start()
+            for one in loads(1):
+                one.wait()
+            for one in late_weights(lax.rem(mine_z + 1, groups)):
+                one.wait_recv()
+            for one in late_weights(mine_z):
+                one.wait_send()
 
         wide_ref, down_ref = wide_all.at[k], down_all.at[k]
         x, d = x_ref[0], d_ref[0]
@@ -1895,7 +1936,7 @@
         r_ref[0, :, :model] = mm(d_both, wide_ref[...], NT).astype(BF16)
         high = d_gates.astype(BF16).astype(F32)
         lane = lax.broadcasted_iota(jnp.int32, (tile, LANES), 1)
-        e = at_ref[2] + k
+        e = me * here + own_first + k
         r_ref[0, :, model:] = (
             jnp.where(lane == e, high, 0.0) + jnp.where(lane == e + experts, d_gates - high, 0.0)
         ).astype(BF16)
@@ -1915,50 +1956,80 @@
         @pl.when(step == steps - 1)
         def _():
             for s in range(groups):
-                z = lax.rem(at_ref[0] + s, groups)
+                z = lax.rem(mine_z + s, groups)
                 at_z = pl.ds(pl.multiple_of(z * part, 128), part)
-                outs[s][0, 0] = acc_wide[at_z, :ff].astype(BF16)
-                outs[s][0, 1] = acc_wide[at_z, ff:].astype(BF16)
-                outs[s][0, 2] = acc_down[:, at_z].T.astype(BF16)
+
+                def put(dst):
+                    dst[0] = acc_wide[at_z, :ff].astype(BF16)
+                    dst[1] = acc_wide[at_z, ff:].astype(BF16)
+                    dst[2] = acc_down[:, at_z].T.astype(BF16)
+
+                if s == 1:
+                    pl.when(k == 0)(lambda: put(early))
+                    pl.when(k == 1)(lambda: put(outs[s]))
+                else:
+                    put(outs[s].at[0])
+
+        @pl.when((k == per - 1) & (step == steps - 1))
+        def _():
+            early_term.wait()
 
     grad = pl.BlockSpec((1, 3, part, ff), lambda k, t: (k, 0, 0, 0), pipeline_mode=pl.Buffered(1))
+    single = pl.BlockSpec((3, part, ff), lambda k, t: (0, 0, 0), pipeline_mode=pl.Buffered(1))
     rows = lambda width: pl.BlockSpec((1, tile, width), lambda k, t: (k, t, 0))
     out = pl.pallas_call(
         kernel,
         grid=(per, steps),
-        in_specs=[SMEM_SPEC, rows(model), rows(model), rows(LANES)] + [ANY_SPEC] * groups,
-        out_specs=[rows(model), rows(model + LANES)] + [grad] * groups,
+        in_specs=[rows(model), rows(model), rows(LANES)] + [ANY_SPEC] * groups,
+        out_specs=[rows(model), rows(model + LANES)]
+        + [single if s == 1 else grad for s in range(groups)]
+        + [ANY_SPEC],
         out_shape=[
             jax.ShapeDtypeStruct((per, total, model), BF16),
             jax.ShapeDtypeStruct((per, total, model + LANES), BF16),
         ]
-        + [jax.ShapeDtypeStruct((per, 3, part, ff), BF16)] * groups,
+        + [
+            jax.ShapeDtypeStruct((3, part, ff) if s == 1 else (per, 3, part, ff), BF16)
+            for s in range(groups)
+        ]
+        + [jax.ShapeDtypeStruct((3, part, ff), BF16)],
         scratch_shapes=[
             pltpu.VMEM((model, 2 * ff), F32),
             pltpu.VMEM((ff, model), F32),
             pltpu.VMEM((per, model, 2 * ff), BF16),
             pltpu.VMEM((per, model, ff), BF16),
+            pltpu.VMEM((3, part, ff), BF16),
             pltpu.SemaphoreType.DMA((per, 3 * groups)),
+            pltpu.SemaphoreType.DMA((3,)),
+            pltpu.SemaphoreType.DMA((3,)),
+            pltpu.SemaphoreType.DMA,
+            pltpu.SemaphoreType.DMA,
         ],
-        compiler_params=pltpu.CompilerParams(vmem_limit_bytes=62 * 1024 * 1024),
+        compiler_params=params(7),
         cost_estimate=cost(18 * per * total * model * ff, 10 * per * total * model),
         name="expert_steps",
-    )(at, rows_in, grads_in, weights, bank, *far)
-    return out[0], out[1], list(out[2:])
+    )(rows_in, grads_in, weights, bank, *far)
+    return out[0], out[1], list(out[2 : 2 + groups]), out[2 + groups]
 
 
 def merge_grads(which, at, terms):
     per, _, part, ff = terms[0].shape
+    flat, places = [], []
+    for one in terms:
+        places.append(len(flat))
+        flat += one if isinstance(one, list) else [one]
     split = 2
     tile = LANES
 
     def kernel(at_ref, *refs):
-        ins, out = refs[: len(terms)], refs[len(terms)]
+        ins, out = refs[: len(flat)], refs[len(flat)]
         for k in range(per):
             for parity in range(split):
                 value = None
-                for one in ins[parity::split]:
-                    more = one[k, 0].astype(F32)
+                for s in range(parity, len(terms), split):
+                    whole = not isinstance(terms[s], list)
+                    more = ins[places[s]][k, 0] if whole else ins[places[s] + k][0]
+                    more = more.astype(F32)
                     value = more if value is None else value + more
                 index = lax.rem(at_ref[0] + parity, split) * per + k
                 out[index] = value.T if which == 2 else value
@@ -1973,12 +2044,17 @@
         kernel,
         grid=(part // tile,),
         in_specs=[SMEM_SPEC]
-        + [pl.BlockSpec((per, 1, tile, ff), lambda t: (0, which, t, 0))] * len(terms),
+        + [
+            pl.BlockSpec((per, 1, tile, ff), lambda t: (0, which, t, 0))
+            if one.ndim == 4
+            else pl.BlockSpec((1, tile, ff), lambda t: (which, t, 0))
+            for one in flat
+        ],
         out_specs=spec,
         out_shape=jax.ShapeDtypeStruct(shape, F32),
         cost_estimate=cost(1e8, 6e6),
         name="merge_grads",
-    )(at, *terms)
+    )(at, *flat)
 
 
 def layer_plane(
@@ -2073,10 +2149,12 @@
     )
     weights_far = [far_one, far_two, far_three]
     tile = 2 * micro * split * cap
-    outs, backs, weight_terms = expert_steps(
-        where, rows_in, grads_in, row_weights, bank, weights_far, experts, tile
+    outs, backs, weight_terms, one_early = expert_steps(
+        rows_in, grads_in, row_weights, bank, weights_far, experts, tile
     )
-    back, term_one = plane_return(backs, ranks, weight_terms[1], micro, count, cap)
+    back, one_late, three_early = plane_return(
+        backs, ranks, weight_terms[1], weight_terms[3], micro, count, cap
+    )
     back = back.reshape(rows, model + LANES)
 
     outs, back, late = lax.optimization_barrier((outs, back, weight_terms[2]))
@@ -2108,13 +2186,13 @@
     grad_one = jnp.sum(d_normed * x * inverse_one, axis=0)
     input_grad = (d_hidden + rms_back(x, inverse_one, gain_one, d_normed)).reshape(tokens.shape)
     gains = jnp.concatenate([grad_one[None], grad_two[None], jnp.zeros((6, model), F32)], axis=0)
-    dense, term_three = plane_gradients(
+    dense, three_late = plane_gradients(
         [(mixed, d_attn), (normed, d_project)], router_grad, gains, weight_terms[3], groups
     )
     mixture_sum, dense = lax.optimization_barrier((mixture_sum, dense))
     mixture = mixture_sum[:micro].astype(F32) + turn(mixture_sum[micro:], 1, split).astype(F32)
     block_out = (hidden + mixture.reshape(rows, model)).astype(BF16).reshape(tokens.shape)
-    terms = [weight_terms[0], term_one, term_two, term_three]
+    terms = [weight_terms[0], [one_early, one_late], term_two, [three_early, three_late]]
     gate_grad, up_grad, down_grad = [merge_grads(which, where, terms) for which in range(3)]
     misc_sum = dense[:, model + query_width + 2 * kv_width :].astype(F32)
     return (
@@ -2138,6 +2216,7 @@
         n == 8
         and exp_here % 2 == 0
         and groups == 4
+        and exp_here == 4
         and part % (16 * n) == 0
         and part % LANES == 0
         and arrays[0].shape[0] == 2

time: 772 us -> 747 us (0.968)
  Pallas kernels: 583 us -> 563 us
    pallas_call x1, Pallas kernels: 108 us -> 99 us  [plane_gradients(): pl.pallas_call(kernel, in_specs=[vmem] * (len(flat) + 2) + [ANY_SPEC], ou...]
    pallas_call x1, Pallas kernels: 78.6 us -> 70.8 us  [plane_dispatch(): pl.pallas_call(kernel, in_specs=[SMEM_SPEC, vmem, vmem, ANY_SPEC], out_sp...]
where the time goes in v5:
time: 747 us; the launch traced here: 737 us
  Pallas kernels  563 us (75%)
  waiting for transfers between devices  73.1 us (10%)
  other arithmetic  28.1 us (4%)
  matrix products  25.6 us (3%)
  local copies, waits for them, and re-layouts  18 us (2%)
  between operations  15 us (2%)
  starting transfers between devices  14.2 us (2%)
    pallas_call x1, Pallas kernels, plane_gradients(): pl.pallas_call(kernel, in_specs=[vmem] * (len(flat) + 2) + [ANY_SPEC], ou...  99 us
    pallas_call x1, Pallas kernels, plane_weights(): pl.pallas_call(kernel, in_specs=[vmem] * kinds + [ANY_SPEC], out_specs=[v...  90.6 us
    pallas_call x1, Pallas kernels, plane_return(): pl.pallas_call(kernel, in_specs=[vmem, vmem, ANY_SPEC, ANY_SPEC], out_spe...  77.1 us
    pallas_call x1, Pallas kernels, expert_steps(): pl.pallas_call(kernel, grid=(per, steps), in_specs=[rows(model), rows(mod...  72.3 us
    pallas_call x1, Pallas kernels, plane_dispatch(): pl.pallas_call(kernel, in_specs=[SMEM_SPEC, vmem, vmem, ANY_SPEC], out_sp...  70.8 us
    pallas_call x1, Pallas kernels, plane_attention_backward(): pl.pallas_call(kernel, in_specs=[vmem] * 5, out_specs=vmem, out_shape=jax...  69.1 us
    all_gather x1, waiting for transfers between devices, layer_plane(): d_slots = lax.all_gather(both, 'expert', axis=0)  59.8 us
    pallas_call x1, Pallas kernels, plane_attention(): pl.pallas_call(kernel, in_specs=[vmem] * 4, out_specs=[vmem] * 3, out_sha...  41 us
  transfers between devices with their start and end apart: 6, of which 2 were waited for; matrix products, arithmetic and copies ran while one was open for 8% of the time, Pallas kernels for 54%

profile of v5, /device:TPU:0, one launch (start us, length us, event | category | flops | bytes accessed | tf_op | source)
XLA Modules:
  0.0 737.2 jit_solution(4419970817410882004)
XLA Ops:
  8.3 2.0 concatenate.26
  10.3 3.1 collective-permute-start
  13.3 1.7 copy.55
  19.7 3.7 pad_maximum_fusion.refs_2_.bank_ref.refs_0_
  27.0 90.6 %plane_weights.1 = (bf16[1536,2560]{1,0:T(8,128)(2,1)}, bf16[1536,1664]{1,0:T(8,128)(2,1)}, bf16[2,3,384,512]{3,2,1,0:T(8,128)(2,1)}) custom-call(bf16[48,2560]{1,0:T(8,128)(2,1)} %constant_dynamic-slice_fusion.3.refs_0_, bf16[48,1664]{1,0:T(8,128)(2,1)} %pad_maximum_fusion.2.refs_1_, bf16[4,3,384,512]{3,2,1,0:T(8,128)(2,1)} %pad_maximum_fusion.refs_2_.bank_ref.refs_0_), custom_call_target="tpu_custom_call" | custom-call | flops 1000000000 | bytes 1000000 | tf_op jit(solution)/shard_map/plane_weights/pallas_call | solution.py:1223
  117.6 3.4 constant_dynamic-slice_fusion
  120.9 2.8 pad_maximum_fusion.1
  128.7 6.7 collective-permute-start.1
  135.4 41.0 %plane_attention.1 = (bf16[2,128,1536]{2,1,0:T(8,128)(2,1)}, bf16[2,128,1536]{2,1,0:T(8,128)(2,1)}, bf16[8,2,128,1024]{3,2,1,0:T(8,128)(2,1)}) custom-call(bf16[256,1536]{1,0:T(8,128)(2,1)} %fusion.16.x_ref.refs_2_, bf16[1536,2560]{1,0:T(8,128)(2,1)} %get-tuple-element.44.w_ref, f32[128,128]{1,0:T(8,128)} %get-tuple-element.148.cos_ref, ...), custom_call_target="tpu_custom_call" | custom-call | flops 1000000000 | bytes 1000000 | tf_op jit(solution)/shard_map/plane_attention/pallas_call | solution.py:1350
  176.4 4.3 multiply_reduce_fusion.2
  180.9 1.9 fusion.34
  184.2 59.8 %all-gather.3.cloned.1.call-done = bf16[32,128,1664]{2,1,0:T(8,128)(2,1)} async-done(((bf16[4,128,1664]{2,1,0:T(8,128)(2,1)}), bf16[32,128,1664]{2,1,0:T(8,128)(2,1)}) %all-gather.3.cloned.1.call-update) | async-done | bytes 13631504 | tf_op jit(solution)/shard_map/all_gather | solution.py:2116
  244.0 15.3 %gather_flags.1 = (bf16[2,1536,1536]{2,1,0:T(8,128)(2,1)}, f32[32,2,128]{2,1,0:T(2,128)}) custom-call(s32[4]{0:T(128)} %pad_add_fusion.at_ref, bf16[8,4,128,1664]{3,2,1,0:T(8,128)(2,1)} %bitcast.87), custom_call_target="tpu_custom_call" | custom-call | flops 5000000000 | bytes 30000000 | tf_op jit(solution)/shard_map/gather_flags/pallas_call | solution.py:1794
  259.3 70.8 %plane_dispatch.1 = (bf16[2,1536,1536]{2,1,0:T(8,128)(2,1)}, f32[2,1536,128]{2,1,0:T(8,128)}, bf16[1,3,384,512]{3,2,1,0:T(8,128)(2,1)}) custom-call(s32[4]{0:T(128)} %pad_add_fusion.at_ref, bf16[2,128,1664]{2,1,0:T(8,128)(2,1)} %bitcast.73, f32[32,2,128]{2,1,0:T(2,128)} %get-tuple-element.48.rank_ref, ...), custom_call_target="tpu_custom_call" | custom-call | flops 1000000000 | bytes 1000000 | tf_op jit(solution)/shard_map/plane_dispatch/pallas_call | solution.py:1539
  330.1 72.3 %expert_steps.1 = (bf16[2,1536,1536]{2,1,0:T(8,128)(2,1)}, bf16[2,1536,1664]{2,1,0:T(8,128)(2,1)}, bf16[2,3,384,512]{3,2,1,0:T(8,128)(2,1)}, bf16[3,384,512]{2,1...) custom-call(bf16[2,1536,1536]{2,1,0:T(8,128)(2,1)} %get-tuple-elemen, ...), custom_call_target="tpu_custom_call" | custom-call | flops 43486543872 | bytes 47185920 | tf_op jit(solution)/shard_map/expert_steps/pallas_call | solution.py:1980
  402.4 77.1 %plane_return.1 = (f32[2,128,1664]{2,1,0:T(8,128)}, bf16[3,384,512]{2,1,0:T(8,128)(2,1)}, bf16[3,384,512]{2,1,0:T(8,128)(2,1)}) custom-call(f32[32,2,128]{2,1,0:T(2,128)} %get-tuple-element.48.rank_ref, bf16[2,1536,1664]{2,1,0:T(8,128)(2,1)} %get-tuple-element.56.in_ref, bf16[3,384,512]{2,1,0:T(8,128)(2,1)} %get-tuple-element.57.next_ref, ...), custom_call_target="tpu_custom_call" | custom-call | flops 1000000000 | bytes 1000000 | tf_op jit(solution)/shard_map/plane_return/pallas_call | solution.py:1634
  479.5 14.0 %scatter_rows.1 = bf16[8,4,128,1536]{3,2,1,0:T(8,128)(2,1)} custom-call(s32[4]{0:T(128)} %pad_add_fusion.at_ref, f32[32,2,128]{2,1,0:T(2,128)} %get-tuple-element.48.rank_ref, bf16[2,1536,1536]{2,1,0:T(8,128)(2,1)} %get-tuple-element.61.in_ref), custom_call_target="tpu_custom_call" | custom-call | flops 5000000000 | bytes 30000000 | tf_op jit(solution)/shard_map/scatter_rows/pallas_call | solution.py:1833
  493.7 2.4 collective-permute-start.3
  497.2 3.0 multiply_reduce_fusion
  502.1 6.3 fusion.7
  508.5 69.1 %plane_attention_backward.1 = bf16[2,128,2560]{2,1,0:T(8,128)(2,1)} custom-call(bf16[2,128,1536]{2,1,0:T(8,128)(2,1)} %get-tuple-element.63.q_ref, bf16[2,128,1536]{2,1,0:T(8,128)(2,1)} %bitcast.80, bf16[8,2,128,1024]{3,2,1,0:T(8,128)(2,1)} %get-tuple-element.64.kv_ref, f32[128,128]{1,0:T(8,128)} %get-tuple-element.148.cos_ref, ...), custom_call_target="tpu_custom_call" | custom-call | flops 1000000000 | bytes 1000000 | tf_op jit(solution)/shard_map/plane_attention_backward/pallas_call | solution.py:1458
  577.6 7.2 fusion.13
  584.7 2.9 fusion.35.refs_4_
  588.4 99.0 %plane_gradients.1 = (bf16[384,4224]{1,0:T(8,128)(2,1)}, bf16[3,384,512]{2,1,0:T(8,128)(2,1)}) custom-call(bf16[256,1536]{1,0:T(8,128)(2,1)} %bitcast.82, bf16[256,1536]{1,0:T(8,128)(2,1)} %copy-done.13, bf16[256,1536]{1,0:T(8,128)(2,1)} %fusion.16.x_ref.refs_2_, bf16[256,2560]{1,0:T(8,128)(2,1)} %bitcast.72, f32[1536,32]{1,0:T(8,128)} %fusion.35.refs_4_, ...), custom_call_target="tpu_custom_call" | custom-call | flops 1000000000 | bytes 1000000 | tf_op jit(solution)/shard_map/plane_gradients/pallas_call | solution.py:1747
  687.9 4.9 merge_grads.5
  692.8 4.4 merge_grads.4
  697.3 4.7 merge_grads.3
  702.0 3.1 slice_convert_fusion.1
  707.0 2.0 collective-permute-start.2
  709.8 4.1 slice_convert_fusion
  713.9 13.2 %collective-permute-done.2 = bf16[2,128,1536]{2,1,0:T(8,128)(2,1)S(1)} collective-permute-done((bf16[2,128,1536]{2,1,0:T(8,128)(2,1)S(1)}, bf16[2,128,1536]{2,1,0:T(8,128)(2,1)S(1)}, u32[]{:S(2)}, u32[]{:S(2)}) %collective-permute-start.2) | collective-permute-done | bytes 786464 | tf_op jit(solution)/shard_map/ppermute | solution.py:44
  727.4 2.5 fusion.20
  (103 shorter events, 23.0 us)
Async XLA Ops:
  7.2 19.1 %copy-start = (bf16[384,2560]{1,0:T(8,128)(2,1)S(1)}, bf16[384,2560]{1,0:T(8,128)(2,1)}, u32[]{:S(2)}) copy-start(bf16[384,2560]{1,0:T(8,128)(2,1)} %param.15) | copy-start | bytes 5898244
  7.2 236.8 %all-gather.3.cloned.1.call-start = ((), (), s32[]{:S(2)}) async-start(), calls=%async_computation.2 | async-start | bytes 15335424 | tf_op jit(solution)/shard_map/all_gather | solution.py:2116
  10.3 110.7 %collective-permute-start = (bf16[2,128,1664]{2,1,0:T(8,128)(2,1)}, bf16[2,128,1664]{2,1,0:T(8,128)(2,1)}, u32[]{:S(2)}, u32[]{:S(2)}) collective-permute-start(bf16[2,128,1664]{2,1,0:T(8,128)(2,1)} %concatenate.26), channel_id=1, source_target_pairs={{8,0},{0,8},{24,16},{16,24},{9,1},{1,9},{25,17},{17,25},{10,2},{2,... | collective-permute-start | bytes 2555912 | tf_op jit(solution)/shard_map/ppermute | solution.py:44
  13.3 1.8 copy-start.23
  13.3 2.5 copy-start.24
  123.7 3.6 copy-start.6
  123.7 578.3 %reduce-scatter.2.cloned.1.call-start = ((), (), s32[]{:S(2)}) async-start(), calls=%async_computation.1 | async-start | bytes 14155776 | tf_op jit(solution)/shard_map/reduce_scatter | solution.py:2162
  127.5 450.0 %copy-start.20 = (f32[256]{0:T(256)}, f32[256]{0:T(256)S(1)}, u32[]{:S(2)}) copy-start(f32[256]{0:T(256)S(1)} %rsqrt_bitcast_fusion) | copy-start | bytes 3076
  128.7 201.4 %collective-permute-start.1 = (bf16[2,3,384,512]{3,2,1,0:T(8,128)(2,1)}, bf16[2,3,384,512]{3,2,1,0:T(8,128)(2,1)}, u32[]{:S(2)}, u32[]{:S(2)}) collective-permute-start(bf16[2,3,384,512]{3,2,1,0:T(8,128)(2,1)} %constant_dynamic-slice_fusion), channel_id=1, source_target_pairs={{0,16},{8,24},{16,0},{24,8},{1,17},{9,25},{17,1},{25,9},{2,18},{10... | collective-permute-start | bytes 7077896 | tf_op jit(solution)/shard_map/ppermute | solution.py:39
  180.6 319.7 %copy-start.2 = (f32[256,1536]{1,0:T(8,128)}, f32[256,1536]{1,0:T(8,128)S(1)}, u32[]{:S(2)}) copy-start(f32[256,1536]{1,0:T(8,128)S(1)} %get-tuple-element.143) | copy-start | bytes 4718596
  180.7 319.7 %copy-start.16 = (f32[256]{0:T(256)}, f32[256]{0:T(256)S(1)}, u32[]{:S(2)}) copy-start(f32[256]{0:T(256)S(1)} %add_rsqrt_fusion) | copy-start | bytes 3076
  180.9 3.3 copy-start.9
  493.7 194.3 %collective-permute-start.3 = (bf16[2,3,384,512]{3,2,1,0:T(8,128)(2,1)}, bf16[2,3,384,512]{3,2,1,0:T(8,128)(2,1)}, u32[]{:S(2)}, u32[]{:S(2)}) collective-permute-start(bf16[2,3,384,512]{3,2,1,0:T(8,128)(2,1)} %get-tuple-element.71), channel_id=1, source_target_pairs={{0,16},{8,24},{16,0},{24,8},{1,17},{9,25},{17,1},{25,9},{2,18},{10... | collective-permute-start | bytes 7077896 | tf_op jit(solution)/shard_map/ppermute | solution.py:39
  497.2 4.2 copy-start.11
  500.3 1.2 copy-start.4
  500.3 1.8 copy-start.18
  502.1 6.4 copy-start.13
  508.5 69.1 %copy-start.7 = (bf16[2,128,1536]{2,1,0:T(8,128)(2,1)S(1)}, bf16[2,128,1536]{2,1,0:T(8,128)(2,1)}, u32[]{:S(2)}) copy-start(bf16[2,128,1536]{2,1,0:T(8,128)(2,1)} %param.11) | copy-start | bytes 2359300
  577.6 7.2 copy-start.10
  702.0 5.0 copy-start.15
  707.0 20.1 %collective-permute-start.2 = (bf16[2,128,1536]{2,1,0:T(8,128)(2,1)S(1)}, bf16[2,128,1536]{2,1,0:T(8,128)(2,1)S(1)}, u32[]{:S(2)}, u32[]{:S(2)}) collective-permute-start(bf16[2,128,1536]{2,1,0:T(8,128)(2,1)S(1)} %slice.57), channel_id=1, source_target_pairs={{8,0},{0,8},{24,16},{16,24},{9,1},{1,9},{25,17},{17,25},{10,2},{2,... | collective-permute-start | bytes 2359304 | tf_op jit(solution)/shard_map/ppermute | solution.py:44
  709.8 17.6 %copy-start.8 = (bf16[2,128,1536]{2,1,0:T(8,128)(2,1)S(1)}, bf16[2,128,1536]{2,1,0:T(8,128)(2,1)}, u32[]{:S(2)}) copy-start(bf16[2,128,1536]{2,1,0:T(8,128)(2,1)} %param.11) | copy-start | bytes 2359300
  709.8 17.6 %copy-start.12 = (bf16[2,128,1536]{2,1,0:T(8,128)(2,1)S(1)}, bf16[2,128,1536]{2,1,0:T(8,128)(2,1)}, u32[]{:S(2)}) copy-start(bf16[2,128,1536]{2,1,0:T(8,128)(2,1)} %param.12) | copy-start | bytes 2359300
  709.8 17.6 %copy-start.14 = (f32[256,1536]{1,0:T(8,128)S(1)}, f32[256,1536]{1,0:T(8,128)}, u32[]{:S(2)}) copy-start(f32[256,1536]{1,0:T(8,128)} %get-tuple-element.147) | copy-start | bytes 4718596
  709.8 17.6 %copy-start.19 = (f32[256]{0:T(256)S(1)}, f32[256]{0:T(256)}, u32[]{:S(2)}) copy-start(f32[256]{0:T(256)} %copy-done.18) | copy-start | bytes 3076
  709.8 17.6 %copy-start.21 = (f32[256]{0:T(256)S(1)}, f32[256]{0:T(256)}, u32[]{:S(2)}) copy-start(f32[256]{0:T(256)} %copy-done.20) | copy-start | bytes 3076
  709.8 17.6 %copy-start.22 = (f32[256]{0:T(256)S(1)}, f32[256]{0:T(256)}, u32[]{:S(2)}) copy-start(f32[256]{0:T(256)} %broadcast_multiply_fusion) | copy-start | bytes 3076
  713.9 13.5 %copy-start.3 = (f32[256,1536]{1,0:T(8,128)S(1)}, f32[256,1536]{1,0:T(8,128)}, u32[]{:S(2)}) copy-start(f32[256,1536]{1,0:T(8,128)} %copy-done.2) | copy-start | bytes 4718596
  713.9 13.5 %copy-start.5 = (f32[256,1536]{1,0:T(8,128)S(1)}, f32[256,1536]{1,0:T(8,128)}, u32[]{:S(2)}) copy-start(f32[256,1536]{1,0:T(8,128)} %copy-done.4) | copy-start | bytes 4718596
  713.9 13.5 %copy-start.17 = (f32[256]{0:T(256)S(1)}, f32[256]{0:T(256)}, u32[]{:S(2)}) copy-start(f32[256]{0:T(256)} %copy-done.16) | copy-start | bytes 3076
  727.4 2.5 copy-start.1
Sparse Core Ops, SparseCore 0:
  123.8 120.1 all-gather.2
  493.7 109.2 reduce-scatter.1

commit v6 on v5

--- a/solution.py
+++ b/solution.py
@@ -1656,7 +1656,7 @@
     )(ranks, rows, next_term, last_terms)
 
 
-def plane_gradients(products, router, gains, terms, groups):
+def plane_gradients(products, router, gains, terms, swapped, groups):
     n = 8
     depth = products[0][0].shape[1]
     widths = [b.shape[1] for a, b in products]
@@ -1668,9 +1668,9 @@
 
     def kernel(*refs):
         ins, refs = refs[: len(flat)], refs[len(flat) :]
-        router_ref, gains_ref, term_ref, out, far_ref, *refs = refs
-        wide, parts, z_out, z_in, z_send, z_recv, send, recv, t_send, t_recv = refs[:10]
-        scratch = refs[10:]
+        router_ref, gains_ref, term_ref, swap_ref, out, far_ref, swap_far, *refs = refs
+        wide, parts, z_out, z_in, z_send, z_recv, send, recv, t_send, t_recv, s_send, s_recv = refs[:12]
+        scratch = refs[12:]
         e, z = lax.axis_index("expert"), lax.axis_index("group")
         red = Reduce(e, lambda r, c: parts.at[r, c], [c % 2 for c in range(groups)], *scratch)
         greet(
@@ -1680,6 +1680,8 @@
         follow = remote(
             term_ref.at[1], far_ref, t_send, t_recv, {"group": lax.rem(z + groups - 1, groups)}
         )
+        exchange = remote(swap_ref, swap_far, s_send, s_recv, {"group": partner(z)})
+        exchange.start()
         follow.start()
 
         def cut(lo, size):
@@ -1738,6 +1740,7 @@
         for c in range(2):
             gather.finish(c)
         follow.wait()
+        exchange.wait()
         for c in range(1, groups):
             far(c).wait_send()
         for c in chunks:
@@ -1746,11 +1749,12 @@
     vmem = pl.BlockSpec(memory_space=pltpu.VMEM)
     return pl.pallas_call(
         kernel,
-        in_specs=[vmem] * (len(flat) + 2) + [ANY_SPEC],
-        out_specs=[vmem, ANY_SPEC],
+        in_specs=[vmem] * (len(flat) + 2) + [ANY_SPEC] * 2,
+        out_specs=[vmem, ANY_SPEC, ANY_SPEC],
         out_shape=[
             jax.ShapeDtypeStruct((n * rows, width), BF16),
             jax.ShapeDtypeStruct(terms.shape[1:], BF16),
+            jax.ShapeDtypeStruct(swapped.shape, BF16),
         ],
         scratch_shapes=[
             pltpu.VMEM((depth, tile), F32),
@@ -1763,23 +1767,27 @@
             pltpu.SemaphoreType.DMA((n, 2)),
             pltpu.SemaphoreType.DMA,
             pltpu.SemaphoreType.DMA,
+            pltpu.SemaphoreType.DMA,
+            pltpu.SemaphoreType.DMA,
         ]
         + reduce_scratch(groups, rows, width),
         compiler_params=params(6),
         cost_estimate=cost(1e9, 1e6),
         name="plane_gradients",
-    )(*flat, router, gains, terms)
-
-
-def gather_flags(slots, where, per, cap, model):
-    n, count, tokens, width = slots.shape
-
-    def kernel(at_ref, in_ref, out, ranks, flags):
+    )(*flat, router, gains, terms, swapped)
+
+
+def gather_flags(halves, where, per, cap, model):
+    n, each, tokens, width = halves[0].shape
+    count = each * len(halves)
+
+    def kernel(at_ref, *refs):
+        ins, (out, ranks, flags) = refs[: len(halves)], refs[len(halves) :]
         row = lax.broadcasted_iota(jnp.int32, (tokens, tokens), 0)
         col = lax.broadcasted_iota(jnp.int32, (tokens, tokens), 1)
         before = jnp.where(row < col, 1.0, 0.0).astype(BF16)
         for b in range(count):
-            payload = in_ref[0, b]
+            payload = ins[b // each][0, b % each]
             flags[...] = payload[:, model:].astype(F32).T
             picked = jnp.concatenate(
                 [flags[pl.ds(at_ref[2] + k, 1), :] for k in range(per)], axis=0
@@ -1798,10 +1806,11 @@
             grid=(n,),
             in_specs=[
                 pl.BlockSpec(
-                    (1, count, tokens, width),
+                    (1, each, tokens, width),
                     lambda r, at: (jnp.bitwise_xor(at[1], r), 0, 0, 0),
                 )
-            ],
+            ]
+            * len(halves),
             out_specs=[
                 pl.BlockSpec((per, count * cap, model), lambda r, at: (0, r, 0)),
                 pl.BlockSpec((count, per, tokens), lambda r, at: (r, 0, 0)),
@@ -1814,13 +1823,15 @@
         ],
         cost_estimate=cost(5e9, 3e7),
         name="gather_flags",
-    )(where, slots)
+    )(where, *halves)
 
 
 def scatter_rows(rows, ranks, where, n, count, tokens, cap):
     per, _, width = rows.shape
 
-    def kernel(at_ref, rank_ref, in_ref, out):
+    half = count // 2
+
+    def kernel(at_ref, rank_ref, in_ref, *outs):
         for b in range(count):
             total = None
             for k in range(per):
@@ -1828,7 +1839,7 @@
                     pick(rank_ref[b, k : k + 1, :], cap), in_ref[k, b * cap : (b + 1) * cap, :], TN
                 )
                 total = one if total is None else total + one
-            out[0, b] = total.astype(BF16)
+            outs[b // half][0, b % half] = total.astype(BF16)
 
     return pl.pallas_call(
         kernel,
@@ -1839,11 +1850,14 @@
                 pl.BlockSpec((count, per, tokens), lambda r, at: (r, 0, 0)),
                 pl.BlockSpec((per, count * cap, width), lambda r, at: (0, r, 0)),
             ],
-            out_specs=pl.BlockSpec(
-                (1, count, tokens, width), lambda r, at: (jnp.bitwise_xor(at[1], r), 0, 0, 0)
-            ),
+            out_specs=[
+                pl.BlockSpec(
+                    (1, half, tokens, width), lambda r, at: (jnp.bitwise_xor(at[1], r), 0, 0, 0)
+                )
+            ]
+            * 2,
         ),
-        out_shape=jax.ShapeDtypeStruct((n, count, tokens, width), BF16),
+        out_shape=[jax.ShapeDtypeStruct((n, half, tokens, width), BF16)] * 2,
         cost_estimate=cost(5e9, 3e7),
         name="scatter_rows",
     )(where, ranks, rows)
@@ -2105,15 +2119,13 @@
     pad = jnp.zeros((micro, count, LANES - experts), BF16)
     d_payload = jnp.concatenate([cotangent, named.astype(BF16), pad], axis=2)
     d_turned = turn(d_payload, 1, split)
+    d_near = lax.all_gather(d_payload, "expert", axis=0)
 
     bank_two = lax.dynamic_slice_in_dim(bank, (z % split) * per, per, axis=0)
     qkv_full, rest_full, far_one = plane_weights(shares, bank, per)
-    (bank_two, d_payload, d_turned), qkv_full = lax.optimization_barrier(
-        ((bank_two, d_payload, d_turned), qkv_full)
-    )
+    (bank_two, d_turned), qkv_full = lax.optimization_barrier(((bank_two, d_turned), qkv_full))
     far_two = shift(bank_two, 2)
-    both = jnp.concatenate([d_payload, d_turned], axis=0)
-    d_slots = lax.all_gather(both, "expert", axis=0)
+    d_slots = [d_near, lax.all_gather(d_turned, "expert", axis=0)]
     out_full, misc_full = rest_full[:, :model], rest_full[:, model:]
     gain_one = misc_full[:, 0].astype(F32)
     gain_two = misc_full[:, 1].astype(F32)
@@ -2148,7 +2160,7 @@
         payload, ranks, bank, where, per, cap, model, experts
     )
     weights_far = [far_one, far_two, far_three]
-    tile = 2 * micro * split * cap
+    tile = 512 if rows_in.shape[1] % 512 == 0 else 2 * micro * split * cap
     outs, backs, weight_terms, one_early = expert_steps(
         rows_in, grads_in, row_weights, bank, weights_far, experts, tile
     )
@@ -2158,8 +2170,9 @@
     back = back.reshape(rows, model + LANES)
 
     outs, back, late = lax.optimization_barrier((outs, back, weight_terms[2]))
-    mixture_parts = scatter_rows(outs, ranks, where, n, micro * split, count, cap)
-    mixture_sum = lax.psum_scatter(mixture_parts, "expert", scatter_dimension=0, tiled=False)
+    parts_near, parts_far = scatter_rows(outs, ranks, where, n, micro * split, count, cap)
+    mixture_far = lax.psum_scatter(parts_far, "expert", scatter_dimension=0, tiled=False)
+    mixture_near = lax.psum_scatter(parts_near, "expert", scatter_dimension=0, tiled=False)
     term_two = shift(late, 2)
 
     d_out = cotangent.reshape(rows, model).astype(F32)
@@ -2186,11 +2199,11 @@
     grad_one = jnp.sum(d_normed * x * inverse_one, axis=0)
     input_grad = (d_hidden + rms_back(x, inverse_one, gain_one, d_normed)).reshape(tokens.shape)
     gains = jnp.concatenate([grad_one[None], grad_two[None], jnp.zeros((6, model), F32)], axis=0)
-    dense, three_late = plane_gradients(
-        [(mixed, d_attn), (normed, d_project)], router_grad, gains, weight_terms[3], groups
+    term_two, gains = lax.optimization_barrier((term_two, gains))
+    dense, three_late, mixture_far = plane_gradients(
+        [(mixed, d_attn), (normed, d_project)], router_grad, gains, weight_terms[3], mixture_far, groups
     )
-    mixture_sum, dense = lax.optimization_barrier((mixture_sum, dense))
-    mixture = mixture_sum[:micro].astype(F32) + turn(mixture_sum[micro:], 1, split).astype(F32)
+    mixture = mixture_near.astype(F32) + mixture_far.astype(F32)
     block_out = (hidden + mixture.reshape(rows, model)).astype(BF16).reshape(tokens.shape)
     terms = [weight_terms[0], [one_early, one_late], term_two, [three_early, three_late]]
     gate_grad, up_grad, down_grad = [merge_grads(which, where, terms) for which in range(3)]

time: 747 us -> 720 us (0.964)
  waiting for transfers between devices: 73.1 us -> 42.5 us
    all_gather x1 -> x2, waiting for transfers between devices: 59.8 us -> 22.1 us  [the longest x1 22.1 us: layer_plane(): d_slots = [d_near, lax.all_gather(d_turned, 'expert', axis=0)]]
    ppermute x2, waiting for transfers between devices: 0.01 us -> 19.8 us  [shift(): return lax.ppermute(x, 'group', [(i, (i + step) % n) for i in range(n)])]
    pallas_call x1, Pallas kernels: 70.8 us -> 84.1 us  [plane_dispatch(): pl.pallas_call(kernel, in_specs=[SMEM_SPEC, vmem, vmem, ANY_SPEC], out_sp...]
    ppermute x2 -> x1, waiting for transfers between devices: 13.2 us -> 0.01 us  [turn(): lax.ppermute(x, 'group', [(i // split * split + (i + step) % split, i) fo...]
    pallas_call x1, Pallas kernels: 99 us -> 109 us  [plane_gradients(): pl.pallas_call(kernel, in_specs=[vmem] * (len(flat) + 2) + [ANY_SPEC] * 2...]
  transfers between devices with their start and end apart: 6 -> 7, of which waited for: 2 -> 2; matrix products, arithmetic and copies ran while one was open for 8% -> 8% of each run, Pallas kernels for 54% -> 58%
where the time goes in v6:
time: 720 us; the launch traced here: 710 us
  Pallas kernels  569 us (79%)
  waiting for transfers between devices  42.5 us (6%)
  other arithmetic  26.6 us (4%)
  matrix products  21.6 us (3%)
  local copies, waits for them, and re-layouts  21.3 us (3%)
  starting transfers between devices  14.8 us (2%)
  between operations  14.6 us (2%)
    pallas_call x1, Pallas kernels, plane_gradients(): pl.pallas_call(kernel, in_specs=[vmem] * (len(flat) + 2) + [ANY_SPEC] * 2...  109 us
    pallas_call x1, Pallas kernels, plane_weights(): pl.pallas_call(kernel, in_specs=[vmem] * kinds + [ANY_SPEC], out_specs=[v...  88.2 us
    pallas_call x1, Pallas kernels, plane_dispatch(): pl.pallas_call(kernel, in_specs=[SMEM_SPEC, vmem, vmem, ANY_SPEC], out_sp...  84.1 us
    pallas_call x1, Pallas kernels, plane_return(): pl.pallas_call(kernel, in_specs=[vmem, vmem, ANY_SPEC, ANY_SPEC], out_spe...  76.5 us
    pallas_call x1, Pallas kernels, expert_steps(): pl.pallas_call(kernel, grid=(per, steps), in_specs=[rows(model), rows(mod...  65.8 us
    pallas_call x1, Pallas kernels, plane_attention_backward(): pl.pallas_call(kernel, in_specs=[vmem] * 5, out_specs=vmem, out_shape=jax...  61.7 us
    pallas_call x1, Pallas kernels, plane_attention(): pl.pallas_call(kernel, in_specs=[vmem] * 4, out_specs=[vmem] * 3, out_sha...  41.1 us
    all_gather x1, waiting for transfers between devices, layer_plane(): d_slots = [d_near, lax.all_gather(d_turned, 'expert', axis=0)]  22.1 us
  transfers between devices with their start and end apart: 7, of which 2 were waited for; matrix products, arithmetic and copies ran while one was open for 8% of the time, Pallas kernels for 58%

profile of v6, /device:TPU:0, one launch (start us, length us, event | category | flops | bytes accessed | tf_op | source)
XLA Modules:
  0.0 710.0 jit_solution(3140080423048436868)
XLA Ops:
  8.3 2.0 concatenate.23
  10.3 3.1 collective-permute-start
  13.5 1.7 copy.55
  19.5 2.0 concatenate.21
  21.5 1.6 constant_dynamic-slice_fusion.2
  23.1 3.8 pad_maximum_fusion.refs_2_.bank_ref.refs_0_
  29.9 88.2 %plane_weights.1 = (bf16[1536,2560]{1,0:T(8,128)(2,1)}, bf16[1536,1664]{1,0:T(8,128)(2,1)}, bf16[2,3,384,512]{3,2,1,0:T(8,128)(2,1)}) custom-call(bf16[48,2560]{1,0:T(8,128)(2,1)} %constant_dynamic-slice_fusion.3.refs_0_, bf16[48,1664]{1,0:T(8,128)(2,1)} %pad_maximum_fusion.1.refs_1_, bf16[4,3,384,512]{3,2,1,0:T(8,128)(2,1)} %pad_maximum_fusion.refs_2_.bank_ref.refs_0_), custom_call_target="tpu_custom_call" | custom-call | flops 1000000000 | bytes 1000000 | tf_op jit(solution)/shard_map/plane_weights/pallas_call | solution.py:1223
  118.1 3.4 constant_dynamic-slice_fusion
  126.5 9.0 %collective-permute-start.1 = (bf16[2,3,384,512]{3,2,1,0:T(8,128)(2,1)}, bf16[2,3,384,512]{3,2,1,0:T(8,128)(2,1)}, u32[]{:S(2)}, u32[]{:S(2)}) collective-permute-start(bf16[2,3,384,512]{3,2,1,0:T(8,128)(2,1)} %constant_dynamic-slice_fusion), channel_id=1, source_target_pairs={{0,16},{8,24},{16,0},{24,8},{1,17},{9,25},{17,1},{25,9},{2,18},{10... | collective-permute-start | bytes 7077896 | tf_op jit(solution)/shard_map/ppermute | solution.py:39
  135.5 41.1 %plane_attention.1 = (bf16[2,128,1536]{2,1,0:T(8,128)(2,1)}, bf16[2,128,1536]{2,1,0:T(8,128)(2,1)}, bf16[8,2,128,1024]{3,2,1,0:T(8,128)(2,1)}) custom-call(bf16[256,1536]{1,0:T(8,128)(2,1)} %fusion.16.x_ref.refs_2_, bf16[1536,2560]{1,0:T(8,128)(2,1)} %get-tuple-element.46.w_ref, f32[128,128]{1,0:T(8,128)} %get-tuple-element.152.cos_ref, ...), custom_call_target="tpu_custom_call" | custom-call | flops 1000000000 | bytes 1000000 | tf_op jit(solution)/shard_map/plane_attention/pallas_call | solution.py:1350
  176.7 4.3 multiply_reduce_fusion.2
  181.2 1.9 fusion.34
  184.5 22.1 %all-gather.7.cloned.1.call-done = bf16[16,128,1664]{2,1,0:T(8,128)(2,1)} async-done(((bf16[2,128,1664]{2,1,0:T(8,128)(2,1)}), bf16[16,128,1664]{2,1,0:T(8,128)(2,1)}) %all-gather.7.cloned.1.call-update) | async-done | bytes 6815760 | tf_op jit(solution)/shard_map/all_gather | solution.py:2128
  206.6 15.2 %gather_flags.1 = (bf16[2,1536,1536]{2,1,0:T(8,128)(2,1)}, f32[32,2,128]{2,1,0:T(2,128)}) custom-call(s32[4]{0:T(128)} %pad_add_fusion.at_ref, bf16[8,2,128,1664]{3,2,1,0:T(8,128)(2,1)} %bitcast.92, bf16[8,2,128,1664]{3,2,1,0:T(8,128)(2,1)} %bitcast.93), custom_call_target="tpu_custom_call" | custom-call | flops 5000000000 | bytes 30000000 | tf_op jit(solution)/shard_map/gather_flags/pallas_call | solution.py:1802
  221.8 84.1 %plane_dispatch.1 = (bf16[2,1536,1536]{2,1,0:T(8,128)(2,1)}, f32[2,1536,128]{2,1,0:T(8,128)}, bf16[1,3,384,512]{3,2,1,0:T(8,128)(2,1)}) custom-call(s32[4]{0:T(128)} %pad_add_fusion.at_ref, bf16[2,128,1664]{2,1,0:T(8,128)(2,1)} %bitcast.77, f32[32,2,128]{2,1,0:T(2,128)} %get-tuple-element.49.rank_ref, ...), custom_call_target="tpu_custom_call" | custom-call | flops 1000000000 | bytes 1000000 | tf_op jit(solution)/shard_map/plane_dispatch/pallas_call | solution.py:1539
  305.8 65.8 %expert_steps.1 = (bf16[2,1536,1536]{2,1,0:T(8,128)(2,1)}, bf16[2,1536,1664]{2,1,0:T(8,128)(2,1)}, bf16[2,3,384,512]{3,2,1,0:T(8,128)(2,1)}, bf16[3,384,512]{2,1...) custom-call(bf16[2,1536,1536]{2,1,0:T(8,128)(2,1)} %get-tuple-elemen, ...), custom_call_target="tpu_custom_call" | custom-call | flops 43486543872 | bytes 47185920 | tf_op jit(solution)/shard_map/expert_steps/pallas_call | solution.py:1994
  371.7 76.5 %plane_return.1 = (f32[2,128,1664]{2,1,0:T(8,128)}, bf16[3,384,512]{2,1,0:T(8,128)(2,1)}, bf16[3,384,512]{2,1,0:T(8,128)(2,1)}) custom-call(f32[32,2,128]{2,1,0:T(2,128)} %get-tuple-element.49.rank_ref, bf16[2,1536,1664]{2,1,0:T(8,128)(2,1)} %get-tuple-element.57.in_ref, bf16[3,384,512]{2,1,0:T(8,128)(2,1)} %get-tuple-element.58.next_ref, ...), custom_call_target="tpu_custom_call" | custom-call | flops 1000000000 | bytes 1000000 | tf_op jit(solution)/shard_map/plane_return/pallas_call | solution.py:1634
  448.1 13.0 %scatter_rows.1 = (bf16[8,2,128,1536]{3,2,1,0:T(8,128)(2,1)}, bf16[8,2,128,1536]{3,2,1,0:T(8,128)(2,1)}) custom-call(s32[4]{0:T(128)} %pad_add_fusion.at_ref, f32[32,2,128]{2,1,0:T(2,128)} %get-tuple-element.49.rank_ref, bf16[2,1536,1536]{2,1,0:T(8,128)(2,1)} %get-tuple-element.62.in_ref), custom_call_target="tpu_custom_call" | custom-call | flops 5000000000 | bytes 30000000 | tf_op jit(solution)/shard_map/scatter_rows/pallas_call | solution.py:1844
  461.8 2.4 collective-permute-start.2
  465.5 3.1 multiply_reduce_fusion
  470.4 2.3 fusion.7
  472.7 61.7 %plane_attention_backward.1 = bf16[2,128,2560]{2,1,0:T(8,128)(2,1)} custom-call(bf16[2,128,1536]{2,1,0:T(8,128)(2,1)} %get-tuple-element.65.q_ref, bf16[2,128,1536]{2,1,0:T(8,128)(2,1)} %bitcast.85, bf16[8,2,128,1024]{3,2,1,0:T(8,128)(2,1)} %get-tuple-element.66.kv_ref, f32[128,128]{1,0:T(8,128)} %get-tuple-element.152.cos_ref, ...), custom_call_target="tpu_custom_call" | custom-call | flops 1000000000 | bytes 1000000 | tf_op jit(solution)/shard_map/plane_attention_backward/pallas_call | solution.py:1458
  534.5 7.2 %fusion.13 = (f32[256]{0:T(256)S(1)}, f32[1536]{0:T(1024)S(1)}, f32[256,1536]{1,0:T(8,128)}) fusion(bf16[2,128,1536]{2,1,0:T(8,128)(2,1)S(1)} %copy-done.7, f32[1536]{0:T(1024)S(1)} %get-tuple-element.129, f32[256]{0:T(256)S(1)} %rsqrt_bitcast_fusion, bf16[256,2560]{1,0:T(8,128)(2,1)} %bitcast.75, bf16[1536,2560]{1,0:T(8,128)(2,1)} %get-tuple-element.46.w_ref), kind=kOutput, calls=%fused_computation.18 | convolution fusion | flops 2016016640 | bytes 11548672 | tf_op jit(solution)/shard_map/dot_general | solution.py:29
  542.2 3.0 fusion.35.refs_4_
  545.9 19.8 %collective-permute-done.2.refs_3_ = bf16[2,3,384,512]{3,2,1,0:T(8,128)(2,1)} collective-permute-done((bf16[2,3,384,512]{3,2,1,0:T(8,128)(2,1)}, bf16[2,3,384,512]{3,2,1,0:T(8,128)(2,1)}, u32[]{:S(2)}, u32[]{:S(2)}) %collective-permute-start.2) | collective-permute-done | bytes 2359328 | tf_op jit(solution)/shard_map/ppermute | solution.py:39
  565.7 109.3 %plane_gradients.1 = (bf16[384,4224]{1,0:T(8,128)(2,1)}, bf16[3,384,512]{2,1,0:T(8,128)(2,1)}, bf16[2,128,1536]{2,1,0:T(8,128)(2,1)}) custom-call(bf16[256,1536]{1,0:T(8,128)(2,1)} %bitcast.82, bf16[256,1536]{1,0:T(8,128)(2,1)} %copy-done.14, bf16[256,1536]{1,0:T(8,128)(2,1)} %fusion.16.x_ref.refs_2_, bf16[256,2560]{1,0:T(8,128)(2,1)} %bitcast.76, ...), custom_call_target="tpu_custom_call" | custom-call | flops 1000000000 | bytes 1000000 | tf_op jit(solution)/shard_map/plane_gradients/pallas_call | solution.py:1750
  676.7 4.9 merge_grads.5
  681.6 4.4 merge_grads.4
  686.1 4.4 merge_grads.3
  691.3 3.1 slice_convert_fusion.1
  694.5 2.4 slice_convert_fusion
  699.0 4.1 fusion.20
  (104 shorter events, 24.6 us)
Async XLA Ops:
  7.2 22.0 %copy-start = (bf16[384,2560]{1,0:T(8,128)(2,1)S(1)}, bf16[384,2560]{1,0:T(8,128)(2,1)}, u32[]{:S(2)}) copy-start(bf16[384,2560]{1,0:T(8,128)(2,1)} %param.15) | copy-start | bytes 5898244
  7.2 177.3 %all-gather.5.cloned.1.call-start = ((), (), s32[]{:S(2)}) async-start(), calls=%async_computation.4 | async-start | bytes 7667712 | tf_op jit(solution)/shard_map/all_gather | solution.py:2122
  10.3 196.3 %all-gather.7.cloned.1.call-start = ((), (), s32[]{:S(2)}) async-start(), calls=%async_computation.5 | async-start | bytes 7667712 | tf_op jit(solution)/shard_map/all_gather | solution.py:2128
  10.3 111.2 %collective-permute-start = (bf16[2,128,1664]{2,1,0:T(8,128)(2,1)}, bf16[2,128,1664]{2,1,0:T(8,128)(2,1)}, u32[]{:S(2)}, u32[]{:S(2)}) collective-permute-start(bf16[2,128,1664]{2,1,0:T(8,128)(2,1)} %concatenate.23), channel_id=1, source_target_pairs={{8,0},{0,8},{24,16},{16,24},{9,1},{1,9},{25,17},{17,25},{10,2},{2,... | collective-permute-start | bytes 2555912 | tf_op jit(solution)/shard_map/ppermute | solution.py:44
  13.4 1.8 copy-start.20
  13.5 2.5 copy-start.21
  121.5 3.6 copy-start.6
  121.5 444.2 %reduce-scatter.5.cloned.1.call-start = ((), (), s32[]{:S(2)}) async-start(), calls=%async_computation.3 | async-start | bytes 7077888 | tf_op jit(solution)/shard_map/reduce_scatter | solution.py:2174
  125.4 409.1 %copy-start.19 = (f32[256]{0:T(256)}, f32[256]{0:T(256)S(1)}, u32[]{:S(2)}) copy-start(f32[256]{0:T(256)S(1)} %rsqrt_bitcast_fusion) | copy-start | bytes 3076
  126.5 179.3 %collective-permute-start.1 = (bf16[2,3,384,512]{3,2,1,0:T(8,128)(2,1)}, bf16[2,3,384,512]{3,2,1,0:T(8,128)(2,1)}, u32[]{:S(2)}, u32[]{:S(2)}) collective-permute-start(bf16[2,3,384,512]{3,2,1,0:T(8,128)(2,1)} %constant_dynamic-slice_fusion), channel_id=1, source_target_pairs={{0,16},{8,24},{16,0},{24,8},{1,17},{9,25},{17,1},{25,9},{2,18},{10... | collective-permute-start | bytes 7077896 | tf_op jit(solution)/shard_map/ppermute | solution.py:39
  180.9 287.7 %copy-start.2 = (f32[256,1536]{1,0:T(8,128)}, f32[256,1536]{1,0:T(8,128)S(1)}, u32[]{:S(2)}) copy-start(f32[256,1536]{1,0:T(8,128)S(1)} %get-tuple-element.147) | copy-start | bytes 4718596
  180.9 287.7 %copy-start.16 = (f32[256]{0:T(256)}, f32[256]{0:T(256)S(1)}, u32[]{:S(2)}) copy-start(f32[256]{0:T(256)S(1)} %add_rsqrt_fusion) | copy-start | bytes 3076
  181.2 3.3 copy-start.9
  461.2 235.7 %reduce-scatter.3.cloned.1.call-start = ((), (), s32[]{:S(2)}) async-start(), calls=%async_computation.2 | async-start | bytes 7077888 | tf_op jit(solution)/shard_map/reduce_scatter | solution.py:2175
  461.2 9.1 %slice-start = ((s8[5111808]{0:T(1024)(128)(4,1)}), s8[917504]{0:T(1024)(128)(4,1)S(1)}, s32[]{:S(2)}) async-start(s8[5111808]{0:T(1024)(128)(4,1)} %bitcast.87), calls=%async_computation.6 | async-start | bytes 1835008
  461.8 103.9 %collective-permute-start.2 = (bf16[2,3,384,512]{3,2,1,0:T(8,128)(2,1)}, bf16[2,3,384,512]{3,2,1,0:T(8,128)(2,1)}, u32[]{:S(2)}, u32[]{:S(2)}) collective-permute-start(bf16[2,3,384,512]{3,2,1,0:T(8,128)(2,1)} %get-tuple-element.67), channel_id=1, source_target_pairs={{0,16},{8,24},{16,0},{24,8},{1,17},{9,25},{17,1},{25,9},{2,18},{10... | collective-permute-start | bytes 7077896 | tf_op jit(solution)/shard_map/ppermute | solution.py:39
  465.4 4.3 copy-start.11
  465.4 4.9 slice-start.1
  468.6 1.2 copy-start.4
  468.6 1.8 copy-start.18
  470.4 2.3 copy-start.14
  472.7 61.8 %copy-start.7 = (bf16[2,128,1536]{2,1,0:T(8,128)(2,1)S(1)}, bf16[2,128,1536]{2,1,0:T(8,128)(2,1)}, u32[]{:S(2)}) copy-start(bf16[2,128,1536]{2,1,0:T(8,128)(2,1)} %param.11) | copy-start | bytes 2359300
  534.5 7.8 %copy-start.10 = (bf16[256,1536]{1,0:T(8,128)(2,1)S(1)}, bf16[256,1536]{1,0:T(8,128)(2,1)}, u32[]{:S(2)}) copy-start(bf16[256,1536]{1,0:T(8,128)(2,1)} %copy-done.9) | copy-start | bytes 2359300
  691.3 3.1 copy-start.13
  694.5 2.4 copy-start.15
  694.5 3.9 copy-start.8
  694.5 4.0 copy-start.12
  696.9 1.6 copy-start.3
  696.9 2.1 copy-start.5
  696.9 2.1 copy-start.17
  699.0 4.1 copy-start.1
Sparse Core Ops, SparseCore 0:
  10.5 67.4 all-gather.4
  121.7 84.8 all-gather.6
  461.3 71.0 reduce-scatter.4
  535.7 70.3 reduce-scatter.2
